TPU v7x, 32 devices: a whole 2x2x4 slice. The times are simulated.
32 devices in a mesh: tm: 2 (over y), space: 16 (over z, x, core).
Axes of the slice: x: 2, y: 2, z: 4, core: 2. Of those that a mesh axis runs over, the one named last changes fastest.
Arguments:
- intensity: float32 [32, 128, 512], P('tm', 'space'), may hold values from 0.05 to 5
- w_first: bfloat16 [3, 3, 48, 32], replicated, may hold values from -0.5 to 0.5
- w_rest: bfloat16 [5, 3, 3, 48, 48], replicated, may hold values from -0.4375 to 0.4375
Outputs:
- front_maps: float32 [48, 128, 512], P(None, 'space', 'tm')
All inputs are finite; a program needn't handle non-finite values.
Results may differ from a plain program's by a relative error of at most 0.03.
Values may be sent and summed in bfloat16 or wider, within the bound.
No kernel may reach another device: no remote copies, remote signals or barrier semaphores. Data moves between devices by JAX's collectives and lax.ppermute only.
A program may use at most 64 MiB of HBM per device.

v0:
```python
import jax
import jax.numpy as jnp
from jax import lax
from jax.sharding import PartitionSpec as P

LAYERS = 6
RADIUS = 3


def extended(x, sides, width):
    for axis, dim in sides:
        size, length = (lax.axis_size(axis), x.shape[dim])
        up = [(i, (i + 1) % size) for i in range(size - 1)]
        down = [(j, i) for i, j in up]
        last = lax.slice_in_dim(x, length - width, length, axis=dim)
        leading = lax.slice_in_dim(x, 0, width, axis=dim)
        before = lax.ppermute(last, axis, up)
        after = lax.ppermute(leading, axis, down)
        x = jnp.concatenate([before, x, after], axis=dim)
    return x


def window_count(start_place, length, overall):
    places = start_place + jnp.arange(length, dtype=jnp.int32)
    upper = jnp.minimum(places + RADIUS, overall - 1)
    lower = jnp.maximum(places - RADIUS, 0)
    return (upper - lower + 1).astype(jnp.float32)


def conv_tile(padded, kernel):
    out_cols = padded.shape[1] - 2
    out_rows = padded.shape[2] - 2
    summed = None
    for a in range(3):
        for b in range(3):
            product = jnp.einsum(
                "oi,ixy->oxy",
                kernel[a, b],
                padded[:, a : a + out_cols, b : b + out_rows],
                preferred_element_type=jnp.float32,
            )
            summed = product if summed is None else summed + product
    return summed


def shards(intensity, w_first, w_rest):
    acq_dev, col_span, row_span = intensity.shape
    space_count = lax.axis_size("space")
    tm_count = lax.axis_size("tm")
    col_start = lax.axis_index("space") * col_span
    widened = extended(intensity, (("space", 1),), RADIUS)
    col_sum = widened[:, 0:col_span, :]
    for k in range(1, 2 * RADIUS + 1):
        col_sum = col_sum + widened[:, k : k + col_span, :]
    row_padded = jnp.pad(col_sum, ((0, 0), (0, 0), (RADIUS, RADIUS)))
    box_sum = row_padded[:, :, 0:row_span]
    for k in range(1, 2 * RADIUS + 1):
        box_sum = box_sum + row_padded[:, :, k : k + row_span]
    cell_count = (
        window_count(col_start, col_span, col_span * space_count)[:, None]
        * window_count(0, row_span, row_span)[None, :]
    )
    local_mean = box_sum / cell_count
    log_mean = jnp.log(local_mean)
    ratio_part = jnp.sum(intensity / local_mean, axis=0)
    acq_total = acq_dev * tm_count
    ratio_sum = lax.psum(ratio_part, "tm")
    features_own = (log_mean + jnp.log(ratio_sum / acq_total)[None]).astype(jnp.bfloat16)
    features = lax.all_to_all(features_own, "tm", split_axis=2, concat_axis=0, tiled=True)
    kernels = [w_first] + [w_rest[k] for k in range(LAYERS - 1)]
    activation = features
    result = None
    for depth_index in range(LAYERS):
        padded = extended(activation, (("tm", 2), ("space", 1)), 1)
        summed = conv_tile(padded, kernels[depth_index])
        if depth_index < LAYERS - 1:
            activation = jnp.maximum(summed, 0.0).astype(jnp.bfloat16)
        else:
            result = summed
    return result


def solution(mesh):
    in_specs = (P("tm", "space", None), P(), P())
    out_specs = P(None, "space", "tm")
    return jax.shard_map(shards, mesh=mesh, in_specs=in_specs, out_specs=out_specs, check_vma=False)
```

profile of v0, /device:TPU:19, one launch (start us, length us, event | category | flops | bytes accessed | tf_op | source)
XLA Modules:
  0.0 145.4 jit_solution(1917381582807719595)
XLA Ops:
  0.0 1.1 fusion.193
  1.1 2.7 %collective-permute-start.1 = (f32[16,3,512]{2,0,1:T(8,128)S(1)}, f32[16,3,512]{2,0,1:T(8,128)S(1)}, u32[]{:S(2)}, u32[]{:S(2)}) collective-permute-start(f32[16,3,512]{2,0,1:T(8,128)S(1)} %copy.56), channel_id=1, source_target_pairs={{1,0},{2,1},{3,2},{4,3},{5,4},{6,5},{7,6},{8,7},{9,8},{10,9},{11,1... | collective-permute-start | bytes 294920 | tf_op jit(solution)/shard_map/ppermute | solution.py:18
  3.9 3.9 %collective-permute-start = (f32[16,3,512]{2,0,1:T(8,128)S(1)}, f32[16,3,512]{2,0,1:T(8,128)S(1)}, u32[]{:S(2)}, u32[]{:S(2)}) collective-permute-start(f32[16,3,512]{2,0,1:T(8,128)S(1)} %copy.55), channel_id=1, source_target_pairs={{0,1},{1,2},{2,3},{3,4},{4,5},{5,6},{6,7},{7,8},{8,9},{9,10},{10,1... | collective-permute-start | bytes 294920 | tf_op jit(solution)/shard_map/ppermute | solution.py:17
  7.9 1.5 %collective-permute-done = f32[16,3,512]{2,0,1:T(8,128)S(1)} collective-permute-done((f32[16,3,512]{2,0,1:T(8,128)S(1)}, f32[16,3,512]{2,0,1:T(8,128)S(1)}, u32[]{:S(2)}, u32[]{:S(2)}) %collective-permute-start) | collective-permute-done | bytes 98336 | tf_op jit(solution)/shard_map/ppermute | solution.py:17
  9.8 0.5 fusion.66
  10.3 6.2 %psum.7 = f32[8,512]{1,0:T(8,128)S(1)} all-reduce(f32[8,512]{1,0:T(8,128)S(1)} %get-tuple-element.5), channel_id=1, replica_groups=mesh['tm'=2,'space'=16] {'tm'}, use_global_device_ids=true, to_apply=%region_1.2 | all-reduce | flops 4096 | bytes 32768 | tf_op jit(solution)/shard_map/psum | solution.py:67
  16.6 0.8 copy.52
  17.4 1.7 %reshape.104 = bf16[2,2,16384]{2,1,0:T(2,128)(2,1)} reshape(bf16[512,8,16]{2,1,0:T(8,128)(2,1)S(1)} %bitcast.310) | data formatting | bytes 262144
  19.1 3.4 %all-to-all-start = ((bf16[2,2,16384]{2,1,0:T(2,128)(2,1)}), bf16[2,2,16384]{2,1,0:T(2,128)(2,1)S(1)}, u32[]{:S(2)}, u32[]{:S(2)}) async-start(bf16[2,2,16384]{2,1,0:T(2,128)(2,1)} %reshape.104), calls=%async_computation | async-start | bytes 262144 | tf_op jit(solution)/shard_map/all_to_all | solution.py:69
  22.6 3.3 %all-to-all-done = bf16[2,2,16384]{2,1,0:T(2,128)(2,1)S(1)} async-done(((bf16[2,2,16384]{2,1,0:T(2,128)(2,1)}), bf16[2,2,16384]{2,1,0:T(2,128)(2,1)S(1)}, u32[]{:S(2)}, u32[]{:S(2)}) %all-to-all-start) | async-done | bytes 131104 | tf_op jit(solution)/shard_map/all_to_all | solution.py:69
  25.8 0.7 reshape.105
  26.5 0.7 copy.53
  27.3 1.9 %collective-permute-start.2 = (bf16[32,8,1]{2,0,1:T(8,128)(2,1)S(1)}, bf16[32,8,1]{2,0,1:T(8,128)(2,1)S(1)}, u32[]{:S(2)}, u32[]{:S(2)}) collective-permute-start(bf16[32,8,1]{2,0,1:T(8,128)(2,1)S(1)} %get-tuple-element.48), channel_id=1, source_target_pairs={{0,16},{1,17},{2,18},{3,19},{4,20},{5,21},{6,22},{7,23},{8,24},{9,... | collective-permute-start | bytes 1544 | tf_op jit(solution)/shard_map/ppermute | solution.py:17
  29.2 1.3 collective-permute-start.3
  30.8 3.4 %collective-permute-done.3 = bf16[32,8,1]{2,0,1:T(8,128)(2,1)S(1)} collective-permute-done((bf16[32,8,1]{2,0,1:T(8,128)(2,1)S(1)}, bf16[32,8,1]{2,0,1:T(8,128)(2,1)S(1)}, u32[]{:S(2)}, u32[]{:S(2)}) %collective-permute-start.3) | collective-permute-done | bytes 544 | tf_op jit(solution)/shard_map/ppermute | solution.py:18
  34.4 9.5 %collective-permute-start.4 = (bf16[32,1,258]{2,0,1:T(8,128)(2,1)S(1)}, bf16[32,1,258]{2,0,1:T(8,128)(2,1)S(1)}, u32[]{:S(2)}, u32[]{:S(2)}) collective-permute-start(bf16[32,1,258]{2,0,1:T(8,128)(2,1)S(1)} %get-tuple-element.34), channel_id=1, source_target_pairs={{0,1},{1,2},{2,3},{3,4},{4,5},{5,6},{6,7},{7,8},{8,9},{9,10},{10,1... | collective-permute-start | bytes 49544 | tf_op jit(solution)/shard_map/ppermute | solution.py:17
  43.9 1.9 %collective-permute-start.5 = (bf16[32,1,258]{2,0,1:T(8,128)(2,1)S(1)}, bf16[32,1,258]{2,0,1:T(8,128)(2,1)S(1)}, u32[]{:S(2)}, u32[]{:S(2)}) collective-permute-start(bf16[32,1,258]{2,0,1:T(8,128)(2,1)S(1)} %get-tuple-element.35), channel_id=1, source_target_pairs={{1,0},{2,1},{3,2},{4,3},{5,4},{6,5},{7,6},{8,7},{9,8},{10,9},{11,1... | collective-permute-start | bytes 49544 | tf_op jit(solution)/shard_map/ppermute | solution.py:18
  46.1 3.8 %collective-permute-done.5 = bf16[32,1,258]{2,0,1:T(8,128)(2,1)S(1)} collective-permute-done((bf16[32,1,258]{2,0,1:T(8,128)(2,1)S(1)}, bf16[32,1,258]{2,0,1:T(8,128)(2,1)S(1)}, u32[]{:S(2)}, u32[]{:S(2)}) %collective-permute-start.5) | collective-permute-done | bytes 16544 | tf_op jit(solution)/shard_map/ppermute | solution.py:18
  50.4 0.3 fusion.148
  50.7 0.3 fusion.137
  51.0 0.3 fusion.139
  51.5 0.3 fusion.41
  51.8 0.3 fusion.51
  52.3 1.3 collective-permute-start.6
  53.6 1.3 collective-permute-start.7
  55.2 3.7 %collective-permute-done.7 = bf16[48,8,1]{2,0,1:T(8,128)(2,1)S(1)} collective-permute-done((bf16[48,8,1]{2,0,1:T(8,128)(2,1)S(1)}, bf16[48,8,1]{2,0,1:T(8,128)(2,1)S(1)}, u32[]{:S(2)}, u32[]{:S(2)}) %collective-permute-start.7) | collective-permute-done | bytes 800 | tf_op jit(solution)/shard_map/ppermute | solution.py:18
  59.0 3.4 %collective-permute-start.8 = (bf16[48,1,258]{2,0,1:T(8,128)(2,1)S(1)}, bf16[48,1,258]{2,0,1:T(8,128)(2,1)S(1)}, u32[]{:S(2)}, u32[]{:S(2)}) collective-permute-start(bf16[48,1,258]{2,0,1:T(8,128)(2,1)S(1)} %get-tuple-element.30), channel_id=1, source_target_pairs={{0,1},{1,2},{2,3},{3,4},{4,5},{5,6},{6,7},{7,8},{8,9},{9,10},{10,1... | collective-permute-start | bytes 74312 | tf_op jit(solution)/shard_map/ppermute | solution.py:17
  62.4 1.9 %collective-permute-start.9 = (bf16[48,1,258]{2,0,1:T(8,128)(2,1)S(1)}, bf16[48,1,258]{2,0,1:T(8,128)(2,1)S(1)}, u32[]{:S(2)}, u32[]{:S(2)}) collective-permute-start(bf16[48,1,258]{2,0,1:T(8,128)(2,1)S(1)} %get-tuple-element.31), channel_id=1, source_target_pairs={{1,0},{2,1},{3,2},{4,3},{5,4},{6,5},{7,6},{8,7},{9,8},{10,9},{11,1... | collective-permute-start | bytes 74312 | tf_op jit(solution)/shard_map/ppermute | solution.py:18
  64.6 4.0 %collective-permute-done.9 = bf16[48,1,258]{2,0,1:T(8,128)(2,1)S(1)} collective-permute-done((bf16[48,1,258]{2,0,1:T(8,128)(2,1)S(1)}, bf16[48,1,258]{2,0,1:T(8,128)(2,1)S(1)}, u32[]{:S(2)}, u32[]{:S(2)}) %collective-permute-start.9) | collective-permute-done | bytes 24800 | tf_op jit(solution)/shard_map/ppermute | solution.py:18
  68.6 0.3 maximum_maximum_fusion
  70.3 0.3 fusion.50
  70.8 1.3 collective-permute-start.10
  72.1 1.3 collective-permute-start.11
  73.7 3.7 %collective-permute-done.11 = bf16[48,8,1]{2,0,1:T(8,128)(2,1)S(1)} collective-permute-done((bf16[48,8,1]{2,0,1:T(8,128)(2,1)S(1)}, bf16[48,8,1]{2,0,1:T(8,128)(2,1)S(1)}, u32[]{:S(2)}, u32[]{:S(2)}) %collective-permute-start.11) | collective-permute-done | bytes 800 | tf_op jit(solution)/shard_map/ppermute | solution.py:18
  77.5 3.3 %collective-permute-start.12 = (bf16[48,1,258]{2,0,1:T(8,128)(2,1)S(1)}, bf16[48,1,258]{2,0,1:T(8,128)(2,1)S(1)}, u32[]{:S(2)}, u32[]{:S(2)}) collective-permute-start(bf16[48,1,258]{2,0,1:T(8,128)(2,1)S(1)} %get-tuple-element.26), channel_id=1, source_target_pairs={{0,1},{1,2},{2,3},{3,4},{4,5},{5,6},{6,7},{7,8},{8,9},{9,10},{10,1... | collective-permute-start | bytes 74312 | tf_op jit(solution)/shard_map/ppermute | solution.py:17
  80.8 1.9 %collective-permute-start.13 = (bf16[48,1,258]{2,0,1:T(8,128)(2,1)S(1)}, bf16[48,1,258]{2,0,1:T(8,128)(2,1)S(1)}, u32[]{:S(2)}, u32[]{:S(2)}) collective-permute-start(bf16[48,1,258]{2,0,1:T(8,128)(2,1)S(1)} %get-tuple-element.27), channel_id=1, source_target_pairs={{1,0},{2,1},{3,2},{4,3},{5,4},{6,5},{7,6},{8,7},{9,8},{10,9},{11,1... | collective-permute-start | bytes 74312 | tf_op jit(solution)/shard_map/ppermute | solution.py:18
  83.0 4.0 %collective-permute-done.13 = bf16[48,1,258]{2,0,1:T(8,128)(2,1)S(1)} collective-permute-done((bf16[48,1,258]{2,0,1:T(8,128)(2,1)S(1)}, bf16[48,1,258]{2,0,1:T(8,128)(2,1)S(1)}, u32[]{:S(2)}, u32[]{:S(2)}) %collective-permute-start.13) | collective-permute-done | bytes 24800 | tf_op jit(solution)/shard_map/ppermute | solution.py:18
  87.0 0.3 maximum_maximum_fusion.1
  88.8 0.3 fusion.49
  89.2 1.3 collective-permute-start.14
  90.5 1.3 collective-permute-start.15
  92.1 3.7 %collective-permute-done.15 = bf16[48,8,1]{2,0,1:T(8,128)(2,1)S(1)} collective-permute-done((bf16[48,8,1]{2,0,1:T(8,128)(2,1)S(1)}, bf16[48,8,1]{2,0,1:T(8,128)(2,1)S(1)}, u32[]{:S(2)}, u32[]{:S(2)}) %collective-permute-start.15) | collective-permute-done | bytes 800 | tf_op jit(solution)/shard_map/ppermute | solution.py:18
  96.0 3.3 %collective-permute-start.16 = (bf16[48,1,258]{2,0,1:T(8,128)(2,1)S(1)}, bf16[48,1,258]{2,0,1:T(8,128)(2,1)S(1)}, u32[]{:S(2)}, u32[]{:S(2)}) collective-permute-start(bf16[48,1,258]{2,0,1:T(8,128)(2,1)S(1)} %get-tuple-element.22), channel_id=1, source_target_pairs={{0,1},{1,2},{2,3},{3,4},{4,5},{5,6},{6,7},{7,8},{8,9},{9,10},{10,1... | collective-permute-start | bytes 74312 | tf_op jit(solution)/shard_map/ppermute | solution.py:17
  99.3 2.1 %collective-permute-start.17 = (bf16[48,1,258]{2,0,1:T(8,128)(2,1)S(1)}, bf16[48,1,258]{2,0,1:T(8,128)(2,1)S(1)}, u32[]{:S(2)}, u32[]{:S(2)}) collective-permute-start(bf16[48,1,258]{2,0,1:T(8,128)(2,1)S(1)} %get-tuple-element.23), channel_id=1, source_target_pairs={{1,0},{2,1},{3,2},{4,3},{5,4},{6,5},{7,6},{8,7},{9,8},{10,9},{11,1... | collective-permute-start | bytes 74312 | tf_op jit(solution)/shard_map/ppermute | solution.py:18
  101.7 3.8 %collective-permute-done.17 = bf16[48,1,258]{2,0,1:T(8,128)(2,1)S(1)} collective-permute-done((bf16[48,1,258]{2,0,1:T(8,128)(2,1)S(1)}, bf16[48,1,258]{2,0,1:T(8,128)(2,1)S(1)}, u32[]{:S(2)}, u32[]{:S(2)}) %collective-permute-start.17) | collective-permute-done | bytes 24800 | tf_op jit(solution)/shard_map/ppermute | solution.py:18
  105.5 0.3 maximum_maximum_fusion.2
  107.2 0.3 fusion.48
  107.6 1.3 collective-permute-start.18
  109.0 1.3 collective-permute-start.19
  110.6 3.7 %collective-permute-done.19 = bf16[48,8,1]{2,0,1:T(8,128)(2,1)S(1)} collective-permute-done((bf16[48,8,1]{2,0,1:T(8,128)(2,1)S(1)}, bf16[48,8,1]{2,0,1:T(8,128)(2,1)S(1)}, u32[]{:S(2)}, u32[]{:S(2)}) %collective-permute-start.19) | collective-permute-done | bytes 800 | tf_op jit(solution)/shard_map/ppermute | solution.py:18
  114.4 3.3 %collective-permute-start.20 = (bf16[48,1,258]{2,0,1:T(8,128)(2,1)S(1)}, bf16[48,1,258]{2,0,1:T(8,128)(2,1)S(1)}, u32[]{:S(2)}, u32[]{:S(2)}) collective-permute-start(bf16[48,1,258]{2,0,1:T(8,128)(2,1)S(1)} %get-tuple-element.18), channel_id=1, source_target_pairs={{0,1},{1,2},{2,3},{3,4},{4,5},{5,6},{6,7},{7,8},{8,9},{9,10},{10,1... | collective-permute-start | bytes 74312 | tf_op jit(solution)/shard_map/ppermute | solution.py:17
  117.7 1.9 %collective-permute-start.21 = (bf16[48,1,258]{2,0,1:T(8,128)(2,1)S(1)}, bf16[48,1,258]{2,0,1:T(8,128)(2,1)S(1)}, u32[]{:S(2)}, u32[]{:S(2)}) collective-permute-start(bf16[48,1,258]{2,0,1:T(8,128)(2,1)S(1)} %get-tuple-element.19), channel_id=1, source_target_pairs={{1,0},{2,1},{3,2},{4,3},{5,4},{6,5},{7,6},{8,7},{9,8},{10,9},{11,1... | collective-permute-start | bytes 74312 | tf_op jit(solution)/shard_map/ppermute | solution.py:18
  119.9 4.0 %collective-permute-done.21 = bf16[48,1,258]{2,0,1:T(8,128)(2,1)S(1)} collective-permute-done((bf16[48,1,258]{2,0,1:T(8,128)(2,1)S(1)}, bf16[48,1,258]{2,0,1:T(8,128)(2,1)S(1)}, u32[]{:S(2)}, u32[]{:S(2)}) %collective-permute-start.21) | collective-permute-done | bytes 24800 | tf_op jit(solution)/shard_map/ppermute | solution.py:18
  123.9 0.3 maximum_maximum_fusion.3
  125.7 0.3 fusion.47
  126.1 1.3 collective-permute-start.22
  127.4 1.3 collective-permute-start.23
  129.0 3.7 %collective-permute-done.23 = bf16[48,8,1]{2,0,1:T(8,128)(2,1)S(1)} collective-permute-done((bf16[48,8,1]{2,0,1:T(8,128)(2,1)S(1)}, bf16[48,8,1]{2,0,1:T(8,128)(2,1)S(1)}, u32[]{:S(2)}, u32[]{:S(2)}) %collective-permute-start.23) | collective-permute-done | bytes 800 | tf_op jit(solution)/shard_map/ppermute | solution.py:18
  132.8 3.3 %collective-permute-start.24 = (bf16[48,1,258]{2,0,1:T(8,128)(2,1)S(1)}, bf16[48,1,258]{2,0,1:T(8,128)(2,1)S(1)}, u32[]{:S(2)}, u32[]{:S(2)}) collective-permute-start(bf16[48,1,258]{2,0,1:T(8,128)(2,1)S(1)} %get-tuple-element.14), channel_id=1, source_target_pairs={{0,1},{1,2},{2,3},{3,4},{4,5},{5,6},{6,7},{7,8},{8,9},{9,10},{10,1... | collective-permute-start | bytes 74312 | tf_op jit(solution)/shard_map/ppermute | solution.py:17
  136.1 1.9 %collective-permute-start.25 = (bf16[48,1,258]{2,0,1:T(8,128)(2,1)S(1)}, bf16[48,1,258]{2,0,1:T(8,128)(2,1)S(1)}, u32[]{:S(2)}, u32[]{:S(2)}) collective-permute-start(bf16[48,1,258]{2,0,1:T(8,128)(2,1)S(1)} %get-tuple-element.15), channel_id=1, source_target_pairs={{1,0},{2,1},{3,2},{4,3},{5,4},{6,5},{7,6},{8,7},{9,8},{10,9},{11,1... | collective-permute-start | bytes 74312 | tf_op jit(solution)/shard_map/ppermute | solution.py:18
  138.3 4.0 %collective-permute-done.25 = bf16[48,1,258]{2,0,1:T(8,128)(2,1)S(1)} collective-permute-done((bf16[48,1,258]{2,0,1:T(8,128)(2,1)S(1)}, bf16[48,1,258]{2,0,1:T(8,128)(2,1)S(1)}, u32[]{:S(2)}, u32[]{:S(2)}) %collective-permute-start.25) | collective-permute-done | bytes 24800 | tf_op jit(solution)/shard_map/ppermute | solution.py:18
  142.3 0.3 maximum_maximum_fusion.4
  144.1 0.3 fusion.14
  144.4 1.0 copy.54
  (88 shorter events, 13.2 us)
Async XLA Ops:
  1.1 6.8 %copy-start = (f32[16,8,512]{2,1,0:T(8,128)S(1)}, f32[16,8,512]{2,1,0:T(8,128)}, u32[]{:S(2)}) copy-start(f32[16,8,512]{2,1,0:T(8,128)} %param.3) | copy-start | bytes 786436
  1.1 8.3 %collective-permute-start.1 = (f32[16,3,512]{2,0,1:T(8,128)S(1)}, f32[16,3,512]{2,0,1:T(8,128)S(1)}, u32[]{:S(2)}, u32[]{:S(2)}) collective-permute-start(f32[16,3,512]{2,0,1:T(8,128)S(1)} %copy.56), channel_id=1, source_target_pairs={{1,0},{2,1},{3,2},{4,3},{5,4},{6,5},{7,6},{8,7},{9,8},{10,9},{11,1... | collective-permute-start | bytes 294920 | tf_op jit(solution)/shard_map/ppermute | solution.py:18
  3.9 5.5 %collective-permute-start = (f32[16,3,512]{2,0,1:T(8,128)S(1)}, f32[16,3,512]{2,0,1:T(8,128)S(1)}, u32[]{:S(2)}, u32[]{:S(2)}) collective-permute-start(f32[16,3,512]{2,0,1:T(8,128)S(1)} %copy.55), channel_id=1, source_target_pairs={{0,1},{1,2},{2,3},{3,4},{4,5},{5,6},{6,7},{7,8},{8,9},{9,10},{10,1... | collective-permute-start | bytes 294920 | tf_op jit(solution)/shard_map/ppermute | solution.py:17
  17.4 5.1 %copy-start.1 = (bf16[5,3,3,48,48]{4,3,2,1,0:T(8,128)(2,1)S(1)}, bf16[5,3,3,48,48]{4,3,2,1,0:T(8,128)(2,1)}, u32[]{:S(2)}) copy-start(bf16[5,3,3,48,48]{4,3,2,1,0:T(8,128)(2,1)} %param.5) | copy-start | bytes 622084
  19.1 6.7 %all-to-all-start = ((bf16[2,2,16384]{2,1,0:T(2,128)(2,1)}), bf16[2,2,16384]{2,1,0:T(2,128)(2,1)S(1)}, u32[]{:S(2)}, u32[]{:S(2)}) async-start(bf16[2,2,16384]{2,1,0:T(2,128)(2,1)} %reshape.104), calls=%async_computation | async-start | bytes 262144 | tf_op jit(solution)/shard_map/all_to_all | solution.py:69
  27.2 3.3 %copy-start.2 = (bf16[3,3,48,32]{2,3,1,0:T(8,128)(2,1)S(1)}, bf16[3,3,48,32]{2,3,1,0:T(8,128)(2,1)}, u32[]{:S(2)}) copy-start(bf16[3,3,48,32]{2,3,1,0:T(8,128)(2,1)} %param.4) | copy-start | bytes 82948
  27.3 3.5 %collective-permute-start.2 = (bf16[32,8,1]{2,0,1:T(8,128)(2,1)S(1)}, bf16[32,8,1]{2,0,1:T(8,128)(2,1)S(1)}, u32[]{:S(2)}, u32[]{:S(2)}) collective-permute-start(bf16[32,8,1]{2,0,1:T(8,128)(2,1)S(1)} %get-tuple-element.48), channel_id=1, source_target_pairs={{0,16},{1,17},{2,18},{3,19},{4,20},{5,21},{6,22},{7,23},{8,24},{9,... | collective-permute-start | bytes 1544 | tf_op jit(solution)/shard_map/ppermute | solution.py:17
  29.2 5.0 %collective-permute-start.3 = (bf16[32,8,1]{2,0,1:T(8,128)(2,1)S(1)}, bf16[32,8,1]{2,0,1:T(8,128)(2,1)S(1)}, u32[]{:S(2)}, u32[]{:S(2)}) collective-permute-start(bf16[32,8,1]{2,0,1:T(8,128)(2,1)S(1)} %get-tuple-element.49), channel_id=1, source_target_pairs={{16,0},{17,1},{18,2},{19,3},{20,4},{21,5},{22,6},{23,7},{24,8},{25... | collective-permute-start | bytes 1544 | tf_op jit(solution)/shard_map/ppermute | solution.py:18
  34.4 11.8 %collective-permute-start.4 = (bf16[32,1,258]{2,0,1:T(8,128)(2,1)S(1)}, bf16[32,1,258]{2,0,1:T(8,128)(2,1)S(1)}, u32[]{:S(2)}, u32[]{:S(2)}) collective-permute-start(bf16[32,1,258]{2,0,1:T(8,128)(2,1)S(1)} %get-tuple-element.34), channel_id=1, source_target_pairs={{0,1},{1,2},{2,3},{3,4},{4,5},{5,6},{6,7},{7,8},{8,9},{9,10},{10,1... | collective-permute-start | bytes 49544 | tf_op jit(solution)/shard_map/ppermute | solution.py:17
  43.9 6.0 %collective-permute-start.5 = (bf16[32,1,258]{2,0,1:T(8,128)(2,1)S(1)}, bf16[32,1,258]{2,0,1:T(8,128)(2,1)S(1)}, u32[]{:S(2)}, u32[]{:S(2)}) collective-permute-start(bf16[32,1,258]{2,0,1:T(8,128)(2,1)S(1)} %get-tuple-element.35), channel_id=1, source_target_pairs={{1,0},{2,1},{3,2},{4,3},{5,4},{6,5},{7,6},{8,7},{9,8},{10,9},{11,1... | collective-permute-start | bytes 49544 | tf_op jit(solution)/shard_map/ppermute | solution.py:18
  52.3 2.9 %collective-permute-start.6 = (bf16[48,8,1]{2,0,1:T(8,128)(2,1)S(1)}, bf16[48,8,1]{2,0,1:T(8,128)(2,1)S(1)}, u32[]{:S(2)}, u32[]{:S(2)}) collective-permute-start(bf16[48,8,1]{2,0,1:T(8,128)(2,1)S(1)} %get-tuple-element.46), channel_id=1, source_target_pairs={{0,16},{1,17},{2,18},{3,19},{4,20},{5,21},{6,22},{7,23},{8,24},{9,... | collective-permute-start | bytes 2312 | tf_op jit(solution)/shard_map/ppermute | solution.py:17
  53.6 5.4 %collective-permute-start.7 = (bf16[48,8,1]{2,0,1:T(8,128)(2,1)S(1)}, bf16[48,8,1]{2,0,1:T(8,128)(2,1)S(1)}, u32[]{:S(2)}, u32[]{:S(2)}) collective-permute-start(bf16[48,8,1]{2,0,1:T(8,128)(2,1)S(1)} %get-tuple-element.47), channel_id=1, source_target_pairs={{16,0},{17,1},{18,2},{19,3},{20,4},{21,5},{22,6},{23,7},{24,8},{25... | collective-permute-start | bytes 2312 | tf_op jit(solution)/shard_map/ppermute | solution.py:18
  59.0 5.6 %collective-permute-start.8 = (bf16[48,1,258]{2,0,1:T(8,128)(2,1)S(1)}, bf16[48,1,258]{2,0,1:T(8,128)(2,1)S(1)}, u32[]{:S(2)}, u32[]{:S(2)}) collective-permute-start(bf16[48,1,258]{2,0,1:T(8,128)(2,1)S(1)} %get-tuple-element.30), channel_id=1, source_target_pairs={{0,1},{1,2},{2,3},{3,4},{4,5},{5,6},{6,7},{7,8},{8,9},{9,10},{10,1... | collective-permute-start | bytes 74312 | tf_op jit(solution)/shard_map/ppermute | solution.py:17
  62.4 6.2 %collective-permute-start.9 = (bf16[48,1,258]{2,0,1:T(8,128)(2,1)S(1)}, bf16[48,1,258]{2,0,1:T(8,128)(2,1)S(1)}, u32[]{:S(2)}, u32[]{:S(2)}) collective-permute-start(bf16[48,1,258]{2,0,1:T(8,128)(2,1)S(1)} %get-tuple-element.31), channel_id=1, source_target_pairs={{1,0},{2,1},{3,2},{4,3},{5,4},{6,5},{7,6},{8,7},{9,8},{10,9},{11,1... | collective-permute-start | bytes 74312 | tf_op jit(solution)/shard_map/ppermute | solution.py:18
  70.8 2.9 %collective-permute-start.10 = (bf16[48,8,1]{2,0,1:T(8,128)(2,1)S(1)}, bf16[48,8,1]{2,0,1:T(8,128)(2,1)S(1)}, u32[]{:S(2)}, u32[]{:S(2)}) collective-permute-start(bf16[48,8,1]{2,0,1:T(8,128)(2,1)S(1)} %get-tuple-element.44), channel_id=1, source_target_pairs={{0,16},{1,17},{2,18},{3,19},{4,20},{5,21},{6,22},{7,23},{8,24},{9,... | collective-permute-start | bytes 2312 | tf_op jit(solution)/shard_map/ppermute | solution.py:17
  72.1 5.4 %collective-permute-start.11 = (bf16[48,8,1]{2,0,1:T(8,128)(2,1)S(1)}, bf16[48,8,1]{2,0,1:T(8,128)(2,1)S(1)}, u32[]{:S(2)}, u32[]{:S(2)}) collective-permute-start(bf16[48,8,1]{2,0,1:T(8,128)(2,1)S(1)} %get-tuple-element.45), channel_id=1, source_target_pairs={{16,0},{17,1},{18,2},{19,3},{20,4},{21,5},{22,6},{23,7},{24,8},{25... | collective-permute-start | bytes 2312 | tf_op jit(solution)/shard_map/ppermute | solution.py:18
  77.5 5.5 %collective-permute-start.12 = (bf16[48,1,258]{2,0,1:T(8,128)(2,1)S(1)}, bf16[48,1,258]{2,0,1:T(8,128)(2,1)S(1)}, u32[]{:S(2)}, u32[]{:S(2)}) collective-permute-start(bf16[48,1,258]{2,0,1:T(8,128)(2,1)S(1)} %get-tuple-element.26), channel_id=1, source_target_pairs={{0,1},{1,2},{2,3},{3,4},{4,5},{5,6},{6,7},{7,8},{8,9},{9,10},{10,1... | collective-permute-start | bytes 74312 | tf_op jit(solution)/shard_map/ppermute | solution.py:17
  80.8 6.2 %collective-permute-start.13 = (bf16[48,1,258]{2,0,1:T(8,128)(2,1)S(1)}, bf16[48,1,258]{2,0,1:T(8,128)(2,1)S(1)}, u32[]{:S(2)}, u32[]{:S(2)}) collective-permute-start(bf16[48,1,258]{2,0,1:T(8,128)(2,1)S(1)} %get-tuple-element.27), channel_id=1, source_target_pairs={{1,0},{2,1},{3,2},{4,3},{5,4},{6,5},{7,6},{8,7},{9,8},{10,9},{11,1... | collective-permute-start | bytes 74312 | tf_op jit(solution)/shard_map/ppermute | solution.py:18
  89.2 2.9 %collective-permute-start.14 = (bf16[48,8,1]{2,0,1:T(8,128)(2,1)S(1)}, bf16[48,8,1]{2,0,1:T(8,128)(2,1)S(1)}, u32[]{:S(2)}, u32[]{:S(2)}) collective-permute-start(bf16[48,8,1]{2,0,1:T(8,128)(2,1)S(1)} %get-tuple-element.42), channel_id=1, source_target_pairs={{0,16},{1,17},{2,18},{3,19},{4,20},{5,21},{6,22},{7,23},{8,24},{9,... | collective-permute-start | bytes 2312 | tf_op jit(solution)/shard_map/ppermute | solution.py:17
  90.5 5.4 %collective-permute-start.15 = (bf16[48,8,1]{2,0,1:T(8,128)(2,1)S(1)}, bf16[48,8,1]{2,0,1:T(8,128)(2,1)S(1)}, u32[]{:S(2)}, u32[]{:S(2)}) collective-permute-start(bf16[48,8,1]{2,0,1:T(8,128)(2,1)S(1)} %get-tuple-element.43), channel_id=1, source_target_pairs={{16,0},{17,1},{18,2},{19,3},{20,4},{21,5},{22,6},{23,7},{24,8},{25... | collective-permute-start | bytes 2312 | tf_op jit(solution)/shard_map/ppermute | solution.py:18
  96.0 5.7 %collective-permute-start.16 = (bf16[48,1,258]{2,0,1:T(8,128)(2,1)S(1)}, bf16[48,1,258]{2,0,1:T(8,128)(2,1)S(1)}, u32[]{:S(2)}, u32[]{:S(2)}) collective-permute-start(bf16[48,1,258]{2,0,1:T(8,128)(2,1)S(1)} %get-tuple-element.22), channel_id=1, source_target_pairs={{0,1},{1,2},{2,3},{3,4},{4,5},{5,6},{6,7},{7,8},{8,9},{9,10},{10,1... | collective-permute-start | bytes 74312 | tf_op jit(solution)/shard_map/ppermute | solution.py:17
  99.3 6.2 %collective-permute-start.17 = (bf16[48,1,258]{2,0,1:T(8,128)(2,1)S(1)}, bf16[48,1,258]{2,0,1:T(8,128)(2,1)S(1)}, u32[]{:S(2)}, u32[]{:S(2)}) collective-permute-start(bf16[48,1,258]{2,0,1:T(8,128)(2,1)S(1)} %get-tuple-element.23), channel_id=1, source_target_pairs={{1,0},{2,1},{3,2},{4,3},{5,4},{6,5},{7,6},{8,7},{9,8},{10,9},{11,1... | collective-permute-start | bytes 74312 | tf_op jit(solution)/shard_map/ppermute | solution.py:18
  107.6 2.9 %collective-permute-start.18 = (bf16[48,8,1]{2,0,1:T(8,128)(2,1)S(1)}, bf16[48,8,1]{2,0,1:T(8,128)(2,1)S(1)}, u32[]{:S(2)}, u32[]{:S(2)}) collective-permute-start(bf16[48,8,1]{2,0,1:T(8,128)(2,1)S(1)} %get-tuple-element.40), channel_id=1, source_target_pairs={{0,16},{1,17},{2,18},{3,19},{4,20},{5,21},{6,22},{7,23},{8,24},{9,... | collective-permute-start | bytes 2312 | tf_op jit(solution)/shard_map/ppermute | solution.py:17
  109.0 5.4 %collective-permute-start.19 = (bf16[48,8,1]{2,0,1:T(8,128)(2,1)S(1)}, bf16[48,8,1]{2,0,1:T(8,128)(2,1)S(1)}, u32[]{:S(2)}, u32[]{:S(2)}) collective-permute-start(bf16[48,8,1]{2,0,1:T(8,128)(2,1)S(1)} %get-tuple-element.41), channel_id=1, source_target_pairs={{16,0},{17,1},{18,2},{19,3},{20,4},{21,5},{22,6},{23,7},{24,8},{25... | collective-permute-start | bytes 2312 | tf_op jit(solution)/shard_map/ppermute | solution.py:18
  114.4 5.5 %collective-permute-start.20 = (bf16[48,1,258]{2,0,1:T(8,128)(2,1)S(1)}, bf16[48,1,258]{2,0,1:T(8,128)(2,1)S(1)}, u32[]{:S(2)}, u32[]{:S(2)}) collective-permute-start(bf16[48,1,258]{2,0,1:T(8,128)(2,1)S(1)} %get-tuple-element.18), channel_id=1, source_target_pairs={{0,1},{1,2},{2,3},{3,4},{4,5},{5,6},{6,7},{7,8},{8,9},{9,10},{10,1... | collective-permute-start | bytes 74312 | tf_op jit(solution)/shard_map/ppermute | solution.py:17
  117.7 6.2 %collective-permute-start.21 = (bf16[48,1,258]{2,0,1:T(8,128)(2,1)S(1)}, bf16[48,1,258]{2,0,1:T(8,128)(2,1)S(1)}, u32[]{:S(2)}, u32[]{:S(2)}) collective-permute-start(bf16[48,1,258]{2,0,1:T(8,128)(2,1)S(1)} %get-tuple-element.19), channel_id=1, source_target_pairs={{1,0},{2,1},{3,2},{4,3},{5,4},{6,5},{7,6},{8,7},{9,8},{10,9},{11,1... | collective-permute-start | bytes 74312 | tf_op jit(solution)/shard_map/ppermute | solution.py:18
  126.1 2.9 %collective-permute-start.22 = (bf16[48,8,1]{2,0,1:T(8,128)(2,1)S(1)}, bf16[48,8,1]{2,0,1:T(8,128)(2,1)S(1)}, u32[]{:S(2)}, u32[]{:S(2)}) collective-permute-start(bf16[48,8,1]{2,0,1:T(8,128)(2,1)S(1)} %get-tuple-element.38), channel_id=1, source_target_pairs={{0,16},{1,17},{2,18},{3,19},{4,20},{5,21},{6,22},{7,23},{8,24},{9,... | collective-permute-start | bytes 2312 | tf_op jit(solution)/shard_map/ppermute | solution.py:17
  127.4 5.4 %collective-permute-start.23 = (bf16[48,8,1]{2,0,1:T(8,128)(2,1)S(1)}, bf16[48,8,1]{2,0,1:T(8,128)(2,1)S(1)}, u32[]{:S(2)}, u32[]{:S(2)}) collective-permute-start(bf16[48,8,1]{2,0,1:T(8,128)(2,1)S(1)} %get-tuple-element.39), channel_id=1, source_target_pairs={{16,0},{17,1},{18,2},{19,3},{20,4},{21,5},{22,6},{23,7},{24,8},{25... | collective-permute-start | bytes 2312 | tf_op jit(solution)/shard_map/ppermute | solution.py:18
  132.8 5.5 %collective-permute-start.24 = (bf16[48,1,258]{2,0,1:T(8,128)(2,1)S(1)}, bf16[48,1,258]{2,0,1:T(8,128)(2,1)S(1)}, u32[]{:S(2)}, u32[]{:S(2)}) collective-permute-start(bf16[48,1,258]{2,0,1:T(8,128)(2,1)S(1)} %get-tuple-element.14), channel_id=1, source_target_pairs={{0,1},{1,2},{2,3},{3,4},{4,5},{5,6},{6,7},{7,8},{8,9},{9,10},{10,1... | collective-permute-start | bytes 74312 | tf_op jit(solution)/shard_map/ppermute | solution.py:17
  136.1 6.2 %collective-permute-start.25 = (bf16[48,1,258]{2,0,1:T(8,128)(2,1)S(1)}, bf16[48,1,258]{2,0,1:T(8,128)(2,1)S(1)}, u32[]{:S(2)}, u32[]{:S(2)}) collective-permute-start(bf16[48,1,258]{2,0,1:T(8,128)(2,1)S(1)} %get-tuple-element.15), channel_id=1, source_target_pairs={{1,0},{2,1},{3,2},{4,3},{5,4},{6,5},{7,6},{8,7},{9,8},{10,9},{11,1... | collective-permute-start | bytes 74312 | tf_op jit(solution)/shard_map/ppermute | solution.py:18
where the time goes:
time: 146 us; the launch traced here: 145 us
  starting transfers between devices  63.9 us (44%)
  waiting for transfers between devices  51.1 us (35%)
  matrix products  13.4 us (9%)
  local copies, waits for them, and re-layouts  6.89 us (5%)
  blocking collectives  6.17 us (4%)
  other arithmetic  3.07 us (2%)
    ppermute x13, waiting for transfers between devices, extended(): after = lax.ppermute(leading, axis, down)  45.7 us
    ppermute x13, starting transfers between devices, extended(): before = lax.ppermute(last, axis, up)  38.3 us
    ppermute x13, starting transfers between devices, extended(): after = lax.ppermute(leading, axis, down)  22.2 us
    dot_general x54, matrix products, conv_tile(): jnp.einsum('oi,ixy->oxy', kernel[a, b], padded[:, a:a + out_cols, b:b + o...  13.4 us
    psum x1, blocking collectives, shards(): ratio_sum = lax.psum(ratio_part, 'tm')  6.17 us
    all_to_all x1, starting transfers between devices, shards(): lax.all_to_all(features_own, 'tm', split_axis=2, concat_axis=0, tiled=True)  3.38 us
    all_to_all x1, waiting for transfers between devices, shards(): lax.all_to_all(features_own, 'tm', split_axis=2, concat_axis=0, tiled=True)  3.25 us
  transfers between devices with their start and end apart: 27, of which 19 were waited for; matrix products, arithmetic and copies ran while one was open for 2% of the time, Pallas kernels for 0%

commit v1 on v0

v1 whole, which is shorter than its diff:
```python
import jax
import jax.numpy as jnp
from jax import lax
from jax.experimental import pallas as pl
from jax.experimental.pallas import tpu as pltpu
from jax.sharding import PartitionSpec as P

LAYERS = 6
RADIUS = 3
HALO = RADIUS + LAYERS
MARGIN = 16
LANES = 128


def shifted(x, axis, by):
    size = lax.axis_size(axis)
    pairs = [(i, i + by) for i in range(size) if 0 <= i + by < size]
    return lax.ppermute(x, axis, pairs)


def window_rows(tile, rows):
    return min(rows, tile + LANES * (1 if rows <= 2 * tile else 2))


def window_base(index, tile, rows):
    return jnp.clip(index * tile - LANES, 0, rows - window_rows(tile, rows))


def rolled(x, by):
    return pltpu.roll(x, by % x.shape[-1], x.ndim - 1)


def body(place, far_lo, lo, own, hi, far_hi, w1, wr, out, inten, sums, act_a, act_b):
    acqs, width = own.shape[1:]
    cols = own.shape[0]
    tile = out.shape[2]
    channels = out.shape[0]
    first_col, all_cols = place[0], place[1]
    base, all_rows, offset = place[2], place[3], place[4]

    lane = lax.broadcasted_iota(jnp.int32, (1, width), 1)
    inside = (lane >= offset - MARGIN) & (lane < offset + tile + MARGIN)
    row_mask = inside.astype(jnp.float32)

    pieces = [(far_lo, 0, HALO - cols), (lo, 0, cols), (own, 0, cols), (hi, 0, cols), (far_hi, 0, HALO - cols)]
    at = 0
    for ref, start, count in pieces:
        for k in range(count):
            inten[at] = jnp.where(inside, jnp.exp(ref[start + k].astype(jnp.float32)), 0.0)
            at += 1

    feature_cols = cols + 2 * LAYERS
    for c in range(at):
        g = first_col - HALO + c
        if c < HALO or c >= HALO + cols:
            ok = ((g >= 0) & (g < all_cols)).astype(jnp.float32)
            inten[c] = inten[c] * ok

    row = base + lane
    row_count = jnp.minimum(row + RADIUS, all_rows - 1) - jnp.maximum(row - RADIUS, 0) + 1
    row_count = row_count.astype(jnp.float32)

    def despeckle(f, _):
        total = inten[f]
        for k in range(1, 2 * RADIUS + 1):
            total = total + inten[f + k]
        three = rolled(total, 1) + total + rolled(total, -1)
        box = rolled(three, 2) + total + rolled(three, -2)
        g = first_col - LAYERS + f
        col_count = jnp.minimum(g + RADIUS, all_cols - 1) - jnp.maximum(g - RADIUS, 0) + 1
        col_count = jnp.maximum(col_count, 1).astype(jnp.float32)
        local_mean = box / (row_count * col_count)
        ratio = jnp.sum(inten[f + RADIUS] / local_mean, axis=0, keepdims=True)
        feature = jnp.log(local_mean) + jnp.log(ratio / acqs)
        ok = (g >= 0) & (g < all_cols)
        feature = jnp.where(inside & ok, feature, 0.0)
        at = pl.multiple_of(f * 3 * acqs, 16)
        act_a[pl.ds(at, acqs), :] = rolled(feature, 1).astype(jnp.bfloat16)
        act_a[pl.ds(at + acqs, acqs), :] = feature.astype(jnp.bfloat16)
        act_a[pl.ds(at + 2 * acqs, acqs), :] = rolled(feature, -1).astype(jnp.bfloat16)
        return 0

    lax.fori_loop(0, feature_cols, despeckle, 0)

    source, target = act_a, act_b
    depth = acqs
    for layer in range(LAYERS):
        weight = w1[...] if layer == 0 else wr[layer - 1]
        out_cols = feature_cols - 2 * (layer + 1)
        last = layer == LAYERS - 1

        def column(j, _, source=source, target=target, depth=depth, weight=weight, layer=layer, last=last):
            at = pl.multiple_of(j * 3 * depth, 16)
            summed = jnp.dot(weight, source[pl.ds(at, 9 * depth), :], preferred_element_type=jnp.float32)
            g = first_col - (LAYERS - 1 - layer) + j
            ok = ((g >= 0) & (g < all_cols)).astype(jnp.float32)
            hidden = jnp.maximum(summed, 0.0) * (row_mask * ok)
            to = pl.multiple_of(j * 3 * channels, 16)
            target[pl.ds(to, channels), :] = rolled(hidden, 1).astype(jnp.bfloat16)
            target[pl.ds(to + channels, channels), :] = hidden.astype(jnp.bfloat16)
            target[pl.ds(to + 2 * channels, channels), :] = rolled(hidden, -1).astype(jnp.bfloat16)
            return 0

        if not last:
            lax.fori_loop(0, out_cols, column, 0)
        else:
            lanes = pl.ds(pl.multiple_of(offset, LANES), tile)
            for j in range(out_cols):
                out[:, j, :] = jnp.dot(
                    weight,
                    source[j * 3 * depth : (j * 3 + 9) * depth, lanes],
                    preferred_element_type=jnp.float32,
                )
        source, target = target, source
        depth = channels


def shards(intensity, w_first, w_rest):
    acqs_own, cols, rows = intensity.shape
    tm = lax.axis_size("tm")
    space = lax.axis_size("space")
    m = lax.axis_index("tm")
    s = lax.axis_index("space")
    tile = rows // tm
    width = window_rows(tile, rows)
    channels, acqs = w_first.shape[2:]

    coded = jnp.log(intensity).astype(jnp.bfloat16).transpose(1, 0, 2)
    base = window_base(m, tile, rows)
    parts = [lax.dynamic_slice_in_dim(coded, base, width, axis=2)]
    for d in range(1, tm):
        to = window_base((m + d) % tm, tile, rows)
        piece = lax.dynamic_slice_in_dim(coded, to, width, axis=2)
        parts.append(lax.ppermute(piece, "tm", [(i, (i + d) % tm) for i in range(tm)]))
    own = jnp.concatenate(parts, axis=1)
    order = (m - jnp.arange(tm)) % tm
    w1 = jnp.take(w_first.reshape(3, 3, channels, tm, acqs_own), order, axis=3)
    w1 = w1.reshape(3, 3, channels, acqs).transpose(2, 0, 1, 3).reshape(channels, 9 * acqs)
    wr = w_rest.transpose(0, 3, 1, 2, 4).reshape(LAYERS - 1, channels, 9 * channels)

    far = HALO - cols
    far_lo = shifted(own[cols - far :], "space", 2)
    far_hi = shifted(own[:far], "space", -2)
    lo = shifted(own, "space", 1)
    hi = shifted(own, "space", -1)

    place = jnp.stack(
        [s * cols, jnp.int32(cols * space), base, jnp.int32(rows), m * tile - base]
    ).astype(jnp.int32)
    vmem = pl.BlockSpec(memory_space=pltpu.VMEM)
    feature_cols = cols + 2 * LAYERS
    act = (feature_cols * 3 * channels, width)
    return pl.pallas_call(
        body,
        out_shape=jax.ShapeDtypeStruct((channels, cols, tile), jnp.float32),
        in_specs=[pl.BlockSpec(memory_space=pltpu.SMEM)] + [vmem] * 7,
        out_specs=vmem,
        scratch_shapes=[
            pltpu.VMEM((cols + 2 * HALO, acqs, width), jnp.float32),
            pltpu.VMEM((8, 128), jnp.float32),
            pltpu.VMEM(act, jnp.bfloat16),
            pltpu.VMEM(act, jnp.bfloat16),
        ],
        compiler_params=pltpu.CompilerParams(vmem_limit_bytes=40 * 1024 * 1024),
    )(place, far_lo, lo, own, hi, far_hi, w1, wr)


def solution(mesh):
    in_specs = (P("tm", "space", None), P(), P())
    out_specs = P(None, "space", "tm")
    return jax.shard_map(shards, mesh=mesh, in_specs=in_specs, out_specs=out_specs, check_vma=False)
```

time: 146 us -> 47.1 us (0.32)
  the two profiles are of different devices: /device:TPU:19 before, /device:TPU:25 now
where the time goes in v1:
time: 47.1 us; the launch traced here: 46.9 us
  Pallas kernels  26.2 us (56%)
  starting transfers between devices  13.3 us (28%)
  waiting for transfers between devices  4.18 us (9%)
  local copies, waits for them, and re-layouts  1.74 us (4%)
  other arithmetic  1.29 us (3%)
    pallas_call x1, Pallas kernels, shards(): pl.pallas_call(body, out_shape=jax.ShapeDtypeStruct((channels, cols, tile...  26.2 us
    ppermute x4, starting transfers between devices, shifted(): return lax.ppermute(x, axis, pairs)  12 us
    ppermute x4, waiting for transfers between devices, shifted(): return lax.ppermute(x, axis, pairs)  2.75 us
    ppermute x1, waiting for transfers between devices, shards(): lax.ppermute(piece, 'tm', [(i, (i + d) % tm) for i in range(tm)])  1.43 us
    ppermute x1, starting transfers between devices, shards(): lax.ppermute(piece, 'tm', [(i, (i + d) % tm) for i in range(tm)])  1.31 us
    convert_element_type x1, other arithmetic, shards(): coded = jnp.log(intensity).astype(jnp.bfloat16).transpose(1, 0, 2)  1.15 us
  transfers between devices with their start and end apart: 5, of which 2 were waited for; matrix products, arithmetic and copies ran while one was open for 4% of the time, Pallas kernels for 0%

profile of v1, /device:TPU:25, one launch (start us, length us, event | category | flops | bytes accessed | tf_op | source)
XLA Modules:
  0.0 46.9 jit_solution(7032723364499436450)
XLA Ops:
  0.0 0.0 copy-start
  0.0 1.1 %fusion = bf16[16,8,512]{2,0,1:T(8,128)(2,1)S(1)} fusion(f32[16,8,512]{2,1,0:T(8,128)} %param.3), kind=kLoop, calls=%fused_computation.2 | loop fusion | flops 65536 | bytes 393216 | tf_op jit(solution)/shard_map/convert_element_type | solution.py:128
  1.1 0.1 dynamic-slice_bitcast_fusion
  1.3 1.3 %collective-permute-start = (bf16[8,16,384]{2,1,0:T(8,128)(2,1)S(1)}, bf16[8,16,384]{2,1,0:T(8,128)(2,1)S(1)}, u32[]{:S(2)}, u32[]{:S(2)}) collective-permute-start(bf16[8,16,384]{2,1,0:T(8,128)(2,1)S(1)} %get-tuple-element.7), channel_id=1, source_target_pairs={{0,16},{16,0},{1,17},{17,1},{2,18},{18,2},{3,19},{19,3},{4,20},{20... | collective-permute-start | bytes 294920 | tf_op jit(solution)/shard_map/ppermute | solution.py:134
  2.6 0.1 broadcast_in_dim.14
  2.7 0.1 broadcast_in_dim.15
  2.8 0.0 copy-done
  2.8 0.6 %gather_fusion = bf16[2,3,3,48,16]{3,4,2,1,0:T(8,128)(2,1)S(1)} fusion(bf16[3,3,48,2,16]{2,4,3,1,0:T(8,128)(2,1)S(1)} %bitcast.17, s32[1024]{0:T(1024)S(1)} %pad_clamp_fusion), kind=kCustom, calls=%fused_computation | custom fusion | bytes 55304 | tf_op jit(solution)/shard_map/jit(_take)/gather | solution.py:137
  3.4 0.0 copy-start.1
  3.4 1.4 %collective-permute-done = bf16[8,16,384]{2,1,0:T(8,128)(2,1)S(1)} collective-permute-done((bf16[8,16,384]{2,1,0:T(8,128)(2,1)S(1)}, bf16[8,16,384]{2,1,0:T(8,128)(2,1)S(1)}, u32[]{:S(2)}, u32[]{:S(2)}) %collective-permute-start) | collective-permute-done | bytes 98336 | tf_op jit(solution)/shard_map/ppermute | solution.py:134
  4.9 3.7 %collective-permute-start.3 = (bf16[8,32,384]{2,1,0:T(8,128)(2,1)S(1)}, bf16[8,32,384]{2,1,0:T(8,128)(2,1)S(1)}, u32[]{:S(2)}, u32[]{:S(2)}) collective-permute-start(bf16[8,32,384]{2,1,0:T(8,128)(2,1)S(1)} %pad_maximum_fusion.own), channel_id=1, source_target_pairs={{1,0},{2,1},{3,2},{4,3},{5,4},{6,5},{7,6},{8,7},{9,8},{10,9},{11,1... | collective-permute-start | bytes 589832 | tf_op jit(solution)/shard_map/ppermute | solution.py:18
  8.6 3.0 %collective-permute-start.2 = (bf16[8,32,384]{2,1,0:T(8,128)(2,1)S(1)}, bf16[8,32,384]{2,1,0:T(8,128)(2,1)S(1)}, u32[]{:S(2)}, u32[]{:S(2)}) collective-permute-start(bf16[8,32,384]{2,1,0:T(8,128)(2,1)S(1)} %pad_maximum_fusion.own), channel_id=1, source_target_pairs={{0,1},{1,2},{2,3},{3,4},{4,5},{5,6},{6,7},{7,8},{8,9},{9,10},{10,1... | collective-permute-start | bytes 589832 | tf_op jit(solution)/shard_map/ppermute | solution.py:18
  11.6 3.1 %collective-permute-start.4 = (bf16[1,32,384]{2,1,0:T(8,128)(2,1)S(1)}, bf16[1,32,384]{2,1,0:T(8,128)(2,1)S(1)}, u32[]{:S(2)}, u32[]{:S(2)}) collective-permute-start(bf16[1,32,384]{2,1,0:T(8,128)(2,1)S(1)} %get-tuple-element.5), channel_id=1, source_target_pairs={{2,0},{3,1},{4,2},{5,3},{6,4},{7,5},{8,6},{9,7},{10,8},{11,9},{12,... | collective-permute-start | bytes 73736 | tf_op jit(solution)/shard_map/ppermute | solution.py:18
  14.7 2.2 %collective-permute-start.1 = (bf16[1,32,384]{2,1,0:T(8,128)(2,1)S(1)}, bf16[1,32,384]{2,1,0:T(8,128)(2,1)S(1)}, u32[]{:S(2)}, u32[]{:S(2)}) collective-permute-start(bf16[1,32,384]{2,1,0:T(8,128)(2,1)S(1)} %get-tuple-element.6), channel_id=1, source_target_pairs={{0,2},{1,3},{2,4},{3,5},{4,6},{5,7},{6,8},{7,9},{8,10},{9,11},{10,... | collective-permute-start | bytes 73736 | tf_op jit(solution)/shard_map/ppermute | solution.py:18
  16.9 0.1 bitcast_select_fusion
  17.0 0.1 copy.13.w1
  17.1 0.0 copy-done.1
  17.1 0.3 copy.12
  17.4 0.4 reshape.68.wr
  17.8 0.1 stack.15.place
  17.9 0.0 collective-permute-done.4.far_hi
  17.9 2.7 %collective-permute-done.1.far_lo = bf16[1,32,384]{2,1,0:T(8,128)(2,1)S(1)} collective-permute-done((bf16[1,32,384]{2,1,0:T(8,128)(2,1)S(1)}, bf16[1,32,384]{2,1,0:T(8,128)(2,1)S(1)}, u32[]{:S(2)}, u32[]{:S(2)}) %collective-permute-start.1) | collective-permute-done | bytes 24608 | tf_op jit(solution)/shard_map/ppermute | solution.py:18
  20.6 0.0 collective-permute-done.3.hi
  20.6 0.0 collective-permute-done.2.lo
  20.7 26.2 %shard_map.37 = f32[48,8,256]{2,1,0:T(8,128)} custom-call(s32[5]{0:T(128)S(1)} %stack.15.place, bf16[1,32,384]{2,1,0:T(8,128)(2,1)S(1)} %collective-permute-done.1.far_lo, bf16[8,32,384]{2,1,0:T(8,128)(2,1)S(1)} %collective-permute-done.2.lo, bf16[8,32,384]{2,1,0:T(8,128)(2,1)S(1)} %pad_maximum_fusion.own, ...), custom_call_target="tpu_custom_call" | custom-call | tf_op jit(solution)/shard_map/pallas_call | solution.py:153
  (6 shorter events, 0.1 us)
Async XLA Ops:
  0.0 2.8 %copy-start = (bf16[3,3,48,32]{2,3,1,0:T(8,128)(2,1)S(1)}, bf16[3,3,48,32]{2,3,1,0:T(8,128)(2,1)}, u32[]{:S(2)}) copy-start(bf16[3,3,48,32]{2,3,1,0:T(8,128)(2,1)} %param.4) | copy-start | bytes 82948
  1.3 3.5 %collective-permute-start = (bf16[8,16,384]{2,1,0:T(8,128)(2,1)S(1)}, bf16[8,16,384]{2,1,0:T(8,128)(2,1)S(1)}, u32[]{:S(2)}, u32[]{:S(2)}) collective-permute-start(bf16[8,16,384]{2,1,0:T(8,128)(2,1)S(1)} %get-tuple-element.7), channel_id=1, source_target_pairs={{0,16},{16,0},{1,17},{17,1},{2,18},{18,2},{3,19},{19,3},{4,20},{20... | collective-permute-start | bytes 294920 | tf_op jit(solution)/shard_map/ppermute | solution.py:134
  3.4 13.7 %copy-start.1 = (bf16[5,3,3,48,48]{4,3,2,1,0:T(8,128)(2,1)S(1)}, bf16[5,3,3,48,48]{4,3,2,1,0:T(8,128)(2,1)}, u32[]{:S(2)}) copy-start(bf16[5,3,3,48,48]{4,3,2,1,0:T(8,128)(2,1)} %param.5) | copy-start | bytes 622084
  4.9 15.8 %collective-permute-start.3 = (bf16[8,32,384]{2,1,0:T(8,128)(2,1)S(1)}, bf16[8,32,384]{2,1,0:T(8,128)(2,1)S(1)}, u32[]{:S(2)}, u32[]{:S(2)}) collective-permute-start(bf16[8,32,384]{2,1,0:T(8,128)(2,1)S(1)} %pad_maximum_fusion.own), channel_id=1, source_target_pairs={{1,0},{2,1},{3,2},{4,3},{5,4},{6,5},{7,6},{8,7},{9,8},{10,9},{11,1... | collective-permute-start | bytes 589832 | tf_op jit(solution)/shard_map/ppermute | solution.py:18
  8.6 12.1 %collective-permute-start.2 = (bf16[8,32,384]{2,1,0:T(8,128)(2,1)S(1)}, bf16[8,32,384]{2,1,0:T(8,128)(2,1)S(1)}, u32[]{:S(2)}, u32[]{:S(2)}) collective-permute-start(bf16[8,32,384]{2,1,0:T(8,128)(2,1)S(1)} %pad_maximum_fusion.own), channel_id=1, source_target_pairs={{0,1},{1,2},{2,3},{3,4},{4,5},{5,6},{6,7},{7,8},{8,9},{9,10},{10,1... | collective-permute-start | bytes 589832 | tf_op jit(solution)/shard_map/ppermute | solution.py:18
  11.6 6.3 %collective-permute-start.4 = (bf16[1,32,384]{2,1,0:T(8,128)(2,1)S(1)}, bf16[1,32,384]{2,1,0:T(8,128)(2,1)S(1)}, u32[]{:S(2)}, u32[]{:S(2)}) collective-permute-start(bf16[1,32,384]{2,1,0:T(8,128)(2,1)S(1)} %get-tuple-element.5), channel_id=1, source_target_pairs={{2,0},{3,1},{4,2},{5,3},{6,4},{7,5},{8,6},{9,7},{10,8},{11,9},{12,... | collective-permute-start | bytes 73736 | tf_op jit(solution)/shard_map/ppermute | solution.py:18
  14.7 5.9 %collective-permute-start.1 = (bf16[1,32,384]{2,1,0:T(8,128)(2,1)S(1)}, bf16[1,32,384]{2,1,0:T(8,128)(2,1)S(1)}, u32[]{:S(2)}, u32[]{:S(2)}) collective-permute-start(bf16[1,32,384]{2,1,0:T(8,128)(2,1)S(1)} %get-tuple-element.6), channel_id=1, source_target_pairs={{0,2},{1,3},{2,4},{3,5},{4,6},{5,7},{6,8},{7,9},{8,10},{9,11},{10,... | collective-permute-start | bytes 73736 | tf_op jit(solution)/shard_map/ppermute | solution.py:18

commit v2 on v1

--- a/solution.py
+++ b/solution.py
@@ -30,7 +30,7 @@
     return pltpu.roll(x, by % x.shape[-1], x.ndim - 1)
 
 
-def body(place, far_lo, lo, own, hi, far_hi, w1, wr, out, inten, sums, act_a, act_b):
+def body(place, far_lo, lo, own, hi, far_hi, w1, wr, out, inten, act_a, act_b):
     acqs, width = own.shape[1:]
     cols = own.shape[0]
     tile = out.shape[2]
@@ -80,7 +80,7 @@
         act_a[pl.ds(at + 2 * acqs, acqs), :] = rolled(feature, -1).astype(jnp.bfloat16)
         return 0
 
-    lax.fori_loop(0, feature_cols, despeckle, 0)
+    lax.fori_loop(0, feature_cols, despeckle, 0, unroll=4)
 
     source, target = act_a, act_b
     depth = acqs
@@ -89,20 +89,20 @@
         out_cols = feature_cols - 2 * (layer + 1)
         last = layer == LAYERS - 1
 
-        def column(j, _, source=source, target=target, depth=depth, weight=weight, layer=layer, last=last):
-            at = pl.multiple_of(j * 3 * depth, 16)
+        def column(j, source=source, target=target, depth=depth, weight=weight, layer=layer, last=last):
+            at = j * 3 * depth
             summed = jnp.dot(weight, source[pl.ds(at, 9 * depth), :], preferred_element_type=jnp.float32)
             g = first_col - (LAYERS - 1 - layer) + j
             ok = ((g >= 0) & (g < all_cols)).astype(jnp.float32)
             hidden = jnp.maximum(summed, 0.0) * (row_mask * ok)
-            to = pl.multiple_of(j * 3 * channels, 16)
+            to = j * 3 * channels
             target[pl.ds(to, channels), :] = rolled(hidden, 1).astype(jnp.bfloat16)
             target[pl.ds(to + channels, channels), :] = hidden.astype(jnp.bfloat16)
             target[pl.ds(to + 2 * channels, channels), :] = rolled(hidden, -1).astype(jnp.bfloat16)
-            return 0
 
         if not last:
-            lax.fori_loop(0, out_cols, column, 0)
+            for j in range(out_cols):
+                column(j)
         else:
             lanes = pl.ds(pl.multiple_of(offset, LANES), tile)
             for j in range(out_cols):
@@ -139,8 +139,9 @@
     wr = w_rest.transpose(0, 3, 1, 2, 4).reshape(LAYERS - 1, channels, 9 * channels)
 
     far = HALO - cols
-    far_lo = shifted(own[cols - far :], "space", 2)
-    far_hi = shifted(own[:far], "space", -2)
+    own, first, final = lax.optimization_barrier((own, own[:far], own[cols - far :]))
+    far_lo = shifted(final, "space", 2)
+    far_hi = shifted(first, "space", -2)
     lo = shifted(own, "space", 1)
     hi = shifted(own, "space", -1)
 
@@ -157,7 +158,6 @@
         out_specs=vmem,
         scratch_shapes=[
             pltpu.VMEM((cols + 2 * HALO, acqs, width), jnp.float32),
-            pltpu.VMEM((8, 128), jnp.float32),
             pltpu.VMEM(act, jnp.bfloat16),
             pltpu.VMEM(act, jnp.bfloat16),
         ],

time: 47.1 us -> 29.4 us (0.62)
  the two profiles are of different devices: /device:TPU:25 before, /device:TPU:0 now
where the time goes in v2:
time: 29.4 us; the launch traced here: 29.2 us
  starting transfers between devices  12.3 us (42%)
  Pallas kernels  8.07 us (27%)
  waiting for transfers between devices  5.63 us (19%)
  local copies, waits for them, and re-layouts  1.74 us (6%)
  other arithmetic  1.29 us (4%)
    ppermute x4, starting transfers between devices, shifted(): return lax.ppermute(x, axis, pairs)  9.32 us
    pallas_call x1, Pallas kernels, shards(): pl.pallas_call(body, out_shape=jax.ShapeDtypeStruct((channels, cols, tile...  8.07 us
    ppermute x4, waiting for transfers between devices, shifted(): return lax.ppermute(x, axis, pairs)  3.64 us
    ppermute x1, starting transfers between devices, shards(): lax.ppermute(piece, 'tm', [(i, (i + d) % tm) for i in range(tm)])  3.03 us
    ppermute x1, waiting for transfers between devices, shards(): lax.ppermute(piece, 'tm', [(i, (i + d) % tm) for i in range(tm)])  2 us
    convert_element_type x1, other arithmetic, shards(): coded = jnp.log(intensity).astype(jnp.bfloat16).transpose(1, 0, 2)  1.15 us
  transfers between devices with their start and end apart: 5, of which 2 were waited for; matrix products, arithmetic and copies ran while one was open for 6% of the time, Pallas kernels for 0%

profile of v2, /device:TPU:0, one launch (start us, length us, event | category | flops | bytes accessed | tf_op | source)
XLA Modules:
  0.0 29.2 jit_solution(8038117514711469468)
XLA Ops:
  0.0 0.0 copy-start
  0.0 1.1 %fusion = bf16[16,8,512]{2,0,1:T(8,128)(2,1)S(1)} fusion(f32[16,8,512]{2,1,0:T(8,128)} %param.3), kind=kLoop, calls=%fused_computation.2 | loop fusion | flops 65536 | bytes 393216 | tf_op jit(solution)/shard_map/convert_element_type | solution.py:128
  1.1 0.1 dynamic-slice_bitcast_fusion.1
  1.3 3.0 %collective-permute-start = (bf16[8,16,384]{2,1,0:T(8,128)(2,1)S(1)}, bf16[8,16,384]{2,1,0:T(8,128)(2,1)S(1)}, u32[]{:S(2)}, u32[]{:S(2)}) collective-permute-start(bf16[8,16,384]{2,1,0:T(8,128)(2,1)S(1)} %get-tuple-element.14), channel_id=1, source_target_pairs={{0,16},{16,0},{1,17},{17,1},{2,18},{18,2},{3,19},{19,3},{4,20},{20... | collective-permute-start | bytes 294920 | tf_op jit(solution)/shard_map/ppermute | solution.py:134
  4.4 0.1 broadcast_in_dim.14
  4.4 0.1 broadcast_in_dim.15
  4.5 0.0 copy-done
  4.5 0.6 %gather_fusion = bf16[2,3,3,48,16]{3,4,2,1,0:T(8,128)(2,1)S(1)} fusion(bf16[3,3,48,2,16]{2,4,3,1,0:T(8,128)(2,1)S(1)} %bitcast.17, s32[1024]{0:T(1024)S(1)} %pad_clamp_fusion), kind=kCustom, calls=%fused_computation | custom fusion | bytes 55304 | tf_op jit(solution)/shard_map/jit(_take)/gather | solution.py:137
  5.1 0.0 copy-start.1
  5.1 2.0 %collective-permute-done = bf16[8,16,384]{2,1,0:T(8,128)(2,1)S(1)} collective-permute-done((bf16[8,16,384]{2,1,0:T(8,128)(2,1)S(1)}, bf16[8,16,384]{2,1,0:T(8,128)(2,1)S(1)}, u32[]{:S(2)}, u32[]{:S(2)}) %collective-permute-start) | collective-permute-done | bytes 98336 | tf_op jit(solution)/shard_map/ppermute | solution.py:134
  7.2 1.3 %collective-permute-start.3 = (bf16[8,32,384]{2,1,0:T(8,128)(2,1)S(1)}, bf16[8,32,384]{2,1,0:T(8,128)(2,1)S(1)}, u32[]{:S(2)}, u32[]{:S(2)}) collective-permute-start(bf16[8,32,384]{2,1,0:T(8,128)(2,1)S(1)} %pad_maximum_fusion.own), channel_id=1, source_target_pairs={{1,0},{2,1},{3,2},{4,3},{5,4},{6,5},{7,6},{8,7},{9,8},{10,9},{11,1... | collective-permute-start | bytes 589832 | tf_op jit(solution)/shard_map/ppermute | solution.py:18
  8.5 3.0 %collective-permute-start.2 = (bf16[8,32,384]{2,1,0:T(8,128)(2,1)S(1)}, bf16[8,32,384]{2,1,0:T(8,128)(2,1)S(1)}, u32[]{:S(2)}, u32[]{:S(2)}) collective-permute-start(bf16[8,32,384]{2,1,0:T(8,128)(2,1)S(1)} %pad_maximum_fusion.own), channel_id=1, source_target_pairs={{0,1},{1,2},{2,3},{3,4},{4,5},{5,6},{6,7},{7,8},{8,9},{9,10},{10,1... | collective-permute-start | bytes 589832 | tf_op jit(solution)/shard_map/ppermute | solution.py:18
  11.5 3.7 %collective-permute-start.1 = (bf16[1,32,384]{2,1,0:T(8,128)(2,1)S(1)}, bf16[1,32,384]{2,1,0:T(8,128)(2,1)S(1)}, u32[]{:S(2)}, u32[]{:S(2)}) collective-permute-start(bf16[1,32,384]{2,1,0:T(8,128)(2,1)S(1)} %get-tuple-element.8), channel_id=1, source_target_pairs={{0,2},{1,3},{2,4},{3,5},{4,6},{5,7},{6,8},{7,9},{8,10},{9,11},{10,... | collective-permute-start | bytes 73736 | tf_op jit(solution)/shard_map/ppermute | solution.py:18
  15.2 1.3 %collective-permute-start.4 = (bf16[1,32,384]{2,1,0:T(8,128)(2,1)S(1)}, bf16[1,32,384]{2,1,0:T(8,128)(2,1)S(1)}, u32[]{:S(2)}, u32[]{:S(2)}) collective-permute-start(bf16[1,32,384]{2,1,0:T(8,128)(2,1)S(1)} %get-tuple-element.10), channel_id=1, source_target_pairs={{2,0},{3,1},{4,2},{5,3},{6,4},{7,5},{8,6},{9,7},{10,8},{11,9},{12,... | collective-permute-start | bytes 73736 | tf_op jit(solution)/shard_map/ppermute | solution.py:18
  16.5 0.1 bitcast_select_fusion
  16.6 0.1 copy.13.w1
  16.7 0.0 copy-done.1
  16.7 0.3 copy.12
  17.0 0.4 %reshape.68.wr = bf16[5,48,432]{2,1,0:T(8,128)(2,1)S(1)} reshape(bf16[5,48,3,3,48]{4,3,2,1,0:T(4,128)(2,1)S(1)} %copy.12) | data formatting | bytes 414720 | tf_op jit(solution)/shard_map/reshape | solution.py:139
  17.4 0.1 stack.15.place
  17.5 0.0 collective-permute-done.1.far_lo
  17.5 3.6 %collective-permute-done.4.far_hi = bf16[1,32,384]{2,1,0:T(8,128)(2,1)S(1)} collective-permute-done((bf16[1,32,384]{2,1,0:T(8,128)(2,1)S(1)}, bf16[1,32,384]{2,1,0:T(8,128)(2,1)S(1)}, u32[]{:S(2)}, u32[]{:S(2)}) %collective-permute-start.4) | collective-permute-done | bytes 24608 | tf_op jit(solution)/shard_map/ppermute | solution.py:18
  21.1 0.0 collective-permute-done.3.hi
  21.1 0.0 collective-permute-done.2.lo
  21.1 8.1 %shard_map.37 = f32[48,8,256]{2,1,0:T(8,128)} custom-call(s32[5]{0:T(128)S(1)} %stack.15.place, bf16[1,32,384]{2,1,0:T(8,128)(2,1)S(1)} %collective-permute-done.1.far_lo, bf16[8,32,384]{2,1,0:T(8,128)(2,1)S(1)} %collective-permute-done.2.lo, bf16[8,32,384]{2,1,0:T(8,128)(2,1)S(1)} %pad_maximum_fusion.own, ...), custom_call_target="tpu_custom_call" | custom-call | tf_op jit(solution)/shard_map/pallas_call | solution.py:154
  (6 shorter events, 0.1 us)
Async XLA Ops:
  0.0 4.5 %copy-start = (bf16[3,3,48,32]{2,3,1,0:T(8,128)(2,1)S(1)}, bf16[3,3,48,32]{2,3,1,0:T(8,128)(2,1)}, u32[]{:S(2)}) copy-start(bf16[3,3,48,32]{2,3,1,0:T(8,128)(2,1)} %param.4) | copy-start | bytes 82948
  1.3 5.8 %collective-permute-start = (bf16[8,16,384]{2,1,0:T(8,128)(2,1)S(1)}, bf16[8,16,384]{2,1,0:T(8,128)(2,1)S(1)}, u32[]{:S(2)}, u32[]{:S(2)}) collective-permute-start(bf16[8,16,384]{2,1,0:T(8,128)(2,1)S(1)} %get-tuple-element.14), channel_id=1, source_target_pairs={{0,16},{16,0},{1,17},{17,1},{2,18},{18,2},{3,19},{19,3},{4,20},{20... | collective-permute-start | bytes 294920 | tf_op jit(solution)/shard_map/ppermute | solution.py:134
  5.1 11.6 %copy-start.1 = (bf16[5,3,3,48,48]{4,3,2,1,0:T(8,128)(2,1)S(1)}, bf16[5,3,3,48,48]{4,3,2,1,0:T(8,128)(2,1)}, u32[]{:S(2)}) copy-start(bf16[5,3,3,48,48]{4,3,2,1,0:T(8,128)(2,1)} %param.5) | copy-start | bytes 622084
  7.2 14.0 %collective-permute-start.3 = (bf16[8,32,384]{2,1,0:T(8,128)(2,1)S(1)}, bf16[8,32,384]{2,1,0:T(8,128)(2,1)S(1)}, u32[]{:S(2)}, u32[]{:S(2)}) collective-permute-start(bf16[8,32,384]{2,1,0:T(8,128)(2,1)S(1)} %pad_maximum_fusion.own), channel_id=1, source_target_pairs={{1,0},{2,1},{3,2},{4,3},{5,4},{6,5},{7,6},{8,7},{9,8},{10,9},{11,1... | collective-permute-start | bytes 589832 | tf_op jit(solution)/shard_map/ppermute | solution.py:18
  8.5 12.7 %collective-permute-start.2 = (bf16[8,32,384]{2,1,0:T(8,128)(2,1)S(1)}, bf16[8,32,384]{2,1,0:T(8,128)(2,1)S(1)}, u32[]{:S(2)}, u32[]{:S(2)}) collective-permute-start(bf16[8,32,384]{2,1,0:T(8,128)(2,1)S(1)} %pad_maximum_fusion.own), channel_id=1, source_target_pairs={{0,1},{1,2},{2,3},{3,4},{4,5},{5,6},{6,7},{7,8},{8,9},{9,10},{10,1... | collective-permute-start | bytes 589832 | tf_op jit(solution)/shard_map/ppermute | solution.py:18
  11.5 6.0 %collective-permute-start.1 = (bf16[1,32,384]{2,1,0:T(8,128)(2,1)S(1)}, bf16[1,32,384]{2,1,0:T(8,128)(2,1)S(1)}, u32[]{:S(2)}, u32[]{:S(2)}) collective-permute-start(bf16[1,32,384]{2,1,0:T(8,128)(2,1)S(1)} %get-tuple-element.8), channel_id=1, source_target_pairs={{0,2},{1,3},{2,4},{3,5},{4,6},{5,7},{6,8},{7,9},{8,10},{9,11},{10,... | collective-permute-start | bytes 73736 | tf_op jit(solution)/shard_map/ppermute | solution.py:18
  15.2 5.9 %collective-permute-start.4 = (bf16[1,32,384]{2,1,0:T(8,128)(2,1)S(1)}, bf16[1,32,384]{2,1,0:T(8,128)(2,1)S(1)}, u32[]{:S(2)}, u32[]{:S(2)}) collective-permute-start(bf16[1,32,384]{2,1,0:T(8,128)(2,1)S(1)} %get-tuple-element.10), channel_id=1, source_target_pairs={{2,0},{3,1},{4,2},{5,3},{6,4},{7,5},{8,6},{9,7},{10,8},{11,9},{12,... | collective-permute-start | bytes 73736 | tf_op jit(solution)/shard_map/ppermute | solution.py:18

commit v3 on v2

--- a/solution.py
+++ b/solution.py
@@ -30,7 +30,7 @@
     return pltpu.roll(x, by % x.shape[-1], x.ndim - 1)
 
 
-def body(place, far_lo, lo, own, hi, far_hi, w1, wr, out, inten, act_a, act_b):
+def body(place, far, lo, own, hi, w1, wr, out, inten, act_a, act_b):
     acqs, width = own.shape[1:]
     cols = own.shape[0]
     tile = out.shape[2]
@@ -42,7 +42,8 @@
     inside = (lane >= offset - MARGIN) & (lane < offset + tile + MARGIN)
     row_mask = inside.astype(jnp.float32)
 
-    pieces = [(far_lo, 0, HALO - cols), (lo, 0, cols), (own, 0, cols), (hi, 0, cols), (far_hi, 0, HALO - cols)]
+    more = HALO - cols
+    pieces = [(far, 0, more), (lo, 0, cols), (own, 0, cols), (hi, 0, cols), (far, more, more)]
     at = 0
     for ref, start, count in pieces:
         for k in range(count):
@@ -127,23 +128,28 @@
 
     coded = jnp.log(intensity).astype(jnp.bfloat16).transpose(1, 0, 2)
     base = window_base(m, tile, rows)
-    parts = [lax.dynamic_slice_in_dim(coded, base, width, axis=2)]
-    for d in range(1, tm):
-        to = window_base((m + d) % tm, tile, rows)
-        piece = lax.dynamic_slice_in_dim(coded, to, width, axis=2)
-        parts.append(lax.ppermute(piece, "tm", [(i, (i + d) % tm) for i in range(tm)]))
-    own = jnp.concatenate(parts, axis=1)
+
+    def gathered(x):
+        parts = [lax.dynamic_slice_in_dim(x, base, width, axis=2)]
+        for d in range(1, tm):
+            to = window_base((m + d) % tm, tile, rows)
+            piece = lax.dynamic_slice_in_dim(x, to, width, axis=2)
+            parts.append(lax.ppermute(piece, "tm", [(i, (i + d) % tm) for i in range(tm)]))
+        return jnp.concatenate(parts, axis=1)
+
+    far = HALO - cols
+    own = gathered(coded)
+    far_own = jnp.concatenate(
+        [shifted(coded[cols - far :], "space", 2), shifted(coded[:far], "space", -2)], axis=0
+    )
+    far_cols = gathered(far_own)
+    lo = shifted(own, "space", 1)
+    hi = shifted(own, "space", -1)
+
     order = (m - jnp.arange(tm)) % tm
     w1 = jnp.take(w_first.reshape(3, 3, channels, tm, acqs_own), order, axis=3)
     w1 = w1.reshape(3, 3, channels, acqs).transpose(2, 0, 1, 3).reshape(channels, 9 * acqs)
     wr = w_rest.transpose(0, 3, 1, 2, 4).reshape(LAYERS - 1, channels, 9 * channels)
-
-    far = HALO - cols
-    own, first, final = lax.optimization_barrier((own, own[:far], own[cols - far :]))
-    far_lo = shifted(final, "space", 2)
-    far_hi = shifted(first, "space", -2)
-    lo = shifted(own, "space", 1)
-    hi = shifted(own, "space", -1)
 
     place = jnp.stack(
         [s * cols, jnp.int32(cols * space), base, jnp.int32(rows), m * tile - base]
@@ -154,7 +160,7 @@
     return pl.pallas_call(
         body,
         out_shape=jax.ShapeDtypeStruct((channels, cols, tile), jnp.float32),
-        in_specs=[pl.BlockSpec(memory_space=pltpu.SMEM)] + [vmem] * 7,
+        in_specs=[pl.BlockSpec(memory_space=pltpu.SMEM)] + [vmem] * 6,
         out_specs=vmem,
         scratch_shapes=[
             pltpu.VMEM((cols + 2 * HALO, acqs, width), jnp.float32),
@@ -162,7 +168,7 @@
             pltpu.VMEM(act, jnp.bfloat16),
         ],
         compiler_params=pltpu.CompilerParams(vmem_limit_bytes=40 * 1024 * 1024),
-    )(place, far_lo, lo, own, hi, far_hi, w1, wr)
+    )(place, far_cols, lo, own, hi, w1, wr)
 
 
 def solution(mesh):

time: 29.4 us -> 30.9 us (1.051)
  the two profiles are of different devices: /device:TPU:0 before, /device:TPU:24 now
where the time goes in v3:
time: 30.9 us; the launch traced here: 30.6 us
  starting transfers between devices  13.3 us (43%)
  Pallas kernels  8.07 us (26%)
  waiting for transfers between devices  5.72 us (19%)
  local copies, waits for them, and re-layouts  1.84 us (6%)
  other arithmetic  1.5 us (5%)
    ppermute x4, starting transfers between devices, shifted(): return lax.ppermute(x, axis, pairs)  10.2 us
    pallas_call x1, Pallas kernels, shards(): pl.pallas_call(body, out_shape=jax.ShapeDtypeStruct((channels, cols, tile...  8.07 us
    ppermute x4, waiting for transfers between devices, shifted(): return lax.ppermute(x, axis, pairs)  5.72 us
    ppermute x2, starting transfers between devices, gathered(): lax.ppermute(piece, 'tm', [(i, (i + d) % tm) for i in range(tm)])  3.17 us
    transpose x1, other arithmetic, shards(): coded = jnp.log(intensity).astype(jnp.bfloat16).transpose(1, 0, 2)  1.19 us
  transfers between devices with their start and end apart: 6, of which 2 were waited for; matrix products, arithmetic and copies ran while one was open for 7% of the time, Pallas kernels for 0%

profile of v3, /device:TPU:24, one launch (start us, length us, event | category | flops | bytes accessed | tf_op | source)
XLA Modules:
  0.0 30.6 jit_solution(9040251463229627451)
XLA Ops:
  0.0 0.0 copy-start
  0.0 0.0 copy-start.1
  0.0 1.2 %fusion.5 = bf16[8,16,512]{2,1,0:T(8,128)(2,1)S(1)} fusion(f32[16,8,512]{2,1,0:T(8,128)} %param.3), kind=kLoop, calls=%fused_computation.26 | loop fusion | flops 65536 | bytes 393216 | tf_op jit(solution)/shard_map/transpose | solution.py:129
  1.2 3.3 %collective-permute-start.1 = (bf16[1,16,512]{2,1,0:T(8,128)(2,1)S(1)}, bf16[1,16,512]{2,1,0:T(8,128)(2,1)S(1)}, u32[]{:S(2)}, u32[]{:S(2)}) collective-permute-start(bf16[1,16,512]{2,1,0:T(8,128)(2,1)S(1)} %get-tuple-element.7), channel_id=1, source_target_pairs={{2,0},{3,1},{4,2},{5,3},{6,4},{7,5},{8,6},{9,7},{10,8},{11,9},{12,... | collective-permute-start | bytes 49160 | tf_op jit(solution)/shard_map/ppermute | solution.py:18
  4.5 2.6 %collective-permute-start = (bf16[1,16,512]{2,1,0:T(8,128)(2,1)S(1)}, bf16[1,16,512]{2,1,0:T(8,128)(2,1)S(1)}, u32[]{:S(2)}, u32[]{:S(2)}) collective-permute-start(bf16[1,16,512]{2,1,0:T(8,128)(2,1)S(1)} %get-tuple-element.8), channel_id=1, source_target_pairs={{0,2},{1,3},{2,4},{3,5},{4,6},{5,7},{6,8},{7,9},{8,10},{9,11},{10,... | collective-permute-start | bytes 49160 | tf_op jit(solution)/shard_map/ppermute | solution.py:18
  7.1 0.0 copy-done.1
  7.1 0.2 fusion
  7.3 0.1 dynamic-slice_bitcast_fusion.1
  7.4 1.6 %collective-permute-start.3 = (bf16[8,16,384]{2,1,0:T(8,128)(2,1)S(1)}, bf16[8,16,384]{2,1,0:T(8,128)(2,1)S(1)}, u32[]{:S(2)}, u32[]{:S(2)}) collective-permute-start(bf16[8,16,384]{2,1,0:T(8,128)(2,1)S(1)} %get-tuple-element.6), channel_id=1, source_target_pairs={{0,16},{16,0},{1,17},{17,1},{2,18},{18,2},{3,19},{19,3},{4,20},{20... | collective-permute-start | bytes 294920 | tf_op jit(solution)/shard_map/ppermute | solution.py:137
  9.0 0.1 broadcast_in_dim.14
  9.1 0.1 broadcast_in_dim.15
  9.2 0.0 copy-done
  9.2 0.6 %gather_fusion = bf16[2,3,3,48,16]{3,4,2,1,0:T(8,128)(2,1)S(1)} fusion(bf16[3,3,48,2,16]{2,4,3,1,0:T(8,128)(2,1)S(1)} %bitcast.19, s32[1024]{0:T(1024)S(1)} %pad_clamp_fusion), kind=kCustom, calls=%fused_computation | custom fusion | bytes 55304 | tf_op jit(solution)/shard_map/jit(_take)/gather | solution.py:150
  9.8 0.0 copy-start.2
  9.8 1.2 %collective-permute-done = bf16[1,16,512]{2,1,0:T(8,128)(2,1)S(1)} collective-permute-done((bf16[1,16,512]{2,1,0:T(8,128)(2,1)S(1)}, bf16[1,16,512]{2,1,0:T(8,128)(2,1)S(1)}, u32[]{:S(2)}, u32[]{:S(2)}) %collective-permute-start) | collective-permute-done | bytes 16416 | tf_op jit(solution)/shard_map/ppermute | solution.py:18
  11.0 0.0 collective-permute-done.1
  11.0 0.1 constant_dynamic-slice_fusion.1
  11.1 1.6 %collective-permute-start.2 = (bf16[2,16,384]{2,1,0:T(8,128)(2,1)S(1)}, bf16[2,16,384]{2,1,0:T(8,128)(2,1)S(1)}, u32[]{:S(2)}, u32[]{:S(2)}) collective-permute-start(bf16[2,16,384]{2,1,0:T(8,128)(2,1)S(1)} %get-tuple-element.10), channel_id=1, source_target_pairs={{0,16},{16,0},{1,17},{17,1},{2,18},{18,2},{3,19},{19,3},{4,20},{20... | collective-permute-start | bytes 73736 | tf_op jit(solution)/shard_map/ppermute | solution.py:137
  12.7 0.0 collective-permute-done.3
  12.8 1.9 %collective-permute-start.5 = (bf16[8,32,384]{2,1,0:T(8,128)(2,1)S(1)}, bf16[8,32,384]{2,1,0:T(8,128)(2,1)S(1)}, u32[]{:S(2)}, u32[]{:S(2)}) collective-permute-start(bf16[8,32,384]{2,1,0:T(8,128)(2,1)S(1)} %pad_maximum_fusion.own), channel_id=1, source_target_pairs={{1,0},{2,1},{3,2},{4,3},{5,4},{6,5},{7,6},{8,7},{9,8},{10,9},{11,1... | collective-permute-start | bytes 589832 | tf_op jit(solution)/shard_map/ppermute | solution.py:18
  14.7 2.4 %collective-permute-start.4 = (bf16[8,32,384]{2,1,0:T(8,128)(2,1)S(1)}, bf16[8,32,384]{2,1,0:T(8,128)(2,1)S(1)}, u32[]{:S(2)}, u32[]{:S(2)}) collective-permute-start(bf16[8,32,384]{2,1,0:T(8,128)(2,1)S(1)} %pad_maximum_fusion.own), channel_id=1, source_target_pairs={{0,1},{1,2},{2,3},{3,4},{4,5},{5,6},{6,7},{7,8},{8,9},{9,10},{10,1... | collective-permute-start | bytes 589832 | tf_op jit(solution)/shard_map/ppermute | solution.py:18
  17.1 0.1 bitcast_select_fusion
  17.2 0.1 copy.13.w1
  17.3 0.0 copy-done.2
  17.3 0.3 copy.12
  17.6 0.4 %reshape.68.wr = bf16[5,48,432]{2,1,0:T(8,128)(2,1)S(1)} reshape(bf16[5,48,3,3,48]{4,3,2,1,0:T(4,128)(2,1)S(1)} %copy.12) | data formatting | bytes 414720 | tf_op jit(solution)/shard_map/reshape | solution.py:152
  18.0 0.1 stack.15.place
  18.1 0.0 collective-permute-done.2
  18.1 0.0 collective-permute-done.5.hi
  18.1 4.5 %collective-permute-done.4.lo = bf16[8,32,384]{2,1,0:T(8,128)(2,1)S(1)} collective-permute-done((bf16[8,32,384]{2,1,0:T(8,128)(2,1)S(1)}, bf16[8,32,384]{2,1,0:T(8,128)(2,1)S(1)}, u32[]{:S(2)}, u32[]{:S(2)}) %collective-permute-start.4) | collective-permute-done | bytes 196640 | tf_op jit(solution)/shard_map/ppermute | solution.py:18
  22.6 8.1 %shard_map.37 = f32[48,8,256]{2,1,0:T(8,128)} custom-call(s32[5]{0:T(128)S(1)} %stack.15.place, bf16[2,32,384]{2,1,0:T(8,128)(2,1)S(1)} %pad_maximum_fusion.1.far, bf16[8,32,384]{2,1,0:T(8,128)(2,1)S(1)} %collective-permute-done.4.lo, bf16[8,32,384]{2,1,0:T(8,128)(2,1)S(1)} %pad_maximum_fusion.own, bf16[8,32,384]{2,1,0:T(8,128)(2,1)S(1)} %collective-permute-done.5.hi, ...), custom_call_target="tpu_custom_call" | custom-call | tf_op jit(solution)/shard_map/pallas_call | solution.py:160
  (9 shorter events, 0.1 us)
Async XLA Ops:
  0.0 9.2 %copy-start = (bf16[3,3,48,32]{2,3,1,0:T(8,128)(2,1)S(1)}, bf16[3,3,48,32]{2,3,1,0:T(8,128)(2,1)}, u32[]{:S(2)}) copy-start(bf16[3,3,48,32]{2,3,1,0:T(8,128)(2,1)} %param.4) | copy-start | bytes 82948
  0.0 7.1 %copy-start.1 = (f32[16,8,512]{2,1,0:T(8,128)S(1)}, f32[16,8,512]{2,1,0:T(8,128)}, u32[]{:S(2)}) copy-start(f32[16,8,512]{2,1,0:T(8,128)} %param.3) | copy-start | bytes 786436
  1.2 9.8 %collective-permute-start.1 = (bf16[1,16,512]{2,1,0:T(8,128)(2,1)S(1)}, bf16[1,16,512]{2,1,0:T(8,128)(2,1)S(1)}, u32[]{:S(2)}, u32[]{:S(2)}) collective-permute-start(bf16[1,16,512]{2,1,0:T(8,128)(2,1)S(1)} %get-tuple-element.7), channel_id=1, source_target_pairs={{2,0},{3,1},{4,2},{5,3},{6,4},{7,5},{8,6},{9,7},{10,8},{11,9},{12,... | collective-permute-start | bytes 49160 | tf_op jit(solution)/shard_map/ppermute | solution.py:18
  4.5 6.5 %collective-permute-start = (bf16[1,16,512]{2,1,0:T(8,128)(2,1)S(1)}, bf16[1,16,512]{2,1,0:T(8,128)(2,1)S(1)}, u32[]{:S(2)}, u32[]{:S(2)}) collective-permute-start(bf16[1,16,512]{2,1,0:T(8,128)(2,1)S(1)} %get-tuple-element.8), channel_id=1, source_target_pairs={{0,2},{1,3},{2,4},{3,5},{4,6},{5,7},{6,8},{7,9},{8,10},{9,11},{10,... | collective-permute-start | bytes 49160 | tf_op jit(solution)/shard_map/ppermute | solution.py:18
  7.4 5.3 %collective-permute-start.3 = (bf16[8,16,384]{2,1,0:T(8,128)(2,1)S(1)}, bf16[8,16,384]{2,1,0:T(8,128)(2,1)S(1)}, u32[]{:S(2)}, u32[]{:S(2)}) collective-permute-start(bf16[8,16,384]{2,1,0:T(8,128)(2,1)S(1)} %get-tuple-element.6), channel_id=1, source_target_pairs={{0,16},{16,0},{1,17},{17,1},{2,18},{18,2},{3,19},{19,3},{4,20},{20... | collective-permute-start | bytes 294920 | tf_op jit(solution)/shard_map/ppermute | solution.py:137
  9.8 7.5 %copy-start.2 = (bf16[5,3,3,48,48]{4,3,2,1,0:T(8,128)(2,1)S(1)}, bf16[5,3,3,48,48]{4,3,2,1,0:T(8,128)(2,1)}, u32[]{:S(2)}) copy-start(bf16[5,3,3,48,48]{4,3,2,1,0:T(8,128)(2,1)} %param.5) | copy-start | bytes 622084
  11.1 6.9 %collective-permute-start.2 = (bf16[2,16,384]{2,1,0:T(8,128)(2,1)S(1)}, bf16[2,16,384]{2,1,0:T(8,128)(2,1)S(1)}, u32[]{:S(2)}, u32[]{:S(2)}) collective-permute-start(bf16[2,16,384]{2,1,0:T(8,128)(2,1)S(1)} %get-tuple-element.10), channel_id=1, source_target_pairs={{0,16},{16,0},{1,17},{17,1},{2,18},{18,2},{3,19},{19,3},{4,20},{20... | collective-permute-start | bytes 73736 | tf_op jit(solution)/shard_map/ppermute | solution.py:137
  12.8 5.3 %collective-permute-start.5 = (bf16[8,32,384]{2,1,0:T(8,128)(2,1)S(1)}, bf16[8,32,384]{2,1,0:T(8,128)(2,1)S(1)}, u32[]{:S(2)}, u32[]{:S(2)}) collective-permute-start(bf16[8,32,384]{2,1,0:T(8,128)(2,1)S(1)} %pad_maximum_fusion.own), channel_id=1, source_target_pairs={{1,0},{2,1},{3,2},{4,3},{5,4},{6,5},{7,6},{8,7},{9,8},{10,9},{11,1... | collective-permute-start | bytes 589832 | tf_op jit(solution)/shard_map/ppermute | solution.py:18
  14.7 7.9 %collective-permute-start.4 = (bf16[8,32,384]{2,1,0:T(8,128)(2,1)S(1)}, bf16[8,32,384]{2,1,0:T(8,128)(2,1)S(1)}, u32[]{:S(2)}, u32[]{:S(2)}) collective-permute-start(bf16[8,32,384]{2,1,0:T(8,128)(2,1)S(1)} %pad_maximum_fusion.own), channel_id=1, source_target_pairs={{0,1},{1,2},{2,3},{3,4},{4,5},{5,6},{6,7},{7,8},{8,9},{9,10},{10,1... | collective-permute-start | bytes 589832 | tf_op jit(solution)/shard_map/ppermute | solution.py:18

commit v4 on v2

--- a/solution.py
+++ b/solution.py
@@ -12,10 +12,19 @@
 LANES = 128
 
 
-def shifted(x, axis, by):
-    size = lax.axis_size(axis)
-    pairs = [(i, i + by) for i in range(size) if 0 <= i + by < size]
-    return lax.ppermute(x, axis, pairs)
+def paired(x, by, phase):
+    size, groups = lax.axis_size("space"), lax.axis_size("tm")
+    low = [i for i in range(size - by) if (i // by) % 2 == phase]
+    partner = {i: i + by for i in low} | {i + by: i for i in low}
+    alone = [i for i in range(size) if i not in partner]
+    pairs = [(g * size + i, g * size + j) for g in range(groups) for i, j in partner.items()]
+    if groups % 2 == 0:
+        pairs += [(g * size + i, (g ^ 1) * size + i) for g in range(groups) for i in alone]
+    else:
+        pairs += [
+            (g * size + i, g * size + j) for g in range(groups) for i, j in zip(alone, reversed(alone))
+        ]
+    return lax.ppermute(x, ("tm", "space"), pairs)
 
 
 def window_rows(tile, rows):
@@ -30,7 +39,7 @@
     return pltpu.roll(x, by % x.shape[-1], x.ndim - 1)
 
 
-def body(place, far_lo, lo, own, hi, far_hi, w1, wr, out, inten, act_a, act_b):
+def body(place, far_in, far_out, own, mate, next_to, w1, wr, out, inten, act_a, act_b):
     acqs, width = own.shape[1:]
     cols = own.shape[0]
     tile = out.shape[2]
@@ -42,11 +51,17 @@
     inside = (lane >= offset - MARGIN) & (lane < offset + tile + MARGIN)
     row_mask = inside.astype(jnp.float32)
 
-    pieces = [(far_lo, 0, HALO - cols), (lo, 0, cols), (own, 0, cols), (hi, 0, cols), (far_hi, 0, HALO - cols)]
+    odd, odd_pair = place[5] == 1, place[6] == 1
+    more = HALO - cols
+    pieces = [(far_out, far_in, odd_pair, more), (next_to, mate, odd, cols), (own, own, None, cols)]
+    pieces += [(mate, next_to, odd, cols), (far_in, far_out, odd_pair, more)]
     at = 0
-    for ref, start, count in pieces:
+    for ref, other, use_other, count in pieces:
         for k in range(count):
-            inten[at] = jnp.where(inside, jnp.exp(ref[start + k].astype(jnp.float32)), 0.0)
+            coded = ref[k].astype(jnp.float32)
+            if use_other is not None:
+                coded = jnp.where(use_other, other[k].astype(jnp.float32), coded)
+            inten[at] = jnp.where(inside, jnp.exp(coded), 0.0)
             at += 1
 
     feature_cols = cols + 2 * LAYERS
@@ -139,14 +154,17 @@
     wr = w_rest.transpose(0, 3, 1, 2, 4).reshape(LAYERS - 1, channels, 9 * channels)
 
     far = HALO - cols
-    own, first, final = lax.optimization_barrier((own, own[:far], own[cols - far :]))
-    far_lo = shifted(final, "space", 2)
-    far_hi = shifted(first, "space", -2)
-    lo = shifted(own, "space", 1)
-    hi = shifted(own, "space", -1)
+    head, tail = own[:far], own[cols - far :]
+    low = (s // 2) % 2 == 0
+    inner, outer = jnp.where(low, tail, head), jnp.where(low, head, tail)
+    own, inner, outer = lax.optimization_barrier((own, inner, outer))
+    far_in = paired(inner, 2, 0)
+    far_out = paired(outer, 2, 1)
+    mate = paired(own, 1, 0)
+    next_to = paired(own, 1, 1)
 
     place = jnp.stack(
-        [s * cols, jnp.int32(cols * space), base, jnp.int32(rows), m * tile - base]
+        [s * cols, jnp.int32(cols * space), base, jnp.int32(rows), m * tile - base, s % 2, (s // 2) % 2]
     ).astype(jnp.int32)
     vmem = pl.BlockSpec(memory_space=pltpu.VMEM)
     feature_cols = cols + 2 * LAYERS
@@ -162,7 +180,7 @@
             pltpu.VMEM(act, jnp.bfloat16),
         ],
         compiler_params=pltpu.CompilerParams(vmem_limit_bytes=40 * 1024 * 1024),
-    )(place, far_lo, lo, own, hi, far_hi, w1, wr)
+    )(place, far_in, far_out, own, mate, next_to, w1, wr)
 
 
 def solution(mesh):

time: 29.4 us -> 22.8 us (0.78)
  starting transfers between devices: 12.3 us -> 8.07 us
  waiting for transfers between devices: 5.63 us -> 3.33 us
    ppermute x4, starting transfers between devices: 9.32 us -> 5.04 us  [paired(): return lax.ppermute(x, ('tm', 'space'), pairs)]
    ppermute x4, waiting for transfers between devices: 3.64 us -> 1.34 us  [paired(): return lax.ppermute(x, ('tm', 'space'), pairs)]
  transfers between devices with their start and end apart: 5 -> 5, of which waited for: 2 -> 2; matrix products, arithmetic and copies ran while one was open for 6% -> 7% of each run, Pallas kernels for 0% -> 0%
where the time goes in v4:
time: 22.8 us; the launch traced here: 22.7 us
  Pallas kernels  8.13 us (36%)
  starting transfers between devices  8.07 us (35%)
  waiting for transfers between devices  3.33 us (15%)
  local copies, waits for them, and re-layouts  1.74 us (8%)
  other arithmetic  1.3 us (6%)
    pallas_call x1, Pallas kernels, shards(): pl.pallas_call(body, out_shape=jax.ShapeDtypeStruct((channels, cols, tile...  8.13 us
    ppermute x4, starting transfers between devices, paired(): return lax.ppermute(x, ('tm', 'space'), pairs)  5.04 us
    ppermute x1, starting transfers between devices, shards(): lax.ppermute(piece, 'tm', [(i, (i + d) % tm) for i in range(tm)])  3.03 us
    ppermute x1, waiting for transfers between devices, shards(): lax.ppermute(piece, 'tm', [(i, (i + d) % tm) for i in range(tm)])  1.98 us
    ppermute x4, waiting for transfers between devices, paired(): return lax.ppermute(x, ('tm', 'space'), pairs)  1.34 us
    convert_element_type x1, other arithmetic, shards(): coded = jnp.log(intensity).astype(jnp.bfloat16).transpose(1, 0, 2)  1.15 us
    gather x2, local copies, waits for them, and re-layouts, shards(): w1 = jnp.take(w_first.reshape(3, 3, channels, tm, acqs_own), order, axis=3)  0.57 us
  transfers between devices with their start and end apart: 5, of which 2 were waited for; matrix products, arithmetic and copies ran while one was open for 7% of the time, Pallas kernels for 0%

profile of v4, /device:TPU:0, one launch (start us, length us, event | category | flops | bytes accessed | tf_op | source)
XLA Modules:
  0.0 22.7 jit_solution(18106722339596732742)
XLA Ops:
  0.0 0.0 copy-start
  0.0 1.1 %fusion = bf16[16,8,512]{2,0,1:T(8,128)(2,1)S(1)} fusion(f32[16,8,512]{2,1,0:T(8,128)} %param.3), kind=kLoop, calls=%fused_computation.2 | loop fusion | flops 65536 | bytes 393216 | tf_op jit(solution)/shard_map/convert_element_type | solution.py:143
  1.1 0.1 dynamic-slice_bitcast_fusion.1
  1.3 3.0 %collective-permute-start = (bf16[8,16,384]{2,1,0:T(8,128)(2,1)S(1)}, bf16[8,16,384]{2,1,0:T(8,128)(2,1)S(1)}, u32[]{:S(2)}, u32[]{:S(2)}) collective-permute-start(bf16[8,16,384]{2,1,0:T(8,128)(2,1)S(1)} %get-tuple-element.15), channel_id=1, source_target_pairs={{0,16},{16,0},{1,17},{17,1},{2,18},{18,2},{3,19},{19,3},{4,20},{20... | collective-permute-start | bytes 294920 | tf_op jit(solution)/shard_map/ppermute | solution.py:149
  4.4 0.1 broadcast_in_dim.14
  4.4 0.1 broadcast_in_dim.15
  4.5 0.0 copy-done
  4.5 0.6 %gather_fusion = bf16[2,3,3,48,16]{3,4,2,1,0:T(8,128)(2,1)S(1)} fusion(bf16[3,3,48,2,16]{2,4,3,1,0:T(8,128)(2,1)S(1)} %bitcast.19, s32[1024]{0:T(1024)S(1)} %pad_clamp_fusion), kind=kCustom, calls=%fused_computation | custom fusion | bytes 55304 | tf_op jit(solution)/shard_map/jit(_take)/gather | solution.py:152
  5.1 0.0 copy-start.1
  5.1 2.0 %collective-permute-done = bf16[8,16,384]{2,1,0:T(8,128)(2,1)S(1)} collective-permute-done((bf16[8,16,384]{2,1,0:T(8,128)(2,1)S(1)}, bf16[8,16,384]{2,1,0:T(8,128)(2,1)S(1)}, u32[]{:S(2)}, u32[]{:S(2)}) %collective-permute-start) | collective-permute-done | bytes 98336 | tf_op jit(solution)/shard_map/ppermute | solution.py:149
  7.2 1.9 %collective-permute-start.4 = (bf16[8,32,384]{2,1,0:T(8,128)(2,1)S(1)}, bf16[8,32,384]{2,1,0:T(8,128)(2,1)S(1)}, u32[]{:S(2)}, u32[]{:S(2)}) collective-permute-start(bf16[8,32,384]{2,1,0:T(8,128)(2,1)S(1)} %pad_maximum_fusion.own), channel_id=1, source_target_pairs={{1,2},{3,4},{5,6},{7,8},{9,10},{11,12},{13,14},{2,1},{4,3},{6,5},{... | collective-permute-start | bytes 589832 | tf_op jit(solution)/shard_map/ppermute | solution.py:27
  9.1 0.1 collective-permute-start.3
  9.2 1.5 %collective-permute-start.1 = (bf16[1,32,384]{2,1,0:T(8,128)(2,1)S(1)}, bf16[1,32,384]{2,1,0:T(8,128)(2,1)S(1)}, u32[]{:S(2)}, u32[]{:S(2)}) collective-permute-start(bf16[1,32,384]{2,1,0:T(8,128)(2,1)S(1)} %broadcast_select_fusion.1), channel_id=1, source_target_pairs={{0,2},{1,3},{4,6},{5,7},{8,10},{9,11},{12,14},{13,15},{2,0},{3,1},... | collective-permute-start | bytes 73736 | tf_op jit(solution)/shard_map/ppermute | solution.py:27
  10.7 1.5 %collective-permute-start.2 = (bf16[1,32,384]{2,1,0:T(8,128)(2,1)S(1)}, bf16[1,32,384]{2,1,0:T(8,128)(2,1)S(1)}, u32[]{:S(2)}, u32[]{:S(2)}) collective-permute-start(bf16[1,32,384]{2,1,0:T(8,128)(2,1)S(1)} %get-tuple-element.9), channel_id=1, source_target_pairs={{2,4},{3,5},{6,8},{7,9},{10,12},{11,13},{4,2},{5,3},{8,6},{9,7},{1... | collective-permute-start | bytes 73736 | tf_op jit(solution)/shard_map/ppermute | solution.py:27
  12.2 0.1 bitcast_select_fusion
  12.3 0.1 copy.13.w1
  12.4 0.0 copy-done.1
  12.4 0.3 %copy.12 = bf16[5,48,3,3,48]{4,3,2,1,0:T(4,128)(2,1)S(1)} copy(bf16[5,48,3,3,48]{4,1,3,2,0:T(8,128)(2,1)S(1)} %bitcast.21) | data formatting | bytes 414720 | tf_op jit(solution)/shard_map/transpose | solution.py:154
  12.7 0.4 %reshape.68.wr = bf16[5,48,432]{2,1,0:T(8,128)(2,1)S(1)} reshape(bf16[5,48,3,3,48]{4,3,2,1,0:T(4,128)(2,1)S(1)} %copy.12) | data formatting | bytes 414720 | tf_op jit(solution)/shard_map/reshape | solution.py:154
  13.1 0.1 stack.23.place
  13.2 0.0 collective-permute-done.1.far_in
  13.2 1.3 %collective-permute-done.2.far_out = bf16[1,32,384]{2,1,0:T(8,128)(2,1)S(1)} collective-permute-done((bf16[1,32,384]{2,1,0:T(8,128)(2,1)S(1)}, bf16[1,32,384]{2,1,0:T(8,128)(2,1)S(1)}, u32[]{:S(2)}, u32[]{:S(2)}) %collective-permute-start.2) | collective-permute-done | bytes 24608 | tf_op jit(solution)/shard_map/ppermute | solution.py:27
  14.5 0.0 collective-permute-done.4.next_to
  14.5 0.0 collective-permute-done.3.mate
  14.5 8.1 %shard_map.37 = f32[48,8,256]{2,1,0:T(8,128)} custom-call(s32[7]{0:T(128)S(1)} %stack.23.place, bf16[1,32,384]{2,1,0:T(8,128)(2,1)S(1)} %collective-permute-done.1.far_in, bf16[1,32,384]{2,1,0:T(8,128)(2,1)S(1)} %collective-permute-done.2.far_out, bf16[8,32,384]{2,1,0:T(8,128)(2,1)S(1)} %pad_maximum_fusion.own, ...), custom_call_target="tpu_custom_call" | custom-call | tf_op jit(solution)/shard_map/pallas_call | solution.py:172
  (7 shorter events, 0.1 us)
Async XLA Ops:
  0.0 4.5 %copy-start = (bf16[3,3,48,32]{2,3,1,0:T(8,128)(2,1)S(1)}, bf16[3,3,48,32]{2,3,1,0:T(8,128)(2,1)}, u32[]{:S(2)}) copy-start(bf16[3,3,48,32]{2,3,1,0:T(8,128)(2,1)} %param.4) | copy-start | bytes 82948
  1.3 5.8 %collective-permute-start = (bf16[8,16,384]{2,1,0:T(8,128)(2,1)S(1)}, bf16[8,16,384]{2,1,0:T(8,128)(2,1)S(1)}, u32[]{:S(2)}, u32[]{:S(2)}) collective-permute-start(bf16[8,16,384]{2,1,0:T(8,128)(2,1)S(1)} %get-tuple-element.15), channel_id=1, source_target_pairs={{0,16},{16,0},{1,17},{17,1},{2,18},{18,2},{3,19},{19,3},{4,20},{20... | collective-permute-start | bytes 294920 | tf_op jit(solution)/shard_map/ppermute | solution.py:149
  5.1 7.3 %copy-start.1 = (bf16[5,3,3,48,48]{4,3,2,1,0:T(8,128)(2,1)S(1)}, bf16[5,3,3,48,48]{4,3,2,1,0:T(8,128)(2,1)}, u32[]{:S(2)}) copy-start(bf16[5,3,3,48,48]{4,3,2,1,0:T(8,128)(2,1)} %param.5) | copy-start | bytes 622084
  7.2 7.4 %collective-permute-start.4 = (bf16[8,32,384]{2,1,0:T(8,128)(2,1)S(1)}, bf16[8,32,384]{2,1,0:T(8,128)(2,1)S(1)}, u32[]{:S(2)}, u32[]{:S(2)}) collective-permute-start(bf16[8,32,384]{2,1,0:T(8,128)(2,1)S(1)} %pad_maximum_fusion.own), channel_id=1, source_target_pairs={{1,2},{3,4},{5,6},{7,8},{9,10},{11,12},{13,14},{2,1},{4,3},{6,5},{... | collective-permute-start | bytes 589832 | tf_op jit(solution)/shard_map/ppermute | solution.py:27
  9.1 5.5 %collective-permute-start.3 = (bf16[8,32,384]{2,1,0:T(8,128)(2,1)S(1)}, bf16[8,32,384]{2,1,0:T(8,128)(2,1)S(1)}, u32[]{:S(2)}, u32[]{:S(2)}) collective-permute-start(bf16[8,32,384]{2,1,0:T(8,128)(2,1)S(1)} %pad_maximum_fusion.own), channel_id=1, source_target_pairs={{0,1},{2,3},{4,5},{6,7},{8,9},{10,11},{12,13},{14,15},{1,0},{3,2},... | collective-permute-start | bytes 589832 | tf_op jit(solution)/shard_map/ppermute | solution.py:27
  9.2 4.1 %collective-permute-start.1 = (bf16[1,32,384]{2,1,0:T(8,128)(2,1)S(1)}, bf16[1,32,384]{2,1,0:T(8,128)(2,1)S(1)}, u32[]{:S(2)}, u32[]{:S(2)}) collective-permute-start(bf16[1,32,384]{2,1,0:T(8,128)(2,1)S(1)} %broadcast_select_fusion.1), channel_id=1, source_target_pairs={{0,2},{1,3},{4,6},{5,7},{8,10},{9,11},{12,14},{13,15},{2,0},{3,1},... | collective-permute-start | bytes 73736 | tf_op jit(solution)/shard_map/ppermute | solution.py:27
  10.7 3.8 %collective-permute-start.2 = (bf16[1,32,384]{2,1,0:T(8,128)(2,1)S(1)}, bf16[1,32,384]{2,1,0:T(8,128)(2,1)S(1)}, u32[]{:S(2)}, u32[]{:S(2)}) collective-permute-start(bf16[1,32,384]{2,1,0:T(8,128)(2,1)S(1)} %get-tuple-element.9), channel_id=1, source_target_pairs={{2,4},{3,5},{6,8},{7,9},{10,12},{11,13},{4,2},{5,3},{8,6},{9,7},{1... | collective-permute-start | bytes 73736 | tf_op jit(solution)/shard_map/ppermute | solution.py:27

commit v5 on v4

v5 whole, which is shorter than its diff:
```python
import jax
import jax.numpy as jnp
from jax import lax
from jax.experimental import pallas as pl
from jax.experimental.pallas import tpu as pltpu
from jax.sharding import PartitionSpec as P

LAYERS = 6
RADIUS = 3
HALO = RADIUS + LAYERS
MARGIN = 16
LANES = 128
PAIR = 2
BESIDE = 2


def swapped(x, lows, by):
    size, groups = lax.axis_size("space"), lax.axis_size("tm")
    partner = {i: i + by for i in lows} | {i + by: i for i in lows}
    alone = [i for i in range(size) if i not in partner]
    pairs = [(g * size + i, g * size + j) for g in range(groups) for i, j in partner.items()]
    if groups % 2 == 0:
        pairs += [(g * size + i, (g ^ 1) * size + i) for g in range(groups) for i in alone]
    else:
        pairs += [
            (g * size + i, g * size + j) for g in range(groups) for i, j in zip(alone, reversed(alone))
        ]
    return lax.ppermute(x, ("tm", "space"), pairs)


def rolled(x, by):
    return pltpu.roll(x, by % x.shape[-1], x.ndim - 1)


def pack(place, inten, *outs):
    acqs, cols, rows = inten.shape
    tiles, blocks = len(outs), outs[0].shape[0]
    tile = rows // tiles
    wide = tile // LANES
    sides = blocks - cols * wide
    lane = lax.broadcasted_iota(jnp.int32, (1, LANES), 1)
    slot = lane // MARGIN
    for d, out in enumerate(outs):
        t = place[0] + d
        t = jnp.where(t >= tiles, t - tiles, t)
        start = t * tile
        after = jnp.minimum(start + tile, rows - LANES)
        before = jnp.maximum(start - LANES, 0)
        right = jnp.zeros((acqs, LANES), jnp.float32)
        left = right
        for c in range(cols):
            main = jnp.log(inten[:, c, pl.ds(pl.multiple_of(start, LANES), tile)])
            for k in range(wide):
                out[c * wide + k] = main[:, k * LANES : (k + 1) * LANES].astype(jnp.bfloat16)
            if sides == 1:
                near = pl.multiple_of(jnp.where(t == 0, after, before), LANES)
                edge = jnp.log(inten[:, c, pl.ds(near, LANES)])
                edge = jnp.where(t == 0, rolled(edge, c * MARGIN), rolled(edge, (c + 1) * MARGIN))
                right = jnp.where(slot == c, edge, right)
            else:
                edge = jnp.log(inten[:, c, pl.ds(pl.multiple_of(after, LANES), LANES)])
                right = jnp.where(slot == c, rolled(edge, c * MARGIN), right)
                edge = jnp.log(inten[:, c, pl.ds(pl.multiple_of(before, LANES), LANES)])
                left = jnp.where(slot == c, rolled(edge, (c + 1) * MARGIN), left)
        out[cols * wide] = right.astype(jnp.bfloat16)
        if sides == 2:
            out[cols * wide + 1] = left.astype(jnp.bfloat16)


def body(place, own, mate, next_to, extra, across, w1, wr, out, inten, act_a, act_b):
    acqs = own.shape[1]
    channels, cols, tile = out.shape
    wide = tile // LANES
    sides = own.shape[0] - cols * wide
    width = tile + LANES
    first_col, all_cols = place[0], place[1]
    base, all_rows = place[2], place[3]
    odd = place[4] == 1

    lane = lax.broadcasted_iota(jnp.int32, (1, width), 1)
    row = jnp.where(lane < tile + LANES // 2, lane, lane - width)
    inside = (row >= -MARGIN) & (row < tile + MARGIN)
    row = row + base
    inside = inside & (row >= 0) & (row < all_rows)
    row_mask = inside.astype(jnp.float32)
    early = lax.broadcasted_iota(jnp.int32, (1, LANES), 1) < LANES // 2
    lowest = base == 0

    def column(ref, k, c, count):
        parts = [ref[k * wide + n].astype(jnp.float32) for n in range(wide)]
        right = ref[count * wide].astype(jnp.float32)
        if sides == 1:
            to_left = rolled(right, -(c + 1) * MARGIN)
            right = jnp.where(lowest, rolled(right, -c * MARGIN), to_left)
        else:
            left = rolled(ref[count * wide + 1].astype(jnp.float32), -(c + 1) * MARGIN)
            right = jnp.where(early, rolled(right, -c * MARGIN), left)
        return jnp.concatenate(parts + [right], axis=1)

    more = HALO - cols
    pieces = [(extra, across, odd, more, cols - more), (next_to, mate, odd, cols, 0), (own, own, None, cols, 0)]
    pieces += [(mate, next_to, odd, cols, 0), (across, extra, odd, more, 0)]
    at = 0
    for ref, other, use_other, count, first in pieces:
        for k in range(count):
            ok = inside
            if use_other is None:
                coded = column(ref, k, first + k, count)
            else:
                coded = jnp.where(use_other, column(other, k, first + k, count), column(ref, k, first + k, count))
                g = first_col - HALO + at
                ok = ok & (g >= 0) & (g < all_cols)
            inten[at] = jnp.where(ok, jnp.exp(coded), 0.0)
            at += 1

    row_count = jnp.minimum(row + RADIUS, all_rows - 1) - jnp.maximum(row - RADIUS, 0) + 1
    row_count = jnp.maximum(row_count, 1).astype(jnp.float32)
    feature_cols = cols + 2 * LAYERS

    def despeckle(f, _):
        total = inten[f]
        for k in range(1, 2 * RADIUS + 1):
            total = total + inten[f + k]
        three = rolled(total, 1) + total + rolled(total, -1)
        box = rolled(three, 2) + total + rolled(three, -2)
        g = first_col - LAYERS + f
        col_count = jnp.minimum(g + RADIUS, all_cols - 1) - jnp.maximum(g - RADIUS, 0) + 1
        col_count = jnp.maximum(col_count, 1).astype(jnp.float32)
        local_mean = box * (1.0 / (row_count * col_count))
        ratio = jnp.sum(inten[f + RADIUS] / local_mean, axis=0, keepdims=True)
        feature = jnp.log(local_mean) + jnp.log(ratio / acqs)
        ok = (g >= 0) & (g < all_cols)
        feature = jnp.where(inside & ok, feature, 0.0).astype(jnp.bfloat16)
        to = pl.multiple_of(f * 3 * acqs, 16)
        act_a[pl.ds(to, acqs), :] = rolled(feature, 1)
        act_a[pl.ds(to + acqs, acqs), :] = feature
        act_a[pl.ds(to + 2 * acqs, acqs), :] = rolled(feature, -1)
        return 0

    lax.fori_loop(0, feature_cols, despeckle, 0, unroll=4)

    source, target = act_a, act_b
    depth = acqs
    for layer in range(LAYERS):
        weight = w1[...] if layer == 0 else wr[layer - 1]
        out_cols = feature_cols - 2 * (layer + 1)
        last = layer == LAYERS - 1
        span = tile if last else width
        for start in range(0, out_cols, PAIR * BESIDE):
            firsts = range(start, min(start + PAIR * BESIDE, out_cols), PAIR)
            taps = [source[j * 3 * depth : (j + PAIR + 2) * 3 * depth, :span] for j in firsts]
            summed = jnp.dot(weight, jnp.concatenate(taps, axis=1), preferred_element_type=jnp.float32)
            for n, j in enumerate(firsts):
                for p in range(PAIR):
                    column_sum = summed[p * channels : (p + 1) * channels, n * span : (n + 1) * span]
                    if last:
                        out[:, j + p, :] = column_sum
                        continue
                    g = first_col - (LAYERS - 1 - layer) + j + p
                    ok = ((g >= 0) & (g < all_cols)).astype(jnp.float32)
                    hidden = (jnp.maximum(column_sum, 0.0) * (row_mask * ok)).astype(jnp.bfloat16)
                    to = (j + p) * 3 * channels
                    target[to : to + channels, :] = rolled(hidden, 1)
                    target[to + channels : to + 2 * channels, :] = hidden
                    target[to + 2 * channels : to + 3 * channels, :] = rolled(hidden, -1)
        source, target = target, source
        depth = channels


def shards(intensity, w_first, w_rest):
    acqs_own, cols, rows = intensity.shape
    tm = lax.axis_size("tm")
    space = lax.axis_size("space")
    m = lax.axis_index("tm")
    s = lax.axis_index("space")
    tile = rows // tm
    wide = tile // LANES
    channels, acqs = w_first.shape[2:]
    vmem = pl.BlockSpec(memory_space=pltpu.VMEM)
    smem = pl.BlockSpec(memory_space=pltpu.SMEM)

    blocks = cols * wide + (1 if tm == 2 else 2)
    packed = pl.pallas_call(
        pack,
        out_shape=[jax.ShapeDtypeStruct((blocks, acqs_own, LANES), jnp.bfloat16)] * tm,
        in_specs=[smem, vmem],
        out_specs=[vmem] * tm,
        compiler_params=pltpu.CompilerParams(vmem_limit_bytes=8 * 1024 * 1024),
    )(jnp.reshape(m, (1,)).astype(jnp.int32), intensity)
    parts = [packed[0]]
    for d in range(1, tm):
        parts.append(lax.ppermute(packed[d], "tm", [(i, (i + d) % tm) for i in range(tm)]))
    evens = list(range(0, space, 2))
    odds = [i - 1 for i in evens[1:]]
    beside = [swapped(packed[0], odds, 1)]
    own = jnp.concatenate(parts, axis=1)
    mate = swapped(own, evens, 1)

    far = HALO - cols
    odd = s % 2 == 1
    edges = mate[cols * wide :]
    head = jnp.concatenate([mate[: far * wide], edges], axis=0)
    tail = jnp.concatenate([mate[(cols - far) * wide : cols * wide], edges], axis=0)
    near, across = jnp.where(odd, tail, head), jnp.where(odd, head, tail)
    onward = parts[1:] + [near[:, d * acqs_own : (d + 1) * acqs_own] for d in range(tm)]
    counts = [x.shape[0] for x in onward]
    onward, across = lax.optimization_barrier((jnp.concatenate(onward, axis=0), across))
    onward = swapped(onward, odds, 1)
    across = swapped(across, evens[:-1], 3)
    arrived, start = [], 0
    for count in counts:
        arrived.append(onward[start : start + count])
        start += count
    beside = jnp.concatenate(beside + arrived[: tm - 1], axis=1)
    extra = jnp.concatenate(arrived[tm - 1 :], axis=1)

    def spread(w):
        step = w.shape[-1] // 3
        rest = [(0, 0)] * (w.ndim - 1)
        moved = [jnp.pad(w, rest + [(p * step, (PAIR - 1 - p) * step)]) for p in range(PAIR)]
        return jnp.concatenate(moved, axis=-2)

    order = (m - jnp.arange(tm)) % tm
    w1 = jnp.take(w_first.reshape(3, 3, channels, tm, acqs_own), order, axis=3)
    w1 = spread(w1.reshape(3, 3, channels, acqs).transpose(2, 0, 1, 3).reshape(channels, 9 * acqs))
    wr = spread(w_rest.transpose(0, 3, 1, 2, 4).reshape(LAYERS - 1, channels, 9 * channels))

    place = jnp.stack(
        [s * cols, jnp.int32(cols * space), m * tile, jnp.int32(rows), s % 2]
    ).astype(jnp.int32)
    width = tile + LANES
    act = ((cols + 2 * LAYERS) * 3 * channels, width)
    return pl.pallas_call(
        body,
        out_shape=jax.ShapeDtypeStruct((channels, cols, tile), jnp.float32),
        in_specs=[smem] + [vmem] * 7,
        out_specs=vmem,
        scratch_shapes=[
            pltpu.VMEM((cols + 2 * HALO, acqs, width), jnp.float32),
            pltpu.VMEM(act, jnp.bfloat16),
            pltpu.VMEM(act, jnp.bfloat16),
        ],
        compiler_params=pltpu.CompilerParams(vmem_limit_bytes=20 * 1024 * 1024),
    )(place, own, mate, beside, extra, across, w1, wr)


def solution(mesh):
    in_specs = (P("tm", "space", None), P(), P())
    out_specs = P(None, "space", "tm")
    return jax.shard_map(shards, mesh=mesh, in_specs=in_specs, out_specs=out_specs, check_vma=False)
```

time: 22.8 us -> 21.3 us (0.934)
  the two profiles are of different devices: /device:TPU:0 before, /device:TPU:25 now
where the time goes in v5:
time: 21.3 us; the launch traced here: 21.2 us
  Pallas kernels  7.56 us (35%)
  starting transfers between devices  6.35 us (30%)
  waiting for transfers between devices  4.09 us (19%)
  local copies, waits for them, and re-layouts  2.62 us (12%)
  other arithmetic  0.37 us (2%)
    pallas_call x1, Pallas kernels, shards(): pl.pallas_call(body, out_shape=jax.ShapeDtypeStruct((channels, cols, tile...  6.99 us
    ppermute x4, starting transfers between devices, swapped(): return lax.ppermute(x, ('tm', 'space'), pairs)  5.05 us
    ppermute x4, waiting for transfers between devices, swapped(): return lax.ppermute(x, ('tm', 'space'), pairs)  4.09 us
    ppermute x1, starting transfers between devices, shards(): lax.ppermute(packed[d], 'tm', [(i, (i + d) % tm) for i in range(tm)])  1.3 us
    unnamed x7, local copies, waits for them, and re-layouts  1 us
    gather x2, local copies, waits for them, and re-layouts, shards(): w1 = jnp.take(w_first.reshape(3, 3, channels, tm, acqs_own), order, axis=3)  0.57 us
    pallas_call x1, Pallas kernels, shards(): pl.pallas_call(pack, out_shape=[jax.ShapeDtypeStruct((blocks, acqs_own, L...  0.57 us
  transfers between devices with their start and end apart: 5, of which 2 were waited for; matrix products, arithmetic and copies ran while one was open for 9% of the time, Pallas kernels for 0%

profile of v5, /device:TPU:25, one launch (start us, length us, event | category | flops | bytes accessed | tf_op | source)
XLA Modules:
  0.0 21.2 jit_solution(9751032098695106694)
XLA Ops:
  0.0 0.0 copy-start
  0.0 0.0 copy-start.1
  0.0 1.0 %copy-done.1 = f32[16,8,512]{2,1,0:T(8,128)S(1)} copy-done((f32[16,8,512]{2,1,0:T(8,128)S(1)}, f32[16,8,512]{2,1,0:T(8,128)}, u32[]{:S(2)}) %copy-start.1) | copy-done | bytes 262168
  1.0 0.0 copy-start.2
  1.0 0.6 %shard_map.37 = (bf16[17,16,128]{2,1,0:T(8,128)(2,1)S(1)}, bf16[17,16,128]{2,1,0:T(8,128)(2,1)S(1)}) custom-call(s32[1]{0:T(128)} %bitcast.3.place, f32[16,8,512]{2,1,0:T(8,128)S(1)} %copy-done.1), custom_call_target="tpu_custom_call" | custom-call | tf_op jit(solution)/shard_map/pallas_call | solution.py:183
  1.6 1.3 %collective-permute-start = (bf16[17,16,128]{2,1,0:T(8,128)(2,1)S(1)}, bf16[17,16,128]{2,1,0:T(8,128)(2,1)S(1)}, u32[]{:S(2)}, u32[]{:S(2)}) collective-permute-start(bf16[17,16,128]{2,1,0:T(8,128)(2,1)S(1)} %get-tuple-element.10), channel_id=1, source_target_pairs={{0,16},{16,0},{1,17},{17,1},{2,18},{18,2},{3,19},{19,3},{4,20},{20... | collective-permute-start | bytes 208904 | tf_op jit(solution)/shard_map/ppermute | solution.py:192
  2.9 2.1 %collective-permute-start.2 = (bf16[17,16,128]{2,1,0:T(8,128)(2,1)S(1)}, bf16[17,16,128]{2,1,0:T(8,128)(2,1)S(1)}, u32[]{:S(2)}, u32[]{:S(2)}) collective-permute-start(bf16[17,16,128]{2,1,0:T(8,128)(2,1)S(1)} %get-tuple-element.9), channel_id=1, source_target_pairs={{1,2},{3,4},{5,6},{7,8},{9,10},{11,12},{13,14},{2,1},{4,3},{6,5},{... | collective-permute-start | bytes 208904 | tf_op jit(solution)/shard_map/ppermute | solution.py:28
  4.9 0.1 broadcast_in_dim.14
  5.0 0.1 broadcast_in_dim.15
  5.1 0.0 copy-done
  5.1 0.6 %gather_fusion = bf16[2,3,3,48,16]{3,4,2,1,0:T(8,128)(2,1)S(1)} fusion(bf16[3,3,48,2,16]{2,4,3,1,0:T(8,128)(2,1)S(1)} %bitcast.14, s32[1024]{0:T(1024)S(1)} %pad_clamp_fusion), kind=kCustom, calls=%fused_computation | custom fusion | bytes 55304 | tf_op jit(solution)/shard_map/jit(_take)/gather | solution.py:224
  5.7 0.0 collective-permute-done
  5.7 0.9 %collective-permute-start.1 = (bf16[17,32,128]{2,1,0:T(8,128)(2,1)S(1)}, bf16[17,32,128]{2,1,0:T(8,128)(2,1)S(1)}, u32[]{:S(2)}, u32[]{:S(2)}) collective-permute-start(bf16[17,32,128]{2,1,0:T(8,128)(2,1)S(1)} %constant_dynamic-update-slice_fusion.own), channel_id=1, source_target_pairs={{0,1},{2,3},{4,5},{6,7},{8,9},{10,11},{12,13},{14,15},{1,0},{3,2},... | collective-permute-start | bytes 417800 | tf_op jit(solution)/shard_map/ppermute | solution.py:28
  6.7 0.1 bitcast_select_fusion
  6.8 0.1 copy.10
  6.9 0.0 copy-done.2
  6.9 0.3 %copy.12 = bf16[5,48,3,3,48]{4,3,2,1,0:T(4,128)(2,1)S(1)} copy(bf16[5,48,3,3,48]{4,1,3,2,0:T(8,128)(2,1)S(1)} %bitcast.16) | data formatting | bytes 414720 | tf_op jit(solution)/shard_map/transpose | solution.py:226
  7.2 0.4 %reshape.72 = bf16[5,48,432]{2,1,0:T(8,128)(2,1)S(1)} reshape(bf16[5,48,3,3,48]{4,3,2,1,0:T(4,128)(2,1)S(1)} %copy.12) | data formatting | bytes 414720 | tf_op jit(solution)/shard_map/reshape | solution.py:226
  7.6 0.1 stack.15.place
  7.7 0.1 fusion.2.wr
  7.8 0.0 collective-permute-done.1.mate
  7.9 2.0 %collective-permute-start.3 = (bf16[23,16,128]{2,1,0:T(8,128)(2,1)S(1)}, bf16[23,16,128]{2,1,0:T(8,128)(2,1)S(1)}, u32[]{:S(2)}, u32[]{:S(2)}) collective-permute-start(bf16[23,16,128]{2,1,0:T(8,128)(2,1)S(1)} %pad_maximum_fusion.1), channel_id=1, source_target_pairs={{1,2},{3,4},{5,6},{7,8},{9,10},{11,12},{13,14},{2,1},{4,3},{6,5},{... | collective-permute-start | bytes 282632 | tf_op jit(solution)/shard_map/ppermute | solution.py:28
  9.9 0.1 fusion.5.w1
  10.0 0.0 collective-permute-start.4
  10.0 3.4 %collective-permute-done.3 = bf16[23,16,128]{2,1,0:T(8,128)(2,1)S(1)} collective-permute-done((bf16[23,16,128]{2,1,0:T(8,128)(2,1)S(1)}, bf16[23,16,128]{2,1,0:T(8,128)(2,1)S(1)}, u32[]{:S(2)}, u32[]{:S(2)}) %collective-permute-start.3) | collective-permute-done | bytes 94240 | tf_op jit(solution)/shard_map/ppermute | solution.py:28
  13.4 0.0 collective-permute-done.2
  13.5 0.7 %collective-permute-done.4.across = bf16[3,32,128]{2,1,0:T(8,128)(2,1)S(1)} collective-permute-done((bf16[3,32,128]{2,1,0:T(8,128)(2,1)S(1)}, bf16[3,32,128]{2,1,0:T(8,128)(2,1)S(1)}, u32[]{:S(2)}, u32[]{:S(2)}) %collective-permute-start.4) | collective-permute-done | bytes 24608 | tf_op jit(solution)/shard_map/ppermute | solution.py:28
  14.2 7.0 %shard_map.38 = f32[48,8,256]{2,1,0:T(8,128)} custom-call(s32[5]{0:T(128)S(1)} %stack.15.place, bf16[17,32,128]{2,1,0:T(8,128)(2,1)S(1)} %constant_dynamic-update-slice_fusion.own, bf16[17,32,128]{2,1,0:T(8,128)(2,1)S(1)} %collective-permute-done.1.mate, bf16[17,32,128]{2,1,0:T(8,128)(2,1)S(1)} %pad_maximum_fusion.next_to, ...), custom_call_target="tpu_custom_call" | custom-call | tf_op jit(solution)/shard_map/pallas_call | solution.py:233
  (15 shorter events, 0.1 us)
Async XLA Ops:
  0.0 5.1 %copy-start = (bf16[3,3,48,32]{2,3,1,0:T(8,128)(2,1)S(1)}, bf16[3,3,48,32]{2,3,1,0:T(8,128)(2,1)}, u32[]{:S(2)}) copy-start(bf16[3,3,48,32]{2,3,1,0:T(8,128)(2,1)} %param.4) | copy-start | bytes 82948
  0.0 1.0 %copy-start.1 = (f32[16,8,512]{2,1,0:T(8,128)S(1)}, f32[16,8,512]{2,1,0:T(8,128)}, u32[]{:S(2)}) copy-start(f32[16,8,512]{2,1,0:T(8,128)} %inten.1) | copy-start | bytes 786436
  1.0 5.9 %copy-start.2 = (bf16[5,3,3,48,48]{4,3,2,1,0:T(8,128)(2,1)S(1)}, bf16[5,3,3,48,48]{4,3,2,1,0:T(8,128)(2,1)}, u32[]{:S(2)}) copy-start(bf16[5,3,3,48,48]{4,3,2,1,0:T(8,128)(2,1)} %param.5) | copy-start | bytes 622084
  1.6 4.2 %collective-permute-start = (bf16[17,16,128]{2,1,0:T(8,128)(2,1)S(1)}, bf16[17,16,128]{2,1,0:T(8,128)(2,1)S(1)}, u32[]{:S(2)}, u32[]{:S(2)}) collective-permute-start(bf16[17,16,128]{2,1,0:T(8,128)(2,1)S(1)} %get-tuple-element.10), channel_id=1, source_target_pairs={{0,16},{16,0},{1,17},{17,1},{2,18},{18,2},{3,19},{19,3},{4,20},{20... | collective-permute-start | bytes 208904 | tf_op jit(solution)/shard_map/ppermute | solution.py:192
  2.9 10.6 %collective-permute-start.2 = (bf16[17,16,128]{2,1,0:T(8,128)(2,1)S(1)}, bf16[17,16,128]{2,1,0:T(8,128)(2,1)S(1)}, u32[]{:S(2)}, u32[]{:S(2)}) collective-permute-start(bf16[17,16,128]{2,1,0:T(8,128)(2,1)S(1)} %get-tuple-element.9), channel_id=1, source_target_pairs={{1,2},{3,4},{5,6},{7,8},{9,10},{11,12},{13,14},{2,1},{4,3},{6,5},{... | collective-permute-start | bytes 208904 | tf_op jit(solution)/shard_map/ppermute | solution.py:28
  5.7 2.1 %collective-permute-start.1 = (bf16[17,32,128]{2,1,0:T(8,128)(2,1)S(1)}, bf16[17,32,128]{2,1,0:T(8,128)(2,1)S(1)}, u32[]{:S(2)}, u32[]{:S(2)}) collective-permute-start(bf16[17,32,128]{2,1,0:T(8,128)(2,1)S(1)} %constant_dynamic-update-slice_fusion.own), channel_id=1, source_target_pairs={{0,1},{2,3},{4,5},{6,7},{8,9},{10,11},{12,13},{14,15},{1,0},{3,2},... | collective-permute-start | bytes 417800 | tf_op jit(solution)/shard_map/ppermute | solution.py:28
  7.9 5.5 %collective-permute-start.3 = (bf16[23,16,128]{2,1,0:T(8,128)(2,1)S(1)}, bf16[23,16,128]{2,1,0:T(8,128)(2,1)S(1)}, u32[]{:S(2)}, u32[]{:S(2)}) collective-permute-start(bf16[23,16,128]{2,1,0:T(8,128)(2,1)S(1)} %pad_maximum_fusion.1), channel_id=1, source_target_pairs={{1,2},{3,4},{5,6},{7,8},{9,10},{11,12},{13,14},{2,1},{4,3},{6,5},{... | collective-permute-start | bytes 282632 | tf_op jit(solution)/shard_map/ppermute | solution.py:28
  10.0 4.2 %collective-permute-start.4 = (bf16[3,32,128]{2,1,0:T(8,128)(2,1)S(1)}, bf16[3,32,128]{2,1,0:T(8,128)(2,1)S(1)}, u32[]{:S(2)}, u32[]{:S(2)}) collective-permute-start(bf16[3,32,128]{2,1,0:T(8,128)(2,1)S(1)} %get-tuple-element.12), channel_id=1, source_target_pairs={{0,3},{2,5},{4,7},{6,9},{8,11},{10,13},{12,15},{3,0},{5,2},{7,4},{... | collective-permute-start | bytes 73736 | tf_op jit(solution)/shard_map/ppermute | solution.py:28

commit v6 on v5

v6 whole, which is shorter than its diff:
```python
import jax
import jax.numpy as jnp
from jax import lax
from jax.experimental import pallas as pl
from jax.experimental.pallas import tpu as pltpu
from jax.sharding import PartitionSpec as P

LAYERS = 6
RADIUS = 3
HALO = RADIUS + LAYERS
MARGIN = 16
LANES = 128
PAIR = 2
BESIDE = 2


def swapped(x, lows, by):
    size, groups = lax.axis_size("space"), lax.axis_size("tm")
    partner = {i: i + by for i in lows} | {i + by: i for i in lows}
    alone = [i for i in range(size) if i not in partner]
    pairs = [(g * size + i, g * size + j) for g in range(groups) for i, j in partner.items()]
    if groups % 2 == 0:
        pairs += [(g * size + i, (g ^ 1) * size + i) for g in range(groups) for i in alone]
    else:
        pairs += [
            (g * size + i, g * size + j) for g in range(groups) for i, j in zip(alone, reversed(alone))
        ]
    return lax.ppermute(x, ("tm", "space"), pairs)


def rolled(x, by):
    return pltpu.roll(x, by % x.shape[-1], x.ndim - 1)


def pack(place, inten, *outs):
    acqs, cols, rows = inten.shape
    tiles, blocks = len(outs), outs[0].shape[0]
    tile = rows // tiles
    wide = tile // LANES
    sides = blocks - cols * wide
    lane = lax.broadcasted_iota(jnp.int32, (1, LANES), 1)
    slot = lane // MARGIN
    for d, out in enumerate(outs):
        t = place[0] + d
        t = jnp.where(t >= tiles, t - tiles, t)
        start = t * tile
        after = jnp.minimum(start + tile, rows - LANES)
        before = jnp.maximum(start - LANES, 0)
        right = jnp.zeros((acqs, LANES), jnp.float32)
        left = right
        for c in range(cols):
            main = jnp.log(inten[:, c, pl.ds(pl.multiple_of(start, LANES), tile)])
            for k in range(wide):
                out[c * wide + k] = main[:, k * LANES : (k + 1) * LANES].astype(jnp.bfloat16)
            if sides == 1:
                near = pl.multiple_of(jnp.where(t == 0, after, before), LANES)
                edge = jnp.log(inten[:, c, pl.ds(near, LANES)])
                edge = jnp.where(t == 0, rolled(edge, c * MARGIN), rolled(edge, (c + 1) * MARGIN))
                right = jnp.where(slot == c, edge, right)
            else:
                edge = jnp.log(inten[:, c, pl.ds(pl.multiple_of(after, LANES), LANES)])
                right = jnp.where(slot == c, rolled(edge, c * MARGIN), right)
                edge = jnp.log(inten[:, c, pl.ds(pl.multiple_of(before, LANES), LANES)])
                left = jnp.where(slot == c, rolled(edge, (c + 1) * MARGIN), left)
        out[cols * wide] = right.astype(jnp.bfloat16)
        if sides == 2:
            out[cols * wide + 1] = left.astype(jnp.bfloat16)


class Window:
    def __init__(self, place, cols, tile, acqs):
        self.cols, self.tile, self.acqs = cols, tile, acqs
        self.width = width = tile + LANES
        self.first, self.all_cols = place[0], place[1]
        self.base, self.all_rows = place[2], place[3]
        self.odd = place[4] == 1
        lane = lax.broadcasted_iota(jnp.int32, (1, width), 1)
        row = jnp.where(lane < tile + LANES // 2, lane, lane - width)
        inside = (row >= -MARGIN) & (row < tile + MARGIN)
        self.row = row + self.base
        self.inside = inside & (self.row >= 0) & (self.row < self.all_rows)
        self.row_mask = self.inside.astype(jnp.float32)
        count = jnp.minimum(self.row + RADIUS, self.all_rows - 1) - jnp.maximum(self.row - RADIUS, 0) + 1
        self.row_count = jnp.maximum(count, 1).astype(jnp.float32)

    def place_of(self, u):
        return self.first + jnp.where(self.odd, self.cols + HALO - 1 - u, u - HALO)

    def within(self, u):
        g = self.place_of(u)
        return (g >= 0) & (g < self.all_cols)

    def intensity(self, ref, k, slot, count, known):
        wide = self.tile // LANES
        k = jnp.where(self.odd, count - 1 - k, k)
        slot = jnp.where(self.odd, self.cols - 1 - slot, slot)
        parts = [ref[k * wide + n].astype(jnp.float32) for n in range(wide)]
        to_right = (self.cols - slot) * MARGIN % LANES
        to_left = (self.cols - slot - 1) * MARGIN % LANES
        edge = ref[count * wide].astype(jnp.float32)
        if ref.shape[0] == count * wide + 1:
            edge = pltpu.roll(edge, jnp.where(self.base == 0, to_right, to_left), 1)
        else:
            early = lax.broadcasted_iota(jnp.int32, (1, LANES), 1) < LANES // 2
            before = pltpu.roll(ref[count * wide + 1].astype(jnp.float32), to_left, 1)
            edge = jnp.where(early, pltpu.roll(edge, to_right, 1), before)
        coded = jnp.concatenate(parts + [edge], axis=1)
        ok = self.inside if known is None else self.inside & self.within(known)
        return jnp.where(ok, jnp.exp(coded), 0.0)

    def feature(self, u, inten):
        total = inten(u - RADIUS)
        for k in range(1 - RADIUS, RADIUS + 1):
            total = total + inten(u + k)
        three = rolled(total, 1) + total + rolled(total, -1)
        box = rolled(three, 2) + total + rolled(three, -2)
        g = self.place_of(u)
        count = jnp.minimum(g + RADIUS, self.all_cols - 1) - jnp.maximum(g - RADIUS, 0) + 1
        count = jnp.maximum(count, 1).astype(jnp.float32)
        local_mean = box * (1.0 / (self.row_count * count))
        ratio = jnp.sum(inten(u) / local_mean, axis=0, keepdims=True)
        feature = jnp.log(local_mean) + jnp.log(ratio / self.acqs)
        return jnp.where(self.inside & self.within(u), feature, 0.0).astype(jnp.bfloat16)

    def hidden(self, u, summed):
        ok = self.within(u).astype(jnp.float32)
        return (jnp.maximum(summed, 0.0) * (self.row_mask * ok)).astype(jnp.bfloat16)


def put(ref, k, value):
    depth = value.shape[0]
    to = k * 3 * depth
    ref[to : to + depth, :] = rolled(value, 1)
    ref[to + depth : to + 2 * depth, :] = value
    ref[to + 2 * depth : to + 3 * depth, :] = rolled(value, -1)


def columns(weight, wanted, source, channels, span, done):
    groups, at = [], 0
    while at < len(wanted):
        size = PAIR if wanted[at : at + PAIR] == list(range(wanted[at], wanted[at] + PAIR)) else 1
        groups.append((size, wanted[at]))
        at += size
    for size in (PAIR, 1):
        firsts = [j for n, j in groups if n == size]
        for start in range(0, len(firsts), BESIDE):
            some = firsts[start : start + BESIDE]
            taps = [jnp.concatenate([source(j + k, span) for k in range(size + 2)], axis=0) for j in some]
            used = weight if size == PAIR else weight[:channels, : taps[0].shape[0]]
            summed = jnp.dot(used, jnp.concatenate(taps, axis=1), preferred_element_type=jnp.float32)
            for n, j in enumerate(some):
                for p in range(size):
                    done(j + p, summed[p * channels : (p + 1) * channels, n * span : (n + 1) * span])


def chip_part(place, own, mate, w1, wr, inten, *layers):
    acqs, width = inten.shape[1:]
    cols = inten.shape[0] // 2
    tile = width - LANES
    channels = wr.shape[1] // PAIR
    win = Window(place, cols, tile, acqs)
    for k in range(cols):
        inten[k] = win.intensity(own, k, k, cols, None)
        inten[cols + k] = win.intensity(mate, k, k, cols, None)
    known = 2 * cols
    features = known - 2 * RADIUS
    for k in range(features):
        put(layers[0], k, win.feature(HALO + RADIUS + k, lambda u: inten[u - HALO]))
    for layer in range(len(layers) - 1):
        left = features - 2 * (layer + 1)
        depth = acqs if layer == 0 else channels

        def source(j, span, ref=layers[layer], depth=depth):
            return ref[j * 3 * depth : (j + 1) * 3 * depth, :span]

        def done(j, summed, layer=layer):
            put(layers[layer + 1], j, win.hidden(HALO + RADIUS + layer + 1 + j, summed))

        weight = w1[...] if layer == 0 else wr[layer - 1]
        columns(weight, list(range(left)), source, channels, width, done)


def rest_part(place, next_to, extra, across, w1, wr, chip, *refs):
    acqs, width = chip.shape[1:]
    count = chip_layers(chip.shape[0] // 2)
    given, out, inten, results, mine = refs[:count], refs[count], refs[count + 1], refs[count + 2], refs[count + 3 :]
    channels, cols, tile = out.shape
    win = Window(place, cols, tile, acqs)
    more = HALO - cols
    for k in range(more):
        inten[k] = win.intensity(extra, k, cols - more + k, more, k)
        inten[HALO + k] = win.intensity(across, k, k, more, HALO + 2 * cols + k)
    for k in range(cols):
        inten[more + k] = win.intensity(next_to, k, k, cols, more + k)

    def intensity(u):
        if HALO <= u < HALO + 2 * cols:
            return chip[u - HALO]
        return inten[u if u < HALO else u - 2 * cols]

    first = HALO
    for layer in range(LAYERS + 1):
        total = cols + 2 * (LAYERS - layer)
        have = max(2 * cols - 2 * RADIUS - 2 * layer, 0) if layer < count else 0
        wanted = [j for j in range(total) if not first <= j < first + have]
        if layer == 0:
            for k, f in enumerate(wanted):
                put(mine[0], k, win.feature(RADIUS + f, intensity))
        else:
            weight = w1[...] if layer == 1 else wr[layer - 2]

            def done(j, summed, layer=layer, wanted=wanted):
                if layer < LAYERS:
                    put(mine[layer], wanted.index(j), win.hidden(RADIUS + layer + j, summed))
                else:
                    results[jnp.where(win.odd, cols - 1 - j, j)] = summed

            columns(weight, wanted, source, channels, tile if layer == LAYERS else width, done)
        depth = acqs if layer == 0 else channels

        def source(j, span, layer=layer, depth=depth, wanted=wanted):
            if j in wanted:
                ref, k = mine[layer], wanted.index(j)
            else:
                ref, k = given[layer], j - first
            return ref[k * 3 * depth : (k + 1) * 3 * depth, :span]

    for j in range(cols):
        out[:, j, :] = results[j]


def chip_layers(cols):
    return min(LAYERS, cols - RADIUS)


def shards(intensity, w_first, w_rest):
    acqs_own, cols, rows = intensity.shape
    tm = lax.axis_size("tm")
    space = lax.axis_size("space")
    m = lax.axis_index("tm")
    s = lax.axis_index("space")
    tile = rows // tm
    wide = tile // LANES
    channels, acqs = w_first.shape[2:]
    vmem = pl.BlockSpec(memory_space=pltpu.VMEM)
    smem = pl.BlockSpec(memory_space=pltpu.SMEM)

    blocks = cols * wide + (1 if tm == 2 else 2)
    packed = pl.pallas_call(
        pack,
        out_shape=[jax.ShapeDtypeStruct((blocks, acqs_own, LANES), jnp.bfloat16)] * tm,
        in_specs=[smem, vmem],
        out_specs=[vmem] * tm,
        compiler_params=pltpu.CompilerParams(vmem_limit_bytes=8 * 1024 * 1024),
    )(jnp.reshape(m, (1,)).astype(jnp.int32), intensity)
    parts = [packed[0]]
    for d in range(1, tm):
        parts.append(lax.ppermute(packed[d], "tm", [(i, (i + d) % tm) for i in range(tm)]))
    evens = list(range(0, space, 2))
    odds = [i - 1 for i in evens[1:]]
    beside = [swapped(packed[0], odds, 1)]
    own = jnp.concatenate(parts, axis=1)
    mate = swapped(own, evens, 1)

    far = HALO - cols
    odd = s % 2 == 1

    def ends(x):
        edges = x[cols * wide :]
        head = jnp.concatenate([x[: far * wide], edges], axis=0)
        tail = jnp.concatenate([x[(cols - far) * wide : cols * wide], edges], axis=0)
        return head, tail

    head, tail = ends(own)
    ring = [(i, i - 2 if i else 1) for i in evens] + [(i + 1, i + 3 if i + 3 < space else i) for i in evens]
    across = lax.ppermute(jnp.where(odd, tail, head), "space", ring)
    head, tail = ends(mate)
    near = jnp.where(odd, tail, head)
    onward = parts[1:] + [near[:, d * acqs_own : (d + 1) * acqs_own] for d in range(tm)]
    counts = [x.shape[0] for x in onward]
    onward = swapped(jnp.concatenate(onward, axis=0), odds, 1)
    arrived, start = [], 0
    for count in counts:
        arrived.append(onward[start : start + count])
        start += count
    beside = jnp.concatenate(beside + arrived[: tm - 1], axis=1)
    extra = jnp.concatenate(arrived[tm - 1 :], axis=1)

    def spread(w):
        step = w.shape[-1] // 3
        rest = [(0, 0)] * (w.ndim - 1)
        moved = [jnp.pad(w, rest + [(p * step, (PAIR - 1 - p) * step)]) for p in range(PAIR)]
        return jnp.concatenate(moved, axis=-2)

    w_first = jnp.where(odd, w_first[::-1], w_first)
    w_rest = jnp.where(odd, w_rest[:, ::-1], w_rest)
    order = (m - jnp.arange(tm)) % tm
    w1 = jnp.take(w_first.reshape(3, 3, channels, tm, acqs_own), order, axis=3)
    w1 = spread(w1.reshape(3, 3, channels, acqs).transpose(2, 0, 1, 3).reshape(channels, 9 * acqs))
    wr = spread(w_rest.transpose(0, 3, 1, 2, 4).reshape(LAYERS - 1, channels, 9 * channels))

    place = jnp.stack(
        [s * cols, jnp.int32(cols * space), m * tile, jnp.int32(rows), s % 2]
    ).astype(jnp.int32)
    width = tile + LANES
    limit = pltpu.CompilerParams(vmem_limit_bytes=20 * 1024 * 1024)
    inputs = chip_layers(cols)
    depths = [acqs] + [channels] * (LAYERS - 1)
    reach = [2 * cols - 2 * RADIUS - 2 * n for n in range(inputs)]
    chip, *given = pl.pallas_call(
        chip_part,
        out_shape=[jax.ShapeDtypeStruct((2 * cols, acqs, width), jnp.float32)]
        + [jax.ShapeDtypeStruct((reach[n] * 3 * depths[n], width), jnp.bfloat16) for n in range(inputs)],
        in_specs=[smem] + [vmem] * 4,
        out_specs=[vmem] * (1 + inputs),
        compiler_params=limit,
        cost_estimate=pl.CostEstimate(flops=10**9, bytes_accessed=4 * 10**6, transcendentals=10**6),
    )(place, own, mate, w1, wr)
    lacking = [cols + 2 * (LAYERS - n) - (reach[n] if n < inputs else 0) for n in range(LAYERS)]
    return pl.pallas_call(
        rest_part,
        out_shape=jax.ShapeDtypeStruct((channels, cols, tile), jnp.float32),
        in_specs=[smem] + [vmem] * (6 + inputs),
        out_specs=vmem,
        scratch_shapes=[
            pltpu.VMEM((2 * HALO - cols, acqs, width), jnp.float32),
            pltpu.VMEM((cols, channels, tile), jnp.float32),
        ]
        + [pltpu.VMEM((lacking[n] * 3 * depths[n], width), jnp.bfloat16) for n in range(LAYERS)],
        compiler_params=limit,
        cost_estimate=pl.CostEstimate(flops=2 * 10**9, bytes_accessed=4 * 10**6, transcendentals=10**6),
    )(place, beside, extra, across, w1, wr, chip, *given)


def solution(mesh):
    in_specs = (P("tm", "space", None), P(), P())
    out_specs = P(None, "space", "tm")
    return jax.shard_map(shards, mesh=mesh, in_specs=in_specs, out_specs=out_specs, check_vma=False)
```

time: 21.3 us -> 19.5 us (0.915)
  the two profiles are of different devices: /device:TPU:25 before, /device:TPU:1 now
where the time goes in v6:
time: 19.5 us; the launch traced here: 19.4 us
  Pallas kernels  7.89 us (40%)
  starting transfers between devices  6.89 us (35%)
  local copies, waits for them, and re-layouts  2.59 us (13%)
  other arithmetic  1.45 us (7%)
  waiting for transfers between devices  0.34 us (2%)
  between operations  0.2 us (1%)
    pallas_call x1, Pallas kernels, shards(): pl.pallas_call(rest_part, out_shape=jax.ShapeDtypeStruct((channels, cols,...  4.62 us
    ppermute x3, starting transfers between devices, swapped(): return lax.ppermute(x, ('tm', 'space'), pairs)  3.54 us
    pallas_call x1, Pallas kernels, shards(): pl.pallas_call(chip_part, out_shape=[jax.ShapeDtypeStruct((2 * cols, acqs...  2.7 us
    ppermute x1, starting transfers between devices, shards(): lax.ppermute(packed[d], 'tm', [(i, (i + d) % tm) for i in range(tm)])  2.13 us
    ppermute x1, starting transfers between devices, shards(): across = lax.ppermute(jnp.where(odd, tail, head), 'space', ring)  1.21 us
    select_n x1, other arithmetic, shards(): w_first = jnp.where(odd, w_first[::-1], w_first)  0.98 us
    unnamed x5, local copies, waits for them, and re-layouts  0.96 us
    gather x2, local copies, waits for them, and re-layouts, shards(): w1 = jnp.take(w_first.reshape(3, 3, channels, tm, acqs_own), order, axis=3)  0.57 us
  transfers between devices with their start and end apart: 5, of which 1 were waited for; matrix products, arithmetic and copies ran while one was open for 16% of the time, Pallas kernels for 14%

profile of v6, /device:TPU:1, one launch (start us, length us, event | category | flops | bytes accessed | tf_op | source)
XLA Modules:
  0.0 19.4 jit_solution(116817547803759850)
XLA Ops:
  0.0 0.0 copy-start
  0.0 0.9 %copy-done = f32[16,8,512]{2,1,0:T(8,128)S(1)} copy-done((f32[16,8,512]{2,1,0:T(8,128)S(1)}, f32[16,8,512]{2,1,0:T(8,128)}, u32[]{:S(2)}) %copy-start) | copy-done | bytes 262168
  1.0 0.0 copy-start.1
  1.0 0.6 %shard_map.37 = (bf16[17,16,128]{2,1,0:T(8,128)(2,1)S(1)}, bf16[17,16,128]{2,1,0:T(8,128)(2,1)S(1)}) custom-call(s32[1]{0:T(128)} %bitcast.3.place, f32[16,8,512]{2,1,0:T(8,128)S(1)} %copy-done), custom_call_target="tpu_custom_call" | custom-call | tf_op jit(solution)/shard_map/pallas_call | solution.py:249
  1.5 2.1 %collective-permute-start.1 = (bf16[17,16,128]{2,1,0:T(8,128)(2,1)S(1)}, bf16[17,16,128]{2,1,0:T(8,128)(2,1)S(1)}, u32[]{:S(2)}, u32[]{:S(2)}) collective-permute-start(bf16[17,16,128]{2,1,0:T(8,128)(2,1)S(1)} %get-tuple-element.14), channel_id=1, source_target_pairs={{0,16},{16,0},{1,17},{17,1},{2,18},{18,2},{3,19},{19,3},{4,20},{20... | collective-permute-start | bytes 208904 | tf_op jit(solution)/shard_map/ppermute | solution.py:258
  3.7 2.1 %collective-permute-start = (bf16[17,16,128]{2,1,0:T(8,128)(2,1)S(1)}, bf16[17,16,128]{2,1,0:T(8,128)(2,1)S(1)}, u32[]{:S(2)}, u32[]{:S(2)}) collective-permute-start(bf16[17,16,128]{2,1,0:T(8,128)(2,1)S(1)} %get-tuple-element.13), channel_id=1, source_target_pairs={{1,2},{3,4},{5,6},{7,8},{9,10},{11,12},{13,14},{2,1},{4,3},{6,5},{... | collective-permute-start | bytes 208904 | tf_op jit(solution)/shard_map/ppermute | solution.py:28
  5.8 0.1 broadcast_in_dim.14
  5.8 0.1 broadcast_in_dim.15
  5.9 1.0 %reverse_select_fusion.1 = bf16[3,3,48,32]{2,3,1,0:T(8,128)(2,1)S(1)} fusion(bf16[3,3,48,32]{2,3,1,0:T(8,128)(2,1)} %param.4, pred[]{:T(512)S(6)} %eq.8), kind=kLoop, calls=%fused_computation.13 | loop fusion | flops 13824 | bytes 55297 | tf_op jit(solution)/shard_map/jit(_where)/select_n | solution.py:295
  6.9 0.6 %gather_fusion = bf16[2,3,3,48,16]{3,4,2,1,0:T(8,128)(2,1)S(1)} fusion(bf16[3,3,48,2,16]{2,4,3,1,0:T(8,128)(2,1)S(1)} %bitcast.16, s32[1024]{0:T(1024)S(1)} %pad_clamp_fusion), kind=kCustom, calls=%fused_computation | custom fusion | bytes 55304 | tf_op jit(solution)/shard_map/jit(_take)/gather | solution.py:298
  7.5 0.1 bitcast_select_fusion
  7.6 0.1 copy.10
  7.7 0.0 copy-done.1
  7.7 0.1 fusion.3
  7.8 0.0 collective-permute-done.1
  7.8 0.1 collective-permute-start.2
  7.9 0.1 fusion.6.w1
  8.0 0.3 %copy.12 = bf16[5,48,3,3,48]{4,3,2,1,0:T(4,128)(2,1)S(1)} copy(bf16[5,48,3,3,48]{4,1,3,2,0:T(8,128)(2,1)S(1)} %fusion.3) | data formatting | bytes 414720 | tf_op jit(solution)/shard_map/transpose | solution.py:300
  8.3 0.4 %reshape.72 = bf16[5,48,432]{2,1,0:T(8,128)(2,1)S(1)} reshape(bf16[5,48,3,3,48]{4,3,2,1,0:T(4,128)(2,1)S(1)} %copy.12) | data formatting | bytes 414720 | tf_op jit(solution)/shard_map/reshape | solution.py:300
  8.7 0.1 stack.15.place
  8.8 0.1 fusion.2.wr
  8.9 0.3 %collective-permute-done.2.mate = bf16[17,32,128]{2,1,0:T(8,128)(2,1)S(1)} collective-permute-done((bf16[17,32,128]{2,1,0:T(8,128)(2,1)S(1)}, bf16[17,32,128]{2,1,0:T(8,128)(2,1)S(1)}, u32[]{:S(2)}, u32[]{:S(2)}) %collective-permute-start.2) | collective-permute-done | bytes 139296 | tf_op jit(solution)/shard_map/ppermute | solution.py:28
  9.3 1.4 %collective-permute-start.3 = (bf16[23,16,128]{2,1,0:T(8,128)(2,1)S(1)}, bf16[23,16,128]{2,1,0:T(8,128)(2,1)S(1)}, u32[]{:S(2)}, u32[]{:S(2)}) collective-permute-start(bf16[23,16,128]{2,1,0:T(8,128)(2,1)S(1)} %pad_maximum_fusion.1), channel_id=1, source_target_pairs={{1,2},{3,4},{5,6},{7,8},{9,10},{11,12},{13,14},{2,1},{4,3},{6,5},{... | collective-permute-start | bytes 282632 | tf_op jit(solution)/shard_map/ppermute | solution.py:28
  10.7 1.2 %collective-permute-start.4 = (bf16[3,32,128]{2,1,0:T(8,128)(2,1)S(1)}, bf16[3,32,128]{2,1,0:T(8,128)(2,1)S(1)}, u32[]{:S(2)}, u32[]{:S(2)}) collective-permute-start(bf16[3,32,128]{2,1,0:T(8,128)(2,1)S(1)} %slice_select_fusion), channel_id=1, source_target_pairs={{0,1},{2,0},{4,2},{6,4},{8,6},{10,8},{12,10},{14,12},{1,3},{3,5},{... | collective-permute-start | bytes 73736 | tf_op jit(solution)/shard_map/ppermute | solution.py:276
  11.9 2.7 %shard_map.38 = (f32[16,32,384]{2,1,0:T(8,128)S(1)}, bf16[960,384]{1,0:T(8,128)(2,1)S(1)}, bf16[1152,384]{1,0:T(8,128)(2,1)S(1)}, bf16[864,384]{1,0:T(8,128)(2,1...) custom-call(s32[5]{0:T(128)S(1)} %stack.15.place, ...), custom_call_target="tpu_custom_call" | custom-call | flops 1000000000 | bytes 4000000 | tf_op jit(solution)/shard_map/pallas_call | solution.py:310
  14.6 0.0 collective-permute-done.3
  14.7 0.0 collective-permute-done
  14.7 0.0 collective-permute-done.4.across
  14.7 4.6 %shard_map.39 = f32[48,8,256]{2,1,0:T(8,128)} custom-call(s32[5]{0:T(128)S(1)} %stack.15.place, bf16[17,32,128]{2,1,0:T(8,128)(2,1)S(1)} %pad_maximum_fusion.next_to, bf16[3,32,128]{2,1,0:T(8,128)(2,1)S(1)} %pad_maximum_fusion.2.extra, bf16[3,32,128]{2,1,0:T(8,128)(2,1)S(1)} %collective-permute-done.4.across, bf16[96,384]{1,0:T(8,128)(2,1)S(1)} %fusion.6.w1, ...), custom_call_target="tpu_custom_call" | custom-call | flops 2000000000 | bytes 4000000 | tf_op jit(solution)/shard_map/pallas_call | solution.py:320
  (18 shorter events, 0.1 us)
Async XLA Ops:
  0.0 0.9 %copy-start = (f32[16,8,512]{2,1,0:T(8,128)S(1)}, f32[16,8,512]{2,1,0:T(8,128)}, u32[]{:S(2)}) copy-start(f32[16,8,512]{2,1,0:T(8,128)} %inten.1) | copy-start | bytes 786436
  1.0 6.7 %copy-start.1 = (bf16[5,3,3,48,48]{4,3,2,1,0:T(8,128)(2,1)S(1)}, bf16[5,3,3,48,48]{4,3,2,1,0:T(8,128)(2,1)}, u32[]{:S(2)}) copy-start(bf16[5,3,3,48,48]{4,3,2,1,0:T(8,128)(2,1)} %param.5) | copy-start | bytes 622084
  1.5 6.3 %collective-permute-start.1 = (bf16[17,16,128]{2,1,0:T(8,128)(2,1)S(1)}, bf16[17,16,128]{2,1,0:T(8,128)(2,1)S(1)}, u32[]{:S(2)}, u32[]{:S(2)}) collective-permute-start(bf16[17,16,128]{2,1,0:T(8,128)(2,1)S(1)} %get-tuple-element.14), channel_id=1, source_target_pairs={{0,16},{16,0},{1,17},{17,1},{2,18},{18,2},{3,19},{19,3},{4,20},{20... | collective-permute-start | bytes 208904 | tf_op jit(solution)/shard_map/ppermute | solution.py:258
  3.7 11.0 %collective-permute-start = (bf16[17,16,128]{2,1,0:T(8,128)(2,1)S(1)}, bf16[17,16,128]{2,1,0:T(8,128)(2,1)S(1)}, u32[]{:S(2)}, u32[]{:S(2)}) collective-permute-start(bf16[17,16,128]{2,1,0:T(8,128)(2,1)S(1)} %get-tuple-element.13), channel_id=1, source_target_pairs={{1,2},{3,4},{5,6},{7,8},{9,10},{11,12},{13,14},{2,1},{4,3},{6,5},{... | collective-permute-start | bytes 208904 | tf_op jit(solution)/shard_map/ppermute | solution.py:28
  7.8 1.4 %collective-permute-start.2 = (bf16[17,32,128]{2,1,0:T(8,128)(2,1)S(1)}, bf16[17,32,128]{2,1,0:T(8,128)(2,1)S(1)}, u32[]{:S(2)}, u32[]{:S(2)}) collective-permute-start(bf16[17,32,128]{2,1,0:T(8,128)(2,1)S(1)} %constant_dynamic-update-slice_fusion.own), channel_id=1, source_target_pairs={{0,1},{2,3},{4,5},{6,7},{8,9},{10,11},{12,13},{14,15},{1,0},{3,2},... | collective-permute-start | bytes 417800 | tf_op jit(solution)/shard_map/ppermute | solution.py:28
  9.3 5.3 %collective-permute-start.3 = (bf16[23,16,128]{2,1,0:T(8,128)(2,1)S(1)}, bf16[23,16,128]{2,1,0:T(8,128)(2,1)S(1)}, u32[]{:S(2)}, u32[]{:S(2)}) collective-permute-start(bf16[23,16,128]{2,1,0:T(8,128)(2,1)S(1)} %pad_maximum_fusion.1), channel_id=1, source_target_pairs={{1,2},{3,4},{5,6},{7,8},{9,10},{11,12},{13,14},{2,1},{4,3},{6,5},{... | collective-permute-start | bytes 282632 | tf_op jit(solution)/shard_map/ppermute | solution.py:28
  10.7 4.0 %collective-permute-start.4 = (bf16[3,32,128]{2,1,0:T(8,128)(2,1)S(1)}, bf16[3,32,128]{2,1,0:T(8,128)(2,1)S(1)}, u32[]{:S(2)}, u32[]{:S(2)}) collective-permute-start(bf16[3,32,128]{2,1,0:T(8,128)(2,1)S(1)} %slice_select_fusion), channel_id=1, source_target_pairs={{0,1},{2,0},{4,2},{6,4},{8,6},{10,8},{12,10},{14,12},{1,3},{3,5},{... | collective-permute-start | bytes 73736 | tf_op jit(solution)/shard_map/ppermute | solution.py:276

commit v7 on v6

--- a/solution.py
+++ b/solution.py
@@ -1,3 +1,5 @@
+import functools
+
 import jax
 import jax.numpy as jnp
 from jax import lax
@@ -67,6 +69,31 @@
             out[cols * wide + 1] = left.astype(jnp.bfloat16)
 
 
+def spread(swap, place, w_first, w_rest, first, rest):
+    channels, depth = w_first.shape[2:]
+
+    def laid(pieces):
+        step = 3 * pieces[0].shape[1]
+        rows = []
+        for p in range(PAIR):
+            before = [jnp.zeros((channels, p * step), jnp.float32)] if p else []
+            after = [jnp.zeros((channels, (PAIR - 1 - p) * step), jnp.float32)] if p < PAIR - 1 else []
+            rows.append(jnp.concatenate(before + pieces + after, axis=1))
+        return jnp.concatenate(rows, axis=0).astype(jnp.bfloat16)
+
+    odd = place[4] == 1
+    taps = [(a, b) for a in range(3) for b in range(3)]
+    late = [(jnp.where(odd, 2 - a, a), b) for a, b in taps]
+    pieces = [w_first[a, b].astype(jnp.float32) for a, b in taps]
+    if swap:
+        half = depth // 2
+        moved = [jnp.concatenate([x[:, half:], x[:, :half]], axis=1) for x in pieces]
+        pieces = [jnp.where(place[2] == 0, x, y) for x, y in zip(pieces, moved)]
+    first[...] = laid(pieces)
+    for layer in range(LAYERS - 1):
+        rest[layer] = laid([w_rest[layer, a, b].astype(jnp.float32) for a, b in late])
+
+
 class Window:
     def __init__(self, place, cols, tile, acqs):
         self.cols, self.tile, self.acqs = cols, tile, acqs
@@ -260,6 +287,9 @@
     odds = [i - 1 for i in evens[1:]]
     beside = [swapped(packed[0], odds, 1)]
     own = jnp.concatenate(parts, axis=1)
+    odd = s % 2 == 1
+    w_first = jnp.where(odd, w_first[::-1], w_first)
+    own, w_first = lax.optimization_barrier((own, w_first))
     mate = swapped(own, evens, 1)
 
     far = HALO - cols
@@ -286,22 +316,24 @@
     beside = jnp.concatenate(beside + arrived[: tm - 1], axis=1)
     extra = jnp.concatenate(arrived[tm - 1 :], axis=1)
 
-    def spread(w):
-        step = w.shape[-1] // 3
-        rest = [(0, 0)] * (w.ndim - 1)
-        moved = [jnp.pad(w, rest + [(p * step, (PAIR - 1 - p) * step)]) for p in range(PAIR)]
-        return jnp.concatenate(moved, axis=-2)
-
-    w_first = jnp.where(odd, w_first[::-1], w_first)
-    w_rest = jnp.where(odd, w_rest[:, ::-1], w_rest)
-    order = (m - jnp.arange(tm)) % tm
-    w1 = jnp.take(w_first.reshape(3, 3, channels, tm, acqs_own), order, axis=3)
-    w1 = spread(w1.reshape(3, 3, channels, acqs).transpose(2, 0, 1, 3).reshape(channels, 9 * acqs))
-    wr = spread(w_rest.transpose(0, 3, 1, 2, 4).reshape(LAYERS - 1, channels, 9 * channels))
-
     place = jnp.stack(
         [s * cols, jnp.int32(cols * space), m * tile, jnp.int32(rows), s % 2]
     ).astype(jnp.int32)
+    if tm != 2:
+        order = (m - jnp.arange(tm)) % tm
+        w_first = jnp.take(w_first.reshape(3, 3, channels, tm, acqs_own), order, axis=3)
+        w_first = w_first.reshape(3, 3, channels, acqs)
+    w1, wr = pl.pallas_call(
+        functools.partial(spread, tm == 2),
+        out_shape=[
+            jax.ShapeDtypeStruct((PAIR * channels, 3 * (PAIR + 2) * acqs), jnp.bfloat16),
+            jax.ShapeDtypeStruct((LAYERS - 1, PAIR * channels, 3 * (PAIR + 2) * channels), jnp.bfloat16),
+        ],
+        in_specs=[smem, vmem, vmem],
+        out_specs=[vmem, vmem],
+        compiler_params=pltpu.CompilerParams(vmem_limit_bytes=8 * 1024 * 1024),
+        cost_estimate=pl.CostEstimate(flops=10**8, bytes_accessed=10**6, transcendentals=0),
+    )(place, w_first, w_rest)
     width = tile + LANES
     limit = pltpu.CompilerParams(vmem_limit_bytes=20 * 1024 * 1024)
     inputs = chip_layers(cols)

time: 19.5 us -> 19 us (0.974)
  the two profiles are of different devices: /device:TPU:1 before, /device:TPU:0 now
where the time goes in v7:
time: 19 us; the launch traced here: 18.9 us
  Pallas kernels  8.87 us (47%)
  starting transfers between devices  5.75 us (30%)
  waiting for transfers between devices  2.8 us (15%)
  local copies, waits for them, and re-layouts  1.19 us (6%)
    pallas_call x1, Pallas kernels, shards(): pl.pallas_call(rest_part, out_shape=jax.ShapeDtypeStruct((channels, cols,...  4.6 us
    ppermute x1, starting transfers between devices, shards(): lax.ppermute(packed[d], 'tm', [(i, (i + d) % tm) for i in range(tm)])  3.03 us
    pallas_call x1, Pallas kernels, shards(): pl.pallas_call(chip_part, out_shape=[jax.ShapeDtypeStruct((2 * cols, acqs...  2.71 us
    ppermute x3, starting transfers between devices, swapped(): return lax.ppermute(x, ('tm', 'space'), pairs)  2.23 us
    ppermute x1, waiting for transfers between devices, shards(): lax.ppermute(packed[d], 'tm', [(i, (i + d) % tm) for i in range(tm)])  1.95 us
    unnamed x7, local copies, waits for them, and re-layouts  1.08 us
    pallas_call x1, Pallas kernels, shards(): pl.pallas_call(functools.partial(spread, tm == 2), out_shape=[jax.ShapeDt...  0.99 us
    ppermute x3, waiting for transfers between devices, swapped(): return lax.ppermute(x, ('tm', 'space'), pairs)  0.85 us
  transfers between devices with their start and end apart: 5, of which 2 were waited for; matrix products, arithmetic and copies ran while one was open for 2% of the time, Pallas kernels for 20%

profile of v7, /device:TPU:0, one launch (start us, length us, event | category | flops | bytes accessed | tf_op | source)
XLA Modules:
  0.0 18.9 jit_solution(15759234842288472318)
XLA Ops:
  0.0 0.0 copy-start.1
  0.0 0.9 %copy-done.1 = f32[16,8,512]{2,1,0:T(8,128)S(1)} copy-done((f32[16,8,512]{2,1,0:T(8,128)S(1)}, f32[16,8,512]{2,1,0:T(8,128)}, u32[]{:S(2)}) %copy-start.1) | copy-done | bytes 262168
  1.0 0.0 copy-start.2
  1.0 0.6 %shard_map.37 = (bf16[17,16,128]{2,1,0:T(8,128)(2,1)S(1)}, bf16[17,16,128]{2,1,0:T(8,128)(2,1)S(1)}) custom-call(s32[1]{0:T(128)} %bitcast.3.place, f32[16,8,512]{2,1,0:T(8,128)S(1)} %copy-done.1), custom_call_target="tpu_custom_call" | custom-call | tf_op jit(solution)/shard_map/pallas_call | solution.py:276
  1.5 3.0 %collective-permute-start.1 = (bf16[17,16,128]{2,1,0:T(8,128)(2,1)S(1)}, bf16[17,16,128]{2,1,0:T(8,128)(2,1)S(1)}, u32[]{:S(2)}, u32[]{:S(2)}) collective-permute-start(bf16[17,16,128]{2,1,0:T(8,128)(2,1)S(1)} %get-tuple-element.18), channel_id=1, source_target_pairs={{0,16},{16,0},{1,17},{17,1},{2,18},{18,2},{3,19},{19,3},{4,20},{20... | collective-permute-start | bytes 208904 | tf_op jit(solution)/shard_map/ppermute | solution.py:285
  4.6 0.1 collective-permute-start
  4.6 0.0 copy-done.2
  4.6 0.0 copy-start
  4.6 0.1 copy.4
  4.8 0.1 stack.15.place
  4.9 2.0 %collective-permute-done.1 = bf16[17,16,128]{2,1,0:T(8,128)(2,1)S(1)} collective-permute-done((bf16[17,16,128]{2,1,0:T(8,128)(2,1)S(1)}, bf16[17,16,128]{2,1,0:T(8,128)(2,1)S(1)}, u32[]{:S(2)}, u32[]{:S(2)}) %collective-permute-start.1) | collective-permute-done | bytes 69664 | tf_op jit(solution)/shard_map/ppermute | solution.py:285
  6.9 0.1 collective-permute-start.2
  7.0 0.5 %collective-permute-start.4 = (bf16[3,32,128]{2,1,0:T(8,128)(2,1)S(1)}, bf16[3,32,128]{2,1,0:T(8,128)(2,1)S(1)}, u32[]{:S(2)}, u32[]{:S(2)}) collective-permute-start(bf16[3,32,128]{2,1,0:T(8,128)(2,1)S(1)} %maximum_select_fusion), channel_id=1, source_target_pairs={{0,1},{2,0},{4,2},{6,4},{8,6},{10,8},{12,10},{14,12},{1,3},{3,5},{... | collective-permute-start | bytes 73736 | tf_op jit(solution)/shard_map/ppermute | solution.py:306
  7.5 0.8 %collective-permute-done.2.mate = bf16[17,32,128]{2,1,0:T(8,128)(2,1)S(1)} collective-permute-done((bf16[17,32,128]{2,1,0:T(8,128)(2,1)S(1)}, bf16[17,32,128]{2,1,0:T(8,128)(2,1)S(1)}, u32[]{:S(2)}, u32[]{:S(2)}) %collective-permute-start.2) | collective-permute-done | bytes 139296 | tf_op jit(solution)/shard_map/ppermute | solution.py:30
  8.4 2.1 %collective-permute-start.3 = (bf16[23,16,128]{2,1,0:T(8,128)(2,1)S(1)}, bf16[23,16,128]{2,1,0:T(8,128)(2,1)S(1)}, u32[]{:S(2)}, u32[]{:S(2)}) collective-permute-start(bf16[23,16,128]{2,1,0:T(8,128)(2,1)S(1)} %pad_maximum_fusion.2), channel_id=1, source_target_pairs={{1,2},{3,4},{5,6},{7,8},{9,10},{11,12},{13,14},{2,1},{4,3},{6,5},{... | collective-permute-start | bytes 282632 | tf_op jit(solution)/shard_map/ppermute | solution.py:30
  10.4 0.0 copy-done
  10.4 1.0 %shard_map.38 = (bf16[96,384]{1,0:T(8,128)(2,1)S(1)}, bf16[5,96,576]{2,1,0:T(8,128)(2,1)S(1)}) custom-call(s32[5]{0:T(128)S(1)} %stack.15.place, bf16[3,3,48,32]{3,2,1,0:T(8,128)(2,1)S(1)} %reverse_select_fusion.w_first, bf16[5,3,3,48,48]{4,3,2,1,0:T(8,128)(2,1)S(1)} %copy-done), custom_call_target="tpu_custom_call" | custom-call | flops 100000000 | bytes 1000000 | tf_op jit(solution)/shard_map/pallas_call | solution.py:326
  11.4 2.7 %shard_map.39 = (f32[16,32,384]{2,1,0:T(8,128)S(1)}, bf16[960,384]{1,0:T(8,128)(2,1)S(1)}, bf16[1152,384]{1,0:T(8,128)(2,1)S(1)}, bf16[864,384]{1,0:T(8,128)(2,1...) custom-call(s32[5]{0:T(128)S(1)} %stack.15.place, bf16[17,32,128]{2,1,0:T(8,128)(2,1)S(1)} %pad_maximum_fusion.own, ...), custom_call_target="tpu_custom_call" | custom-call | flops 1000000000 | bytes 4000000 | tf_op jit(solution)/shard_map/pallas_call | solution.py:342
  14.2 0.0 collective-permute-done.3
  14.2 0.0 collective-permute-done
  14.2 0.0 collective-permute-done.4.across
  14.2 4.6 %shard_map.40 = f32[48,8,256]{2,1,0:T(8,128)} custom-call(s32[5]{0:T(128)S(1)} %stack.15.place, bf16[17,32,128]{2,1,0:T(8,128)(2,1)S(1)} %pad_maximum_fusion.1.next_to, bf16[3,32,128]{2,1,0:T(8,128)(2,1)S(1)} %pad_maximum_fusion.3.extra, bf16[3,32,128]{2,1,0:T(8,128)(2,1)S(1)} %collective-permute-done.4.across, bf16[96,384]{1,0:T(8,128)(2,1)S(1)} %get-tuple-element.21.w1, ...), custom_call_target="tpu_custom_call" | custom-call | flops 2000000000 | bytes 4000000 | tf_op jit(solution)/shard_map/pallas_call | solution.py:352
  (14 shorter events, 0.1 us)
Async XLA Ops:
  0.0 0.9 %copy-start.1 = (f32[16,8,512]{2,1,0:T(8,128)S(1)}, f32[16,8,512]{2,1,0:T(8,128)}, u32[]{:S(2)}) copy-start(f32[16,8,512]{2,1,0:T(8,128)} %inten.1) | copy-start | bytes 786436
  1.0 3.7 %copy-start.2 = (bf16[3,3,48,32]{2,3,1,0:T(8,128)(2,1)S(1)}, bf16[3,3,48,32]{2,3,1,0:T(8,128)(2,1)}, u32[]{:S(2)}) copy-start(bf16[3,3,48,32]{2,3,1,0:T(8,128)(2,1)} %param.4) | copy-start | bytes 82948
  1.5 5.3 %collective-permute-start.1 = (bf16[17,16,128]{2,1,0:T(8,128)(2,1)S(1)}, bf16[17,16,128]{2,1,0:T(8,128)(2,1)S(1)}, u32[]{:S(2)}, u32[]{:S(2)}) collective-permute-start(bf16[17,16,128]{2,1,0:T(8,128)(2,1)S(1)} %get-tuple-element.18), channel_id=1, source_target_pairs={{0,16},{16,0},{1,17},{17,1},{2,18},{18,2},{3,19},{19,3},{4,20},{20... | collective-permute-start | bytes 208904 | tf_op jit(solution)/shard_map/ppermute | solution.py:285
  4.6 9.6 %collective-permute-start = (bf16[17,16,128]{2,1,0:T(8,128)(2,1)S(1)}, bf16[17,16,128]{2,1,0:T(8,128)(2,1)S(1)}, u32[]{:S(2)}, u32[]{:S(2)}) collective-permute-start(bf16[17,16,128]{2,1,0:T(8,128)(2,1)S(1)} %get-tuple-element.17), channel_id=1, source_target_pairs={{1,2},{3,4},{5,6},{7,8},{9,10},{11,12},{13,14},{2,1},{4,3},{6,5},{... | collective-permute-start | bytes 208904 | tf_op jit(solution)/shard_map/ppermute | solution.py:30
  4.6 5.8 %copy-start = (bf16[5,3,3,48,48]{4,3,2,1,0:T(8,128)(2,1)S(1)}, bf16[5,3,3,48,48]{4,3,2,1,0:T(8,128)(2,1)}, u32[]{:S(2)}) copy-start(bf16[5,3,3,48,48]{4,3,2,1,0:T(8,128)(2,1)} %w_rest.1) | copy-start | bytes 622084
  6.9 1.4 %collective-permute-start.2 = (bf16[17,32,128]{2,1,0:T(8,128)(2,1)S(1)}, bf16[17,32,128]{2,1,0:T(8,128)(2,1)S(1)}, u32[]{:S(2)}, u32[]{:S(2)}) collective-permute-start(bf16[17,32,128]{2,1,0:T(8,128)(2,1)S(1)} %pad_maximum_fusion.own), channel_id=1, source_target_pairs={{0,1},{2,3},{4,5},{6,7},{8,9},{10,11},{12,13},{14,15},{1,0},{3,2},... | collective-permute-start | bytes 417800 | tf_op jit(solution)/shard_map/ppermute | solution.py:30
  7.0 7.3 %collective-permute-start.4 = (bf16[3,32,128]{2,1,0:T(8,128)(2,1)S(1)}, bf16[3,32,128]{2,1,0:T(8,128)(2,1)S(1)}, u32[]{:S(2)}, u32[]{:S(2)}) collective-permute-start(bf16[3,32,128]{2,1,0:T(8,128)(2,1)S(1)} %maximum_select_fusion), channel_id=1, source_target_pairs={{0,1},{2,0},{4,2},{6,4},{8,6},{10,8},{12,10},{14,12},{1,3},{3,5},{... | collective-permute-start | bytes 73736 | tf_op jit(solution)/shard_map/ppermute | solution.py:306
  8.4 5.8 %collective-permute-start.3 = (bf16[23,16,128]{2,1,0:T(8,128)(2,1)S(1)}, bf16[23,16,128]{2,1,0:T(8,128)(2,1)S(1)}, u32[]{:S(2)}, u32[]{:S(2)}) collective-permute-start(bf16[23,16,128]{2,1,0:T(8,128)(2,1)S(1)} %pad_maximum_fusion.2), channel_id=1, source_target_pairs={{1,2},{3,4},{5,6},{7,8},{9,10},{11,12},{13,14},{2,1},{4,3},{6,5},{... | collective-permute-start | bytes 282632 | tf_op jit(solution)/shard_map/ppermute | solution.py:30

commit v8 on v7

--- a/solution.py
+++ b/solution.py
@@ -34,9 +34,15 @@
     return pltpu.roll(x, by % x.shape[-1], x.ndim - 1)
 
 
-def pack(place, inten, *outs):
+def pack(place, source, w_first, w_rest, first, rest, *refs):
+    *outs, inten, sems = refs
+    copies = [(source, inten), (w_first, first), (w_rest, rest)]
+    copies = [pltpu.make_async_copy(x, y, sems.at[k]) for k, (x, y) in enumerate(copies)]
+    for copy in copies:
+        copy.start()
     acqs, cols, rows = inten.shape
     tiles, blocks = len(outs), outs[0].shape[0]
+    copies[0].wait()
     tile = rows // tiles
     wide = tile // LANES
     sides = blocks - cols * wide
@@ -67,10 +73,12 @@
         out[cols * wide] = right.astype(jnp.bfloat16)
         if sides == 2:
             out[cols * wide + 1] = left.astype(jnp.bfloat16)
+    for copy in copies[1:]:
+        copy.wait()
 
 
 def spread(swap, place, w_first, w_rest, first, rest):
-    channels, depth = w_first.shape[2:]
+    depth, channels = w_first.shape[2:]
 
     def laid(pieces):
         step = 3 * pieces[0].shape[1]
@@ -84,7 +92,7 @@
     odd = place[4] == 1
     taps = [(a, b) for a in range(3) for b in range(3)]
     late = [(jnp.where(odd, 2 - a, a), b) for a, b in taps]
-    pieces = [w_first[a, b].astype(jnp.float32) for a, b in taps]
+    pieces = [w_first[a, b].astype(jnp.float32).T for a, b in late]
     if swap:
         half = depth // 2
         moved = [jnp.concatenate([x[:, half:], x[:, :half]], axis=1) for x in pieces]
@@ -273,13 +281,20 @@
     smem = pl.BlockSpec(memory_space=pltpu.SMEM)
 
     blocks = cols * wide + (1 if tm == 2 else 2)
-    packed = pl.pallas_call(
+    far_away = pl.BlockSpec(memory_space=pltpu.HBM)
+    given = [intensity, w_first.transpose(0, 1, 3, 2), w_rest]
+    w_first, w_rest, *packed = pl.pallas_call(
         pack,
-        out_shape=[jax.ShapeDtypeStruct((blocks, acqs_own, LANES), jnp.bfloat16)] * tm,
-        in_specs=[smem, vmem],
-        out_specs=[vmem] * tm,
+        out_shape=[jax.ShapeDtypeStruct(x.shape, x.dtype) for x in given[1:]]
+        + [jax.ShapeDtypeStruct((blocks, acqs_own, LANES), jnp.bfloat16)] * tm,
+        in_specs=[smem] + [far_away] * 3,
+        out_specs=[vmem] * (2 + tm),
+        scratch_shapes=[pltpu.VMEM(intensity.shape, intensity.dtype), pltpu.SemaphoreType.DMA((3,))],
         compiler_params=pltpu.CompilerParams(vmem_limit_bytes=8 * 1024 * 1024),
-    )(jnp.reshape(m, (1,)).astype(jnp.int32), intensity)
+    )(
+        jnp.reshape(m, (1,)).astype(jnp.int32),
+        *(pltpu.with_memory_space_constraint(x, pltpu.HBM) for x in given),
+    )
     parts = [packed[0]]
     for d in range(1, tm):
         parts.append(lax.ppermute(packed[d], "tm", [(i, (i + d) % tm) for i in range(tm)]))
@@ -288,8 +303,25 @@
     beside = [swapped(packed[0], odds, 1)]
     own = jnp.concatenate(parts, axis=1)
     odd = s % 2 == 1
-    w_first = jnp.where(odd, w_first[::-1], w_first)
-    own, w_first = lax.optimization_barrier((own, w_first))
+    place = jnp.stack(
+        [s * cols, jnp.int32(cols * space), m * tile, jnp.int32(rows), s % 2]
+    ).astype(jnp.int32)
+    if tm != 2:
+        order = (m - jnp.arange(tm)) % tm
+        w_first = jnp.take(w_first.reshape(3, 3, tm, acqs_own, channels), order, axis=2)
+        w_first = w_first.reshape(3, 3, acqs, channels)
+    w1, wr = pl.pallas_call(
+        functools.partial(spread, tm == 2),
+        out_shape=[
+            jax.ShapeDtypeStruct((PAIR * channels, 3 * (PAIR + 2) * acqs), jnp.bfloat16),
+            jax.ShapeDtypeStruct((LAYERS - 1, PAIR * channels, 3 * (PAIR + 2) * channels), jnp.bfloat16),
+        ],
+        in_specs=[smem, vmem, vmem],
+        out_specs=[vmem, vmem],
+        compiler_params=pltpu.CompilerParams(vmem_limit_bytes=8 * 1024 * 1024),
+        cost_estimate=pl.CostEstimate(flops=100000000, bytes_accessed=1000000, transcendentals=0),
+    )(place, w_first, w_rest)
+    own, w1, wr = lax.optimization_barrier((own, w1, wr))
     mate = swapped(own, evens, 1)
 
     far = HALO - cols
@@ -316,24 +348,6 @@
     beside = jnp.concatenate(beside + arrived[: tm - 1], axis=1)
     extra = jnp.concatenate(arrived[tm - 1 :], axis=1)
 
-    place = jnp.stack(
-        [s * cols, jnp.int32(cols * space), m * tile, jnp.int32(rows), s % 2]
-    ).astype(jnp.int32)
-    if tm != 2:
-        order = (m - jnp.arange(tm)) % tm
-        w_first = jnp.take(w_first.reshape(3, 3, channels, tm, acqs_own), order, axis=3)
-        w_first = w_first.reshape(3, 3, channels, acqs)
-    w1, wr = pl.pallas_call(
-        functools.partial(spread, tm == 2),
-        out_shape=[
-            jax.ShapeDtypeStruct((PAIR * channels, 3 * (PAIR + 2) * acqs), jnp.bfloat16),
-            jax.ShapeDtypeStruct((LAYERS - 1, PAIR * channels, 3 * (PAIR + 2) * channels), jnp.bfloat16),
-        ],
-        in_specs=[smem, vmem, vmem],
-        out_specs=[vmem, vmem],
-        compiler_params=pltpu.CompilerParams(vmem_limit_bytes=8 * 1024 * 1024),
-        cost_estimate=pl.CostEstimate(flops=10**8, bytes_accessed=10**6, transcendentals=0),
-    )(place, w_first, w_rest)
     width = tile + LANES
     limit = pltpu.CompilerParams(vmem_limit_bytes=20 * 1024 * 1024)
     inputs = chip_layers(cols)
@@ -346,7 +360,7 @@
         in_specs=[smem] + [vmem] * 4,
         out_specs=[vmem] * (1 + inputs),
         compiler_params=limit,
-        cost_estimate=pl.CostEstimate(flops=10**9, bytes_accessed=4 * 10**6, transcendentals=10**6),
+        cost_estimate=pl.CostEstimate(flops=4000000000, bytes_accessed=4 * 10**6, transcendentals=10**6),
     )(place, own, mate, w1, wr)
     lacking = [cols + 2 * (LAYERS - n) - (reach[n] if n < inputs else 0) for n in range(LAYERS)]
     return pl.pallas_call(

time: 19 us -> 18.3 us (0.963)
  the two profiles are of different devices: /device:TPU:0 before, /device:TPU:25 now
where the time goes in v8:
time: 18.3 us; the launch traced here: 18.2 us
  Pallas kernels  9.93 us (54%)
  starting transfers between devices  7.07 us (39%)
  waiting for transfers between devices  0.91 us (5%)
    pallas_call x1, Pallas kernels, shards(): pl.pallas_call(rest_part, out_shape=jax.ShapeDtypeStruct((channels, cols,...  4.61 us
    ppermute x3, starting transfers between devices, swapped(): return lax.ppermute(x, ('tm', 'space'), pairs)  3.91 us
    pallas_call x1, Pallas kernels, shards(): pl.pallas_call(chip_part, out_shape=[jax.ShapeDtypeStruct((2 * cols, acqs...  2.7 us
    ppermute x1, starting transfers between devices, shards(): across = lax.ppermute(jnp.where(odd, tail, head), 'space', ring)  1.85 us
    pallas_call x1, Pallas kernels, shards(): pl.pallas_call(pack, out_shape=[jax.ShapeDtypeStruct(x.shape, x.dtype) fo...  1.54 us
    ppermute x1, starting transfers between devices, shards(): lax.ppermute(packed[d], 'tm', [(i, (i + d) % tm) for i in range(tm)])  1.31 us
    pallas_call x1, Pallas kernels, shards(): pl.pallas_call(functools.partial(spread, tm == 2), out_shape=[jax.ShapeDt...  1.08 us
    ppermute x3, waiting for transfers between devices, swapped(): return lax.ppermute(x, ('tm', 'space'), pairs)  0.91 us
  transfers between devices with their start and end apart: 5, of which 1 were waited for; matrix products, arithmetic and copies ran while one was open for 1% of the time, Pallas kernels for 21%

profile of v8, /device:TPU:25, one launch (start us, length us, event | category | flops | bytes accessed | tf_op | source)
XLA Modules:
  0.0 18.2 jit_solution(14570130358132954820)
XLA Ops:
  0.0 1.5 %shard_map.37 = (bf16[3,3,32,48]{3,2,1,0:T(8,128)(2,1)S(1)}, bf16[5,3,3,48,48]{4,3,2,1,0:T(8,128)(2,1)S(1)}, bf16[17,16,128]{2,1,0:T(8,128)(2,1)S(1)}, bf16[17,16,128]{2,1,0:T(8,128)(2,1)S(1)}) custom-call(s32[1]{0:T(128)} %bitcast.3.place, f32[16,8,512]{2,1,0:T(8,128)} %source.1, bf16[3,3,32,48]{3,2,1,0:T(8,128)(2,1)} %bitcast.5, ...), custom_call_target="tpu_custom_call" | custom-call | tf_op jit(solution)/shard_map/pallas_call | solution.py:286
  1.5 1.3 %collective-permute-start.1 = (bf16[17,16,128]{2,1,0:T(8,128)(2,1)S(1)}, bf16[17,16,128]{2,1,0:T(8,128)(2,1)S(1)}, u32[]{:S(2)}, u32[]{:S(2)}) collective-permute-start(bf16[17,16,128]{2,1,0:T(8,128)(2,1)S(1)} %get-tuple-element.21), channel_id=1, source_target_pairs={{0,16},{16,0},{1,17},{17,1},{2,18},{18,2},{3,19},{19,3},{4,20},{20... | collective-permute-start | bytes 208904 | tf_op jit(solution)/shard_map/ppermute | solution.py:300
  2.9 2.1 %collective-permute-start = (bf16[17,16,128]{2,1,0:T(8,128)(2,1)S(1)}, bf16[17,16,128]{2,1,0:T(8,128)(2,1)S(1)}, u32[]{:S(2)}, u32[]{:S(2)}) collective-permute-start(bf16[17,16,128]{2,1,0:T(8,128)(2,1)S(1)} %get-tuple-element.20), channel_id=1, source_target_pairs={{1,2},{3,4},{5,6},{7,8},{9,10},{11,12},{13,14},{2,1},{4,3},{6,5},{... | collective-permute-start | bytes 208904 | tf_op jit(solution)/shard_map/ppermute | solution.py:30
  4.9 0.1 stack.15.place
  5.0 1.1 %shard_map.38 = (bf16[96,384]{1,0:T(8,128)(2,1)S(1)}, bf16[5,96,576]{2,1,0:T(8,128)(2,1)S(1)}) custom-call(s32[5]{0:T(128)S(1)} %stack.15.place, bf16[3,3,32,48]{3,2,1,0:T(8,128)(2,1)S(1)} %get-tuple-element.22.w_first, bf16[5,3,3,48,48]{4,3,2,1,0:T(8,128)(2,1)S(1)} %get-tuple-element.23.w_rest), custom_call_target="tpu_custom_call" | custom-call | flops 100000000 | bytes 1000000 | tf_op jit(solution)/shard_map/pallas_call | solution.py:313
  6.1 0.0 collective-permute-done.1
  6.1 0.6 %collective-permute-start.2 = (bf16[17,32,128]{2,1,0:T(8,128)(2,1)S(1)}, bf16[17,32,128]{2,1,0:T(8,128)(2,1)S(1)}, u32[]{:S(2)}, u32[]{:S(2)}) collective-permute-start(bf16[17,32,128]{2,1,0:T(8,128)(2,1)S(1)} %pad_maximum_fusion.own), channel_id=1, source_target_pairs={{0,1},{2,3},{4,5},{6,7},{8,9},{10,11},{12,13},{14,15},{1,0},{3,2},... | collective-permute-start | bytes 417800 | tf_op jit(solution)/shard_map/ppermute | solution.py:30
  6.7 1.8 %collective-permute-start.4 = (bf16[3,32,128]{2,1,0:T(8,128)(2,1)S(1)}, bf16[3,32,128]{2,1,0:T(8,128)(2,1)S(1)}, u32[]{:S(2)}, u32[]{:S(2)}) collective-permute-start(bf16[3,32,128]{2,1,0:T(8,128)(2,1)S(1)} %maximum_select_fusion), channel_id=1, source_target_pairs={{0,1},{2,0},{4,2},{6,4},{8,6},{10,8},{12,10},{14,12},{1,3},{3,5},{... | collective-permute-start | bytes 73736 | tf_op jit(solution)/shard_map/ppermute | solution.py:338
  8.6 0.0 collective-permute-done.2.mate
  8.6 1.3 %collective-permute-start.3 = (bf16[23,16,128]{2,1,0:T(8,128)(2,1)S(1)}, bf16[23,16,128]{2,1,0:T(8,128)(2,1)S(1)}, u32[]{:S(2)}, u32[]{:S(2)}) collective-permute-start(bf16[23,16,128]{2,1,0:T(8,128)(2,1)S(1)} %pad_maximum_fusion.2), channel_id=1, source_target_pairs={{1,2},{3,4},{5,6},{7,8},{9,10},{11,12},{13,14},{2,1},{4,3},{6,5},{... | collective-permute-start | bytes 282632 | tf_op jit(solution)/shard_map/ppermute | solution.py:30
  9.9 2.7 %shard_map.39 = (f32[16,32,384]{2,1,0:T(8,128)S(1)}, bf16[960,384]{1,0:T(8,128)(2,1)S(1)}, bf16[1152,384]{1,0:T(8,128)(2,1)S(1)}, bf16[864,384]{1,0:T(8,128)(2,1...) custom-call(s32[5]{0:T(128)S(1)} %stack.15.place, bf16[17,32,128]{2,1,0:T(8,128)(2,1)S(1)} %pad_maximum_fusion.own, ...), custom_call_target="tpu_custom_call" | custom-call | flops 4000000000 | bytes 4000000 | tf_op jit(solution)/shard_map/pallas_call | solution.py:356
  12.6 0.9 %collective-permute-done.3 = bf16[23,16,128]{2,1,0:T(8,128)(2,1)S(1)} collective-permute-done((bf16[23,16,128]{2,1,0:T(8,128)(2,1)S(1)}, bf16[23,16,128]{2,1,0:T(8,128)(2,1)S(1)}, u32[]{:S(2)}, u32[]{:S(2)}) %collective-permute-start.3) | collective-permute-done | bytes 94240 | tf_op jit(solution)/shard_map/ppermute | solution.py:30
  13.5 0.0 collective-permute-done
  13.6 0.0 collective-permute-done.4.across
  13.6 4.6 %shard_map.40 = f32[48,8,256]{2,1,0:T(8,128)} custom-call(s32[5]{0:T(128)S(1)} %stack.15.place, bf16[17,32,128]{2,1,0:T(8,128)(2,1)S(1)} %pad_maximum_fusion.1.next_to, bf16[3,32,128]{2,1,0:T(8,128)(2,1)S(1)} %pad_maximum_fusion.3.extra, bf16[3,32,128]{2,1,0:T(8,128)(2,1)S(1)} %collective-permute-done.4.across, bf16[96,384]{1,0:T(8,128)(2,1)S(1)} %get-tuple-element.27.w1, ...), custom_call_target="tpu_custom_call" | custom-call | flops 2000000000 | bytes 4000000 | tf_op jit(solution)/shard_map/pallas_call | solution.py:366
  (13 shorter events, 0.1 us)
Async XLA Ops:
  1.5 4.5 %collective-permute-start.1 = (bf16[17,16,128]{2,1,0:T(8,128)(2,1)S(1)}, bf16[17,16,128]{2,1,0:T(8,128)(2,1)S(1)}, u32[]{:S(2)}, u32[]{:S(2)}) collective-permute-start(bf16[17,16,128]{2,1,0:T(8,128)(2,1)S(1)} %get-tuple-element.21), channel_id=1, source_target_pairs={{0,16},{16,0},{1,17},{17,1},{2,18},{18,2},{3,19},{19,3},{4,20},{20... | collective-permute-start | bytes 208904 | tf_op jit(solution)/shard_map/ppermute | solution.py:300
  2.9 10.7 %collective-permute-start = (bf16[17,16,128]{2,1,0:T(8,128)(2,1)S(1)}, bf16[17,16,128]{2,1,0:T(8,128)(2,1)S(1)}, u32[]{:S(2)}, u32[]{:S(2)}) collective-permute-start(bf16[17,16,128]{2,1,0:T(8,128)(2,1)S(1)} %get-tuple-element.20), channel_id=1, source_target_pairs={{1,2},{3,4},{5,6},{7,8},{9,10},{11,12},{13,14},{2,1},{4,3},{6,5},{... | collective-permute-start | bytes 208904 | tf_op jit(solution)/shard_map/ppermute | solution.py:30
  6.1 2.4 %collective-permute-start.2 = (bf16[17,32,128]{2,1,0:T(8,128)(2,1)S(1)}, bf16[17,32,128]{2,1,0:T(8,128)(2,1)S(1)}, u32[]{:S(2)}, u32[]{:S(2)}) collective-permute-start(bf16[17,32,128]{2,1,0:T(8,128)(2,1)S(1)} %pad_maximum_fusion.own), channel_id=1, source_target_pairs={{0,1},{2,3},{4,5},{6,7},{8,9},{10,11},{12,13},{14,15},{1,0},{3,2},... | collective-permute-start | bytes 417800 | tf_op jit(solution)/shard_map/ppermute | solution.py:30
  6.7 6.9 %collective-permute-start.4 = (bf16[3,32,128]{2,1,0:T(8,128)(2,1)S(1)}, bf16[3,32,128]{2,1,0:T(8,128)(2,1)S(1)}, u32[]{:S(2)}, u32[]{:S(2)}) collective-permute-start(bf16[3,32,128]{2,1,0:T(8,128)(2,1)S(1)} %maximum_select_fusion), channel_id=1, source_target_pairs={{0,1},{2,0},{4,2},{6,4},{8,6},{10,8},{12,10},{14,12},{1,3},{3,5},{... | collective-permute-start | bytes 73736 | tf_op jit(solution)/shard_map/ppermute | solution.py:338
  8.6 4.9 %collective-permute-start.3 = (bf16[23,16,128]{2,1,0:T(8,128)(2,1)S(1)}, bf16[23,16,128]{2,1,0:T(8,128)(2,1)S(1)}, u32[]{:S(2)}, u32[]{:S(2)}) collective-permute-start(bf16[23,16,128]{2,1,0:T(8,128)(2,1)S(1)} %pad_maximum_fusion.2), channel_id=1, source_target_pairs={{1,2},{3,4},{5,6},{7,8},{9,10},{11,12},{13,14},{2,1},{4,3},{6,5},{... | collective-permute-start | bytes 282632 | tf_op jit(solution)/shard_map/ppermute | solution.py:30

commit v9 on v8

--- a/solution.py
+++ b/solution.py
@@ -13,7 +13,7 @@
 MARGIN = 16
 LANES = 128
 PAIR = 2
-BESIDE = 2
+BESIDE = 3
 
 
 def swapped(x, lows, by):
@@ -218,7 +218,7 @@
 def rest_part(place, next_to, extra, across, w1, wr, chip, *refs):
     acqs, width = chip.shape[1:]
     count = chip_layers(chip.shape[0] // 2)
-    given, out, inten, results, mine = refs[:count], refs[count], refs[count + 1], refs[count + 2], refs[count + 3 :]
+    given, out, inten, mine = refs[:count], refs[count], refs[count + 1], refs[count + 2 :]
     channels, cols, tile = out.shape
     win = Window(place, cols, tile, acqs)
     more = HALO - cols
@@ -248,7 +248,7 @@
                 if layer < LAYERS:
                     put(mine[layer], wanted.index(j), win.hidden(RADIUS + layer + j, summed))
                 else:
-                    results[jnp.where(win.odd, cols - 1 - j, j)] = summed
+                    out[:, pl.ds(jnp.where(win.odd, cols - 1 - j, j), 1), :] = summed[:, None, :]
 
             columns(weight, wanted, source, channels, tile if layer == LAYERS else width, done)
         depth = acqs if layer == 0 else channels
@@ -259,9 +259,6 @@
             else:
                 ref, k = given[layer], j - first
             return ref[k * 3 * depth : (k + 1) * 3 * depth, :span]
-
-    for j in range(cols):
-        out[:, j, :] = results[j]
 
 
 def chip_layers(cols):
@@ -370,7 +367,6 @@
         out_specs=vmem,
         scratch_shapes=[
             pltpu.VMEM((2 * HALO - cols, acqs, width), jnp.float32),
-            pltpu.VMEM((cols, channels, tile), jnp.float32),
         ]
         + [pltpu.VMEM((lacking[n] * 3 * depths[n], width), jnp.bfloat16) for n in range(LAYERS)],
         compiler_params=limit,

time: 18.3 us -> 18.3 us (level)
  no operation moved by 1% of the time
where the time goes in v9:
time: 18.3 us; the launch traced here: 18.1 us
  Pallas kernels  9.96 us (54%)
  starting transfers between devices  7.07 us (39%)
  waiting for transfers between devices  0.82 us (4%)
    pallas_call x1, Pallas kernels, shards(): pl.pallas_call(rest_part, out_shape=jax.ShapeDtypeStruct((channels, cols,...  4.55 us
    ppermute x3, starting transfers between devices, swapped(): return lax.ppermute(x, ('tm', 'space'), pairs)  3.91 us
    pallas_call x1, Pallas kernels, shards(): pl.pallas_call(chip_part, out_shape=[jax.ShapeDtypeStruct((2 * cols, acqs...  2.79 us
    ppermute x1, starting transfers between devices, shards(): across = lax.ppermute(jnp.where(odd, tail, head), 'space', ring)  1.85 us
    pallas_call x1, Pallas kernels, shards(): pl.pallas_call(pack, out_shape=[jax.ShapeDtypeStruct(x.shape, x.dtype) fo...  1.54 us
    ppermute x1, starting transfers between devices, shards(): lax.ppermute(packed[d], 'tm', [(i, (i + d) % tm) for i in range(tm)])  1.31 us
    pallas_call x1, Pallas kernels, shards(): pl.pallas_call(functools.partial(spread, tm == 2), out_shape=[jax.ShapeDt...  1.08 us
    ppermute x3, waiting for transfers between devices, swapped(): return lax.ppermute(x, ('tm', 'space'), pairs)  0.82 us
  transfers between devices with their start and end apart: 5, of which 1 were waited for; matrix products, arithmetic and copies ran while one was open for 1% of the time, Pallas kernels for 21%

profile of v9, /device:TPU:25, one launch (start us, length us, event | category | flops | bytes accessed | tf_op | source)
XLA Modules:
  0.0 18.1 jit_solution(4642680275897551309)
XLA Ops:
  0.0 1.5 %shard_map.37 = (bf16[3,3,32,48]{3,2,1,0:T(8,128)(2,1)S(1)}, bf16[5,3,3,48,48]{4,3,2,1,0:T(8,128)(2,1)S(1)}, bf16[17,16,128]{2,1,0:T(8,128)(2,1)S(1)}, bf16[17,16,128]{2,1,0:T(8,128)(2,1)S(1)}) custom-call(s32[1]{0:T(128)} %bitcast.3.place, f32[16,8,512]{2,1,0:T(8,128)} %source.1, bf16[3,3,32,48]{3,2,1,0:T(8,128)(2,1)} %bitcast.5, ...), custom_call_target="tpu_custom_call" | custom-call | tf_op jit(solution)/shard_map/pallas_call | solution.py:283
  1.5 1.3 %collective-permute-start.1 = (bf16[17,16,128]{2,1,0:T(8,128)(2,1)S(1)}, bf16[17,16,128]{2,1,0:T(8,128)(2,1)S(1)}, u32[]{:S(2)}, u32[]{:S(2)}) collective-permute-start(bf16[17,16,128]{2,1,0:T(8,128)(2,1)S(1)} %get-tuple-element.21), channel_id=1, source_target_pairs={{0,16},{16,0},{1,17},{17,1},{2,18},{18,2},{3,19},{19,3},{4,20},{20... | collective-permute-start | bytes 208904 | tf_op jit(solution)/shard_map/ppermute | solution.py:297
  2.9 2.1 %collective-permute-start = (bf16[17,16,128]{2,1,0:T(8,128)(2,1)S(1)}, bf16[17,16,128]{2,1,0:T(8,128)(2,1)S(1)}, u32[]{:S(2)}, u32[]{:S(2)}) collective-permute-start(bf16[17,16,128]{2,1,0:T(8,128)(2,1)S(1)} %get-tuple-element.20), channel_id=1, source_target_pairs={{1,2},{3,4},{5,6},{7,8},{9,10},{11,12},{13,14},{2,1},{4,3},{6,5},{... | collective-permute-start | bytes 208904 | tf_op jit(solution)/shard_map/ppermute | solution.py:30
  4.9 0.1 stack.15.place
  5.0 1.1 %shard_map.38 = (bf16[96,384]{1,0:T(8,128)(2,1)S(1)}, bf16[5,96,576]{2,1,0:T(8,128)(2,1)S(1)}) custom-call(s32[5]{0:T(128)S(1)} %stack.15.place, bf16[3,3,32,48]{3,2,1,0:T(8,128)(2,1)S(1)} %get-tuple-element.22.w_first, bf16[5,3,3,48,48]{4,3,2,1,0:T(8,128)(2,1)S(1)} %get-tuple-element.23.w_rest), custom_call_target="tpu_custom_call" | custom-call | flops 100000000 | bytes 1000000 | tf_op jit(solution)/shard_map/pallas_call | solution.py:310
  6.1 0.0 collective-permute-done.1
  6.1 0.6 %collective-permute-start.2 = (bf16[17,32,128]{2,1,0:T(8,128)(2,1)S(1)}, bf16[17,32,128]{2,1,0:T(8,128)(2,1)S(1)}, u32[]{:S(2)}, u32[]{:S(2)}) collective-permute-start(bf16[17,32,128]{2,1,0:T(8,128)(2,1)S(1)} %pad_maximum_fusion.own), channel_id=1, source_target_pairs={{0,1},{2,3},{4,5},{6,7},{8,9},{10,11},{12,13},{14,15},{1,0},{3,2},... | collective-permute-start | bytes 417800 | tf_op jit(solution)/shard_map/ppermute | solution.py:30
  6.7 1.8 %collective-permute-start.4 = (bf16[3,32,128]{2,1,0:T(8,128)(2,1)S(1)}, bf16[3,32,128]{2,1,0:T(8,128)(2,1)S(1)}, u32[]{:S(2)}, u32[]{:S(2)}) collective-permute-start(bf16[3,32,128]{2,1,0:T(8,128)(2,1)S(1)} %maximum_select_fusion), channel_id=1, source_target_pairs={{0,1},{2,0},{4,2},{6,4},{8,6},{10,8},{12,10},{14,12},{1,3},{3,5},{... | collective-permute-start | bytes 73736 | tf_op jit(solution)/shard_map/ppermute | solution.py:335
  8.6 0.0 collective-permute-done.2.mate
  8.6 1.3 %collective-permute-start.3 = (bf16[23,16,128]{2,1,0:T(8,128)(2,1)S(1)}, bf16[23,16,128]{2,1,0:T(8,128)(2,1)S(1)}, u32[]{:S(2)}, u32[]{:S(2)}) collective-permute-start(bf16[23,16,128]{2,1,0:T(8,128)(2,1)S(1)} %pad_maximum_fusion.2), channel_id=1, source_target_pairs={{1,2},{3,4},{5,6},{7,8},{9,10},{11,12},{13,14},{2,1},{4,3},{6,5},{... | collective-permute-start | bytes 282632 | tf_op jit(solution)/shard_map/ppermute | solution.py:30
  9.9 2.8 %shard_map.39 = (f32[16,32,384]{2,1,0:T(8,128)S(1)}, bf16[960,384]{1,0:T(8,128)(2,1)S(1)}, bf16[1152,384]{1,0:T(8,128)(2,1)S(1)}, bf16[864,384]{1,0:T(8,128)(2,1...) custom-call(s32[5]{0:T(128)S(1)} %stack.15.place, bf16[17,32,128]{2,1,0:T(8,128)(2,1)S(1)} %pad_maximum_fusion.own, ...), custom_call_target="tpu_custom_call" | custom-call | flops 4000000000 | bytes 4000000 | tf_op jit(solution)/shard_map/pallas_call | solution.py:353
  12.7 0.8 %collective-permute-done.3 = bf16[23,16,128]{2,1,0:T(8,128)(2,1)S(1)} collective-permute-done((bf16[23,16,128]{2,1,0:T(8,128)(2,1)S(1)}, bf16[23,16,128]{2,1,0:T(8,128)(2,1)S(1)}, u32[]{:S(2)}, u32[]{:S(2)}) %collective-permute-start.3) | collective-permute-done | bytes 94240 | tf_op jit(solution)/shard_map/ppermute | solution.py:30
  13.5 0.0 collective-permute-done
  13.6 0.0 collective-permute-done.4.across
  13.6 4.5 %shard_map.40 = f32[48,8,256]{2,1,0:T(8,128)} custom-call(s32[5]{0:T(128)S(1)} %stack.15.place, bf16[17,32,128]{2,1,0:T(8,128)(2,1)S(1)} %pad_maximum_fusion.1.next_to, bf16[3,32,128]{2,1,0:T(8,128)(2,1)S(1)} %pad_maximum_fusion.3.extra, bf16[3,32,128]{2,1,0:T(8,128)(2,1)S(1)} %collective-permute-done.4.across, bf16[96,384]{1,0:T(8,128)(2,1)S(1)} %get-tuple-element.27.w1, ...), custom_call_target="tpu_custom_call" | custom-call | flops 2000000000 | bytes 4000000 | tf_op jit(solution)/shard_map/pallas_call | solution.py:363
  (13 shorter events, 0.1 us)
Async XLA Ops:
  1.5 4.5 %collective-permute-start.1 = (bf16[17,16,128]{2,1,0:T(8,128)(2,1)S(1)}, bf16[17,16,128]{2,1,0:T(8,128)(2,1)S(1)}, u32[]{:S(2)}, u32[]{:S(2)}) collective-permute-start(bf16[17,16,128]{2,1,0:T(8,128)(2,1)S(1)} %get-tuple-element.21), channel_id=1, source_target_pairs={{0,16},{16,0},{1,17},{17,1},{2,18},{18,2},{3,19},{19,3},{4,20},{20... | collective-permute-start | bytes 208904 | tf_op jit(solution)/shard_map/ppermute | solution.py:297
  2.9 10.7 %collective-permute-start = (bf16[17,16,128]{2,1,0:T(8,128)(2,1)S(1)}, bf16[17,16,128]{2,1,0:T(8,128)(2,1)S(1)}, u32[]{:S(2)}, u32[]{:S(2)}) collective-permute-start(bf16[17,16,128]{2,1,0:T(8,128)(2,1)S(1)} %get-tuple-element.20), channel_id=1, source_target_pairs={{1,2},{3,4},{5,6},{7,8},{9,10},{11,12},{13,14},{2,1},{4,3},{6,5},{... | collective-permute-start | bytes 208904 | tf_op jit(solution)/shard_map/ppermute | solution.py:30
  6.1 2.4 %collective-permute-start.2 = (bf16[17,32,128]{2,1,0:T(8,128)(2,1)S(1)}, bf16[17,32,128]{2,1,0:T(8,128)(2,1)S(1)}, u32[]{:S(2)}, u32[]{:S(2)}) collective-permute-start(bf16[17,32,128]{2,1,0:T(8,128)(2,1)S(1)} %pad_maximum_fusion.own), channel_id=1, source_target_pairs={{0,1},{2,3},{4,5},{6,7},{8,9},{10,11},{12,13},{14,15},{1,0},{3,2},... | collective-permute-start | bytes 417800 | tf_op jit(solution)/shard_map/ppermute | solution.py:30
  6.7 6.9 %collective-permute-start.4 = (bf16[3,32,128]{2,1,0:T(8,128)(2,1)S(1)}, bf16[3,32,128]{2,1,0:T(8,128)(2,1)S(1)}, u32[]{:S(2)}, u32[]{:S(2)}) collective-permute-start(bf16[3,32,128]{2,1,0:T(8,128)(2,1)S(1)} %maximum_select_fusion), channel_id=1, source_target_pairs={{0,1},{2,0},{4,2},{6,4},{8,6},{10,8},{12,10},{14,12},{1,3},{3,5},{... | collective-permute-start | bytes 73736 | tf_op jit(solution)/shard_map/ppermute | solution.py:335
  8.6 4.9 %collective-permute-start.3 = (bf16[23,16,128]{2,1,0:T(8,128)(2,1)S(1)}, bf16[23,16,128]{2,1,0:T(8,128)(2,1)S(1)}, u32[]{:S(2)}, u32[]{:S(2)}) collective-permute-start(bf16[23,16,128]{2,1,0:T(8,128)(2,1)S(1)} %pad_maximum_fusion.2), channel_id=1, source_target_pairs={{1,2},{3,4},{5,6},{7,8},{9,10},{11,12},{13,14},{2,1},{4,3},{6,5},{... | collective-permute-start | bytes 282632 | tf_op jit(solution)/shard_map/ppermute | solution.py:30

commit v10 on v9

--- a/solution.py
+++ b/solution.py
@@ -215,13 +215,27 @@
         columns(weight, list(range(left)), source, channels, width, done)
 
 
-def rest_part(place, next_to, extra, across, w1, wr, chip, *refs):
+class Joined:
+    def __init__(self, blocks, first, others, start, count):
+        self.shape, self.first, self.others = (blocks,), first, others
+        self.starts = [start + d * blocks for d in range(count)]
+
+    def __getitem__(self, k):
+        parts = [] if self.first is None else [self.first[k]]
+        parts += [self.others[start + k] for start in self.starts]
+        return jnp.concatenate([x.astype(jnp.float32) for x in parts], axis=0)
+
+
+def rest_part(place, first_part, others, across, w1, wr, chip, *refs):
     acqs, width = chip.shape[1:]
     count = chip_layers(chip.shape[0] // 2)
     given, out, inten, mine = refs[:count], refs[count], refs[count + 1], refs[count + 2 :]
     channels, cols, tile = out.shape
     win = Window(place, cols, tile, acqs)
     more = HALO - cols
+    blocks, tiles = first_part.shape[0], acqs // first_part.shape[1]
+    next_to = Joined(blocks, first_part, others, 0, tiles - 1)
+    extra = Joined(across.shape[0], None, others, (tiles - 1) * blocks, tiles)
     for k in range(more):
         inten[k] = win.intensity(extra, k, cols - more + k, more, k)
         inten[HALO + k] = win.intensity(across, k, k, more, HALO + 2 * cols + k)
@@ -336,14 +350,7 @@
     head, tail = ends(mate)
     near = jnp.where(odd, tail, head)
     onward = parts[1:] + [near[:, d * acqs_own : (d + 1) * acqs_own] for d in range(tm)]
-    counts = [x.shape[0] for x in onward]
     onward = swapped(jnp.concatenate(onward, axis=0), odds, 1)
-    arrived, start = [], 0
-    for count in counts:
-        arrived.append(onward[start : start + count])
-        start += count
-    beside = jnp.concatenate(beside + arrived[: tm - 1], axis=1)
-    extra = jnp.concatenate(arrived[tm - 1 :], axis=1)
 
     width = tile + LANES
     limit = pltpu.CompilerParams(vmem_limit_bytes=20 * 1024 * 1024)
@@ -371,7 +378,7 @@
         + [pltpu.VMEM((lacking[n] * 3 * depths[n], width), jnp.bfloat16) for n in range(LAYERS)],
         compiler_params=limit,
         cost_estimate=pl.CostEstimate(flops=2 * 10**9, bytes_accessed=4 * 10**6, transcendentals=10**6),
-    )(place, beside, extra, across, w1, wr, chip, *given)
+    )(place, beside[0], onward, across, w1, wr, chip, *given)
 
 
 def solution(mesh):

time: 18.3 us -> 18.2 us (level)
  no operation moved by 1% of the time
where the time goes in v10:
time: 18.2 us; the launch traced here: 18.1 us
  Pallas kernels  9.97 us (55%)
  starting transfers between devices  7.07 us (39%)
  waiting for transfers between devices  0.8 us (4%)
    pallas_call x1, Pallas kernels, shards(): pl.pallas_call(rest_part, out_shape=jax.ShapeDtypeStruct((channels, cols,...  4.55 us
    ppermute x3, starting transfers between devices, swapped(): return lax.ppermute(x, ('tm', 'space'), pairs)  3.91 us
    pallas_call x1, Pallas kernels, shards(): pl.pallas_call(chip_part, out_shape=[jax.ShapeDtypeStruct((2 * cols, acqs...  2.8 us
    ppermute x1, starting transfers between devices, shards(): across = lax.ppermute(jnp.where(odd, tail, head), 'space', ring)  1.85 us
    pallas_call x1, Pallas kernels, shards(): pl.pallas_call(pack, out_shape=[jax.ShapeDtypeStruct(x.shape, x.dtype) fo...  1.54 us
    ppermute x1, starting transfers between devices, shards(): lax.ppermute(packed[d], 'tm', [(i, (i + d) % tm) for i in range(tm)])  1.31 us
    pallas_call x1, Pallas kernels, shards(): pl.pallas_call(functools.partial(spread, tm == 2), out_shape=[jax.ShapeDt...  1.08 us
    ppermute x3, waiting for transfers between devices, swapped(): return lax.ppermute(x, ('tm', 'space'), pairs)  0.79 us
  transfers between devices with their start and end apart: 5, of which 1 were waited for; matrix products, arithmetic and copies ran while one was open for 1% of the time, Pallas kernels for 21%

profile of v10, /device:TPU:25, one launch (start us, length us, event | category | flops | bytes accessed | tf_op | source)
XLA Modules:
  0.0 18.1 jit_solution(1596821955225676772)
XLA Ops:
  0.0 1.5 %shard_map.37 = (bf16[3,3,32,48]{3,2,1,0:T(8,128)(2,1)S(1)}, bf16[5,3,3,48,48]{4,3,2,1,0:T(8,128)(2,1)S(1)}, bf16[17,16,128]{2,1,0:T(8,128)(2,1)S(1)}, bf16[17,16,128]{2,1,0:T(8,128)(2,1)S(1)}) custom-call(s32[1]{0:T(128)} %bitcast.3.place, f32[16,8,512]{2,1,0:T(8,128)} %source.1, bf16[3,3,32,48]{3,2,1,0:T(8,128)(2,1)} %bitcast.5, ...), custom_call_target="tpu_custom_call" | custom-call | tf_op jit(solution)/shard_map/pallas_call | solution.py:297
  1.5 1.3 %collective-permute-start.1 = (bf16[17,16,128]{2,1,0:T(8,128)(2,1)S(1)}, bf16[17,16,128]{2,1,0:T(8,128)(2,1)S(1)}, u32[]{:S(2)}, u32[]{:S(2)}) collective-permute-start(bf16[17,16,128]{2,1,0:T(8,128)(2,1)S(1)} %get-tuple-element.21), channel_id=1, source_target_pairs={{0,16},{16,0},{1,17},{17,1},{2,18},{18,2},{3,19},{19,3},{4,20},{20... | collective-permute-start | bytes 208904 | tf_op jit(solution)/shard_map/ppermute | solution.py:311
  2.9 2.1 %collective-permute-start = (bf16[17,16,128]{2,1,0:T(8,128)(2,1)S(1)}, bf16[17,16,128]{2,1,0:T(8,128)(2,1)S(1)}, u32[]{:S(2)}, u32[]{:S(2)}) collective-permute-start(bf16[17,16,128]{2,1,0:T(8,128)(2,1)S(1)} %get-tuple-element.20), channel_id=1, source_target_pairs={{1,2},{3,4},{5,6},{7,8},{9,10},{11,12},{13,14},{2,1},{4,3},{6,5},{... | collective-permute-start | bytes 208904 | tf_op jit(solution)/shard_map/ppermute | solution.py:30
  4.9 0.1 stack.15.place
  5.0 1.1 %shard_map.38 = (bf16[96,384]{1,0:T(8,128)(2,1)S(1)}, bf16[5,96,576]{2,1,0:T(8,128)(2,1)S(1)}) custom-call(s32[5]{0:T(128)S(1)} %stack.15.place, bf16[3,3,32,48]{3,2,1,0:T(8,128)(2,1)S(1)} %get-tuple-element.22.w_first, bf16[5,3,3,48,48]{4,3,2,1,0:T(8,128)(2,1)S(1)} %get-tuple-element.23.w_rest), custom_call_target="tpu_custom_call" | custom-call | flops 100000000 | bytes 1000000 | tf_op jit(solution)/shard_map/pallas_call | solution.py:324
  6.1 0.0 collective-permute-done.1
  6.1 0.6 %collective-permute-start.2 = (bf16[17,32,128]{2,1,0:T(8,128)(2,1)S(1)}, bf16[17,32,128]{2,1,0:T(8,128)(2,1)S(1)}, u32[]{:S(2)}, u32[]{:S(2)}) collective-permute-start(bf16[17,32,128]{2,1,0:T(8,128)(2,1)S(1)} %pad_maximum_fusion.own), channel_id=1, source_target_pairs={{0,1},{2,3},{4,5},{6,7},{8,9},{10,11},{12,13},{14,15},{1,0},{3,2},... | collective-permute-start | bytes 417800 | tf_op jit(solution)/shard_map/ppermute | solution.py:30
  6.7 1.8 %collective-permute-start.4 = (bf16[3,32,128]{2,1,0:T(8,128)(2,1)S(1)}, bf16[3,32,128]{2,1,0:T(8,128)(2,1)S(1)}, u32[]{:S(2)}, u32[]{:S(2)}) collective-permute-start(bf16[3,32,128]{2,1,0:T(8,128)(2,1)S(1)} %maximum_select_fusion), channel_id=1, source_target_pairs={{0,1},{2,0},{4,2},{6,4},{8,6},{10,8},{12,10},{14,12},{1,3},{3,5},{... | collective-permute-start | bytes 73736 | tf_op jit(solution)/shard_map/ppermute | solution.py:349
  8.6 0.0 collective-permute-done.2.mate
  8.6 1.3 %collective-permute-start.3 = (bf16[23,16,128]{2,1,0:T(8,128)(2,1)S(1)}, bf16[23,16,128]{2,1,0:T(8,128)(2,1)S(1)}, u32[]{:S(2)}, u32[]{:S(2)}) collective-permute-start(bf16[23,16,128]{2,1,0:T(8,128)(2,1)S(1)} %pad_maximum_fusion.1), channel_id=1, source_target_pairs={{1,2},{3,4},{5,6},{7,8},{9,10},{11,12},{13,14},{2,1},{4,3},{6,5},{... | collective-permute-start | bytes 282632 | tf_op jit(solution)/shard_map/ppermute | solution.py:30
  9.9 2.8 %shard_map.39 = (f32[16,32,384]{2,1,0:T(8,128)S(1)}, bf16[960,384]{1,0:T(8,128)(2,1)S(1)}, bf16[1152,384]{1,0:T(8,128)(2,1)S(1)}, bf16[864,384]{1,0:T(8,128)(2,1...) custom-call(s32[5]{0:T(128)S(1)} %stack.15.place, bf16[17,32,128]{2,1,0:T(8,128)(2,1)S(1)} %pad_maximum_fusion.own, ...), custom_call_target="tpu_custom_call" | custom-call | flops 4000000000 | bytes 4000000 | tf_op jit(solution)/shard_map/pallas_call | solution.py:360
  12.7 0.0 collective-permute-done.first_part
  12.7 0.0 collective-permute-done.4.across
  12.7 0.8 %collective-permute-done.3.others = bf16[23,16,128]{2,1,0:T(8,128)(2,1)S(1)} collective-permute-done((bf16[23,16,128]{2,1,0:T(8,128)(2,1)S(1)}, bf16[23,16,128]{2,1,0:T(8,128)(2,1)S(1)}, u32[]{:S(2)}, u32[]{:S(2)}) %collective-permute-start.3) | collective-permute-done | bytes 94240 | tf_op jit(solution)/shard_map/ppermute | solution.py:30
  13.5 4.5 %shard_map.40 = f32[48,8,256]{2,1,0:T(8,128)} custom-call(s32[5]{0:T(128)S(1)} %stack.15.place, bf16[17,16,128]{2,1,0:T(8,128)(2,1)S(1)} %collective-permute-done.first_part, bf16[23,16,128]{2,1,0:T(8,128)(2,1)S(1)} %collective-permute-done.3.others, bf16[3,32,128]{2,1,0:T(8,128)(2,1)S(1)} %collective-permute-done.4.across, ...), custom_call_target="tpu_custom_call" | custom-call | flops 2000000000 | bytes 4000000 | tf_op jit(solution)/shard_map/pallas_call | solution.py:370
  (9 shorter events, 0.1 us)
Async XLA Ops:
  1.5 4.5 %collective-permute-start.1 = (bf16[17,16,128]{2,1,0:T(8,128)(2,1)S(1)}, bf16[17,16,128]{2,1,0:T(8,128)(2,1)S(1)}, u32[]{:S(2)}, u32[]{:S(2)}) collective-permute-start(bf16[17,16,128]{2,1,0:T(8,128)(2,1)S(1)} %get-tuple-element.21), channel_id=1, source_target_pairs={{0,16},{16,0},{1,17},{17,1},{2,18},{18,2},{3,19},{19,3},{4,20},{20... | collective-permute-start | bytes 208904 | tf_op jit(solution)/shard_map/ppermute | solution.py:311
  2.9 9.9 %collective-permute-start = (bf16[17,16,128]{2,1,0:T(8,128)(2,1)S(1)}, bf16[17,16,128]{2,1,0:T(8,128)(2,1)S(1)}, u32[]{:S(2)}, u32[]{:S(2)}) collective-permute-start(bf16[17,16,128]{2,1,0:T(8,128)(2,1)S(1)} %get-tuple-element.20), channel_id=1, source_target_pairs={{1,2},{3,4},{5,6},{7,8},{9,10},{11,12},{13,14},{2,1},{4,3},{6,5},{... | collective-permute-start | bytes 208904 | tf_op jit(solution)/shard_map/ppermute | solution.py:30
  6.1 2.4 %collective-permute-start.2 = (bf16[17,32,128]{2,1,0:T(8,128)(2,1)S(1)}, bf16[17,32,128]{2,1,0:T(8,128)(2,1)S(1)}, u32[]{:S(2)}, u32[]{:S(2)}) collective-permute-start(bf16[17,32,128]{2,1,0:T(8,128)(2,1)S(1)} %pad_maximum_fusion.own), channel_id=1, source_target_pairs={{0,1},{2,3},{4,5},{6,7},{8,9},{10,11},{12,13},{14,15},{1,0},{3,2},... | collective-permute-start | bytes 417800 | tf_op jit(solution)/shard_map/ppermute | solution.py:30
  6.7 6.0 %collective-permute-start.4 = (bf16[3,32,128]{2,1,0:T(8,128)(2,1)S(1)}, bf16[3,32,128]{2,1,0:T(8,128)(2,1)S(1)}, u32[]{:S(2)}, u32[]{:S(2)}) collective-permute-start(bf16[3,32,128]{2,1,0:T(8,128)(2,1)S(1)} %maximum_select_fusion), channel_id=1, source_target_pairs={{0,1},{2,0},{4,2},{6,4},{8,6},{10,8},{12,10},{14,12},{1,3},{3,5},{... | collective-permute-start | bytes 73736 | tf_op jit(solution)/shard_map/ppermute | solution.py:349
  8.6 4.9 %collective-permute-start.3 = (bf16[23,16,128]{2,1,0:T(8,128)(2,1)S(1)}, bf16[23,16,128]{2,1,0:T(8,128)(2,1)S(1)}, u32[]{:S(2)}, u32[]{:S(2)}) collective-permute-start(bf16[23,16,128]{2,1,0:T(8,128)(2,1)S(1)} %pad_maximum_fusion.1), channel_id=1, source_target_pairs={{1,2},{3,4},{5,6},{7,8},{9,10},{11,12},{13,14},{2,1},{4,3},{6,5},{... | collective-permute-start | bytes 282632 | tf_op jit(solution)/shard_map/ppermute | solution.py:30
